TPU v7x, 256 devices: a whole 4x4x8 slice. The times are simulated.
256 devices in a mesh: seq: 32 (over x, z), head: 8 (over y, core).
Axes of the slice: x: 4, y: 4, z: 8, core: 2. Of those that a mesh axis runs over, the one named last changes fastest.
Arguments:
- tokens: bfloat16 [16384, 4096], P('seq'), may hold values from -6 to 6
- w_xz: bfloat16 [4096, 2, 4096], P('seq', None, 'head'), may hold values from -0.09375 to 0.09375
- w_bc: bfloat16 [4096, 256], P('seq'), may hold values from -0.09375 to 0.09375
- conv_x: float32 [4, 4096], P(None, 'head'), may hold values from -3 to 3
- conv_bc: float32 [4, 256], replicated, may hold values from -3 to 3
- tail_x: bfloat16 [3, 4096], P(None, 'head'), may hold values from -6 to 6
- tail_bc: bfloat16 [3, 256], replicated, may hold values from -6 to 6
- decay_code: int32 [16384, 64], P('seq', 'head'), may hold values from 0 to 196608, as said below
- skip_gain: float32 [64], P('head'), may hold values from 0.5 to 2
- state_in: float32 [64, 64, 128], P('head'), may hold values from -180 to 180
- norm_gain: float32 [4096], P('head'), may hold values from 0.1 to 1.9
- w_out: bfloat16 [4096, 4096], P('head', 'seq'), may hold values from -0.1875 to 0.1875
Outputs:
- mixed: bfloat16 [16384, 4096], P('seq', 'head')
Inputs may be any that keep to these rules, and one draw needn't show every extreme that they name: `decay_code`: the decay factor of a token and head is exp(-code / 262144).
All inputs are finite; a program needn't handle non-finite values.
Results may differ from a plain program's by a relative error of at most 0.0085.
Values may be sent and summed in bfloat16 or wider, within the bound.
A program may use at most 128 MiB of HBM per device.

v0:
```python
import jax
import jax.numpy as jnp
from jax import lax
from jax.sharding import PartitionSpec as P

Q = 256


def passed_along(value, axis, by):
    size = lax.axis_size(axis)
    pairs = [(i, i + by) for i in range(size) if 0 <= i + by < size]
    return lax.ppermute(value, axis, pairs)


def depthwise(pre, tail, kernel):
    whole = jnp.concatenate([tail, pre], axis=0).astype(jnp.float32)
    length = pre.shape[0]
    total = jnp.zeros((length, pre.shape[1]), jnp.float32)
    for offset in range(kernel.shape[0]):
        total = total + kernel[offset] * whole[offset : offset + length]
    return jax.nn.silu(total).astype(jnp.bfloat16)


def block_step(state, inputs):
    xval, bval, cval, logdec = inputs
    cum = jnp.cumsum(logdec, axis=0)
    span = cum.shape[0]
    places = jnp.arange(span)
    lower = places[:, None] >= places[None, :]
    cumt = cum.T
    diff = cumt[:, :, None] - cumt[:, None, :]
    decay = jnp.where(lower[None], jnp.exp(jnp.where(lower[None], diff, 0.0)), 0.0)
    scores = jnp.dot(cval, bval.T, preferred_element_type=jnp.float32)
    weights = (decay * scores[None]).astype(jnp.bfloat16)
    inner = jnp.einsum("hts,shp->thp", weights, xval, preferred_element_type=jnp.float32)
    carried = jnp.einsum(
        "tn,hpn->thp", cval.astype(jnp.float32), state, precision=lax.Precision.HIGHEST
    )
    carried = carried * jnp.exp(cum)[:, :, None]
    tail_decay = jnp.exp(cum[-1][None, :] - cum)
    decayed_b = (tail_decay.T[:, :, None] * bval.astype(jnp.float32)[None]).astype(jnp.bfloat16)
    added = jnp.einsum("hsn,shp->hpn", decayed_b, xval, preferred_element_type=jnp.float32)
    new_state = jnp.exp(cum[-1])[:, None, None] * state + added
    return (new_state, inner + carried)


def local(
    tokens,
    w_xz,
    w_bc,
    conv_x,
    conv_bc,
    tail_x,
    tail_bc,
    decay_code,
    skip_gain,
    state_in,
    norm_gain,
    w_out,
):
    rows = tokens.shape[0]
    heads, head_dim, nstate = state_in.shape
    inner = heads * head_dim
    seq_count = lax.axis_size("seq")
    first = lax.axis_index("seq") == 0
    pieces = (
        lax.all_gather(w_xz, "seq", axis=0, tiled=True),
        lax.all_gather(w_bc, "seq", axis=0, tiled=True),
    )
    count = pieces[0].shape[0]
    xz = jnp.dot(tokens, pieces[0].reshape(count, 2 * inner), preferred_element_type=jnp.float32)
    bc_sum = jnp.dot(tokens, pieces[1], preferred_element_type=jnp.float32)
    x_pre = xz[:, :inner].astype(jnp.bfloat16)
    z_val = xz[:, inner:].astype(jnp.bfloat16)
    bc_pre = bc_sum.astype(jnp.bfloat16)
    lag = conv_x.shape[0] - 1
    before_x, before_bc = passed_along((x_pre[rows - lag :], bc_pre[rows - lag :]), "seq", 1)
    before_x = jnp.where(first, tail_x, before_x)
    before_bc = jnp.where(first, tail_bc, before_bc)
    x_conv = depthwise(x_pre, before_x, conv_x)
    bc_conv = depthwise(bc_pre, before_bc, conv_bc)
    b_val = bc_conv[:, :nstate]
    c_val = bc_conv[:, nstate:]
    logdec = -decay_code.astype(jnp.float32) / (16.0 * rows * seq_count)
    blocks = rows // Q
    inputs = (
        x_conv.reshape(blocks, Q, heads, head_dim),
        b_val.reshape(blocks, Q, nstate),
        c_val.reshape(blocks, Q, nstate),
        logdec.reshape(blocks, Q, heads),
    )
    local_state, parts = lax.scan(block_step, jnp.zeros_like(state_in), inputs)
    parts = parts.reshape(rows, heads, head_dim)
    cum_range = jnp.cumsum(logdec, axis=0)
    range_decay = jnp.exp(cum_range[-1])

    def link(step, incoming):
        outgoing = range_decay[:, None, None] * incoming + local_state
        received = passed_along(outgoing, "seq", 1)
        return jnp.where(first, state_in, received)

    opening = jnp.where(first, state_in, jnp.zeros_like(state_in))
    incoming = lax.fori_loop(0, seq_count - 1, link, opening)
    correction = jnp.einsum(
        "tn,hpn->thp", c_val.astype(jnp.float32), incoming, precision=lax.Precision.HIGHEST
    )
    parts = (parts + correction * jnp.exp(cum_range)[:, :, None]).reshape(rows, inner)
    y_val = parts / nstate + jnp.repeat(skip_gain, head_dim)[None, :] * x_conv.astype(jnp.float32)
    gated = y_val * jax.nn.silu(z_val.astype(jnp.float32))
    total_sq = lax.psum(jnp.sum(gated * gated, axis=1), "head")
    meansq = total_sq / (inner * lax.axis_size("head"))
    normed = (gated * lax.rsqrt(meansq[:, None] + 1e-05) * norm_gain[None, :]).astype(jnp.bfloat16)
    partial_out = jnp.dot(
        normed, lax.all_gather(w_out, "seq", axis=1, tiled=True), preferred_element_type=jnp.float32
    )
    result = lax.psum_scatter(partial_out, "head", scatter_dimension=1, tiled=True)
    return result.astype(jnp.bfloat16)


def solution(mesh):
    return jax.shard_map(
        local,
        mesh=mesh,
        in_specs=(
            P("seq", None),
            P("seq", None, "head"),
            P("seq", None),
            P(None, "head"),
            P(),
            P(None, "head"),
            P(),
            P("seq", "head"),
            P("head"),
            P("head", None, None),
            P("head"),
            P("head", "seq"),
        ),
        out_specs=P("seq", "head"),
        check_vma=False,
    )
```

profile of v0, /device:TPU:1, one launch (start us, length us, event | category | flops | bytes accessed | tf_op | source)
XLA Modules:
  0.0 687.8 jit_solution(6303912154717134488)
XLA Ops:
  13.6 74.2 %all-gather.6.cloned.1.call-done = bf16[4096,256]{1,0:T(8,128)(2,1)} async-done(((bf16[128,256]{1,0:T(8,128)(2,1)}), bf16[4096,256]{1,0:T(8,128)(2,1)}) %all-gather.6.cloned.1.call-update) | async-done | bytes 2097168 | tf_op jit(solution)/shard_map/all_gather | solution.py:68
  95.5 93.9 %all-gather.4.cloned.1.call-done = bf16[4096,2,512]{2,1,0:T(2,128)(2,1)} async-done(((bf16[128,2,512]{2,1,0:T(2,128)(2,1)}), bf16[4096,2,512]{2,1,0:T(2,128)(2,1)}) %all-gather.4.cloned.1.call-update) | async-done | bytes 8388624 | tf_op jit(solution)/shard_map/all_gather | solution.py:67
  189.4 9.3 %copy.40 = bf16[512,8,2,512]{3,1,2,0:T(8,128)(2,1)} copy(bf16[512,8,2,512]{3,2,1,0:T(2,128)(2,1)} %bitcast.88) | data formatting | bytes 16777216
  198.7 9.3 %convolution_convert_fusion = bf16[512,1024]{1,0:T(8,128)(2,1)S(1)} fusion(bf16[512,4096]{1,0:T(8,128)(2,1)} %param.16, bf16[4096,1024]{1,0:T(8,128)(2,1)} %bitcast.89), kind=kOutput, calls=%fused_computation.44 | convolution fusion | flops 4295491584 | bytes 13631488 | tf_op jit(solution)/shard_map/dot_general | solution.py:71
  212.1 30.3 %while.24 = (s32[]{:T(128)}, f32[8,64,128]{2,1,0:T(8,128)S(1)}, f32[2,256,8,64]{1,0,3,2:T(2,128)}, f32[2,256,8]{1,2,0:T(8,128)S(1)}, bf16[2,256,8,64]{1,3,2,0:T(...) while((s32[]{:T(128)}, f32[8,64,128]{2,1,0:T(8,128)S(1)}, ...), condition=%wide.region_3.4_spmd.clone, body=%wide.region_0.3_spmd.clone.sunk | while | flops 322801696 | bytes 6277456 | solution.py:92
  215.2 11.5 %dynamic_update_slice.6 = f32[2,256,8,64]{1,0,3,2:T(2,128)} dynamic-update-slice(f32[2,256,8,64]{1,0,3,2:T(2,128)} %get-tuple-element.276, f32[1,256,8,64]{1,0,3,2:T(1,128)S(1)} %copy.42, s32[]{:T(128)} %get-tuple-element.274, s32[]{:T(128)} %constant.46.clone.1..sunk, s32[]{:T(128)} %constant.46.clone.1..sunk, s32[]{:T(128)} %constant.46.clone.1..sunk) | dynamic-update-slice | bytes 1048580 | tf_op jit(solution)/shard_map/while/body/jit(dynamic_update_index_in_dim)/dynamic_update_slice | solution.py:92
  230.3 11.5 %dynamic_update_slice.6 = f32[2,256,8,64]{1,0,3,2:T(2,128)} dynamic-update-slice(f32[2,256,8,64]{1,0,3,2:T(2,128)} %get-tuple-element.276, f32[1,256,8,64]{1,0,3,2:T(1,128)S(1)} %copy.42, s32[]{:T(128)} %get-tuple-element.274, s32[]{:T(128)} %constant.46.clone.1..sunk, s32[]{:T(128)} %constant.46.clone.1..sunk, s32[]{:T(128)} %constant.46.clone.1..sunk) | dynamic-update-slice | bytes 1048580 | tf_op jit(solution)/shard_map/while/body/jit(dynamic_update_index_in_dim)/dynamic_update_slice | solution.py:92
  244.6 299.9 %while.23 = (s32[]{:T(128)}, f32[8,64,128]{2,1,0:T(8,128)S(1)}, pred[]{:T(512)}, f32[8]{0:T(128)S(1)}, f32[8,64,128]{2,1,0:T(8,128)S(1)}, /*index=5*/f32[8,64,128]{2,1,0:T(8,128)S(1)}, s32[]{:T(128)}) while((s32[]{:T(128)}, f32[8,64,128]{2,1,0:T(8,128)S(1)}, pred[]{:T(512)}, f32[8]{0:T(128)S(1)}, f32[8,64,128]{2,1,0:T(8,128)S(1)}, ...), condition=%wide.region_7.8_spmd, body=%wide.region_6.7_spmd.sunk | while | flops 196610 | bytes 2621590 | solution.py:103
  248.6 8.4 %collective-permute-done = f32[8,64,128]{2,1,0:T(8,128)S(1)} collective-permute-done((f32[8,64,128]{2,1,0:T(8,128)S(1)}, f32[8,64,128]{2,1,0:T(8,128)S(1)}, u32[]{:S(2)}, u32[]{:S(2)}) %collective-permute-start) | collective-permute-done | bytes 262176 | tf_op jit(solution)/shard_map/while/body/eval_jaxpr/ppermute | solution.py:12
  261.3 7.3 %collective-permute-done = f32[8,64,128]{2,1,0:T(8,128)S(1)} collective-permute-done((f32[8,64,128]{2,1,0:T(8,128)S(1)}, f32[8,64,128]{2,1,0:T(8,128)S(1)}, u32[]{:S(2)}, u32[]{:S(2)}) %collective-permute-start) | collective-permute-done | bytes 262176 | tf_op jit(solution)/shard_map/while/body/eval_jaxpr/ppermute | solution.py:12
  305.1 5.3 collective-permute-done
  314.4 5.8 collective-permute-done
  337.7 6.9 %collective-permute-start = (f32[8,64,128]{2,1,0:T(8,128)S(1)}, f32[8,64,128]{2,1,0:T(8,128)S(1)}, u32[]{:S(2)}, u32[]{:S(2)}) collective-permute-start(f32[8,64,128]{2,1,0:T(8,128)S(1)} %multiply_add_fusion.2), channel_id=1, source_target_pairs={{0,8},{8,16},{16,24},{24,32},{32,40},{40,48},{48,56},{56,64},{64,7... | collective-permute-start | bytes 786440 | tf_op jit(solution)/shard_map/while/body/eval_jaxpr/ppermute | solution.py:12
  356.8 5.2 collective-permute-start
  365.5 5.3 collective-permute-start
  374.2 5.3 collective-permute-start
  400.9 5.6 collective-permute-start
  406.5 5.2 collective-permute-done
  411.9 5.9 collective-permute-start
  417.8 5.8 collective-permute-done
  423.8 5.3 collective-permute-start
  459.3 10.4 %collective-permute-start = (f32[8,64,128]{2,1,0:T(8,128)S(1)}, f32[8,64,128]{2,1,0:T(8,128)S(1)}, u32[]{:S(2)}, u32[]{:S(2)}) collective-permute-start(f32[8,64,128]{2,1,0:T(8,128)S(1)} %multiply_add_fusion.2), channel_id=1, source_target_pairs={{0,8},{8,16},{16,24},{24,32},{32,40},{40,48},{48,56},{56,64},{64,7... | collective-permute-start | bytes 786440 | tf_op jit(solution)/shard_map/while/body/eval_jaxpr/ppermute | solution.py:12
  473.2 5.7 collective-permute-start
  482.3 5.4 collective-permute-start
  499.8 6.2 collective-permute-start
  509.7 6.2 collective-permute-start
  520.3 6.1 collective-permute-start
  531.5 6.9 collective-permute-start
  538.4 6.1 collective-permute-done
  552.1 45.7 %psum.7 = f32[512]{0:T(512)S(1)} all-reduce(f32[512]{0:T(512)S(1)} %get-tuple-element.160), channel_id=1, replica_groups=mesh['seq'=32,'head'=8] {'head'}, use_global_device_ids=true, to_apply=%region_9.10 | all-reduce | flops 512 | bytes 4096 | tf_op jit(solution)/shard_map/psum | solution.py:110
  597.8 7.8 %fusion.38 = f32[512,4096]{1,0:T(8,128)} fusion(bf16[512,4096]{1,0:T(8,128)(2,1)} %all-gather.8.cloned.1.call-done, f32[512,512]{1,0:T(8,128)S(1)} %get-tuple-element.161, f32[512]{0:T(512)S(1)} %copy-done.3, f32[512]{0:T(512)S(1)} %add_rsqrt_fusion), kind=kOutput, calls=%fused_computation.66 | convolution fusion | flops 2148270080 | bytes 13635584 | tf_op jit(solution)/shard_map/dot_general | solution.py:113
  605.6 73.5 %reduce-scatter.2.cloned.1.call-done = f32[512,512]{1,0:T(8,128)} async-done(((f32[512,4096]{1,0:T(8,128)}), f32[512,512]{1,0:T(8,128)}) %reduce-scatter.2.cloned.1.call-update) | async-done | bytes 1048592 | tf_op jit(solution)/shard_map/reduce_scatter | solution.py:116
  (195 shorter events, 206.1 us)
Async XLA Ops:
  6.5 81.3 %all-gather.6.cloned.1.call-start = ((), (), s32[]{:S(2)}) async-start(), calls=%async_computation.2 | async-start | bytes 2162688 | tf_op jit(solution)/shard_map/all_gather | solution.py:68
  7.3 182.2 %all-gather.4.cloned.1.call-start = ((), (), s32[]{:S(2)}) async-start(), calls=%async_computation.1 | async-start | bytes 8650752 | tf_op jit(solution)/shard_map/all_gather | solution.py:67
  8.0 589.8 %all-gather.8.cloned.1.call-start = ((), (), s32[]{:S(2)}) async-start(), calls=%async_computation.3 | async-start | bytes 4325376 | tf_op jit(solution)/shard_map/all_gather | solution.py:114
  8.7 670.4 %reduce-scatter.2.cloned.1.call-start = ((), (), s32[]{:S(2)}) async-start(), calls=%async_computation.4 | async-start | bytes 9437184 | tf_op jit(solution)/shard_map/reduce_scatter | solution.py:116
  244.7 12.3 %collective-permute-start = (f32[8,64,128]{2,1,0:T(8,128)S(1)}, f32[8,64,128]{2,1,0:T(8,128)S(1)}, u32[]{:S(2)}, u32[]{:S(2)}) collective-permute-start(f32[8,64,128]{2,1,0:T(8,128)S(1)} %multiply_add_fusion.2), channel_id=1, source_target_pairs={{0,8},{8,16},{16,24},{24,32},{32,40},{40,48},{48,56},{56,64},{64,7... | collective-permute-start | bytes 786440 | tf_op jit(solution)/shard_map/while/body/eval_jaxpr/ppermute | solution.py:12
  257.1 11.6 %collective-permute-start = (f32[8,64,128]{2,1,0:T(8,128)S(1)}, f32[8,64,128]{2,1,0:T(8,128)S(1)}, u32[]{:S(2)}, u32[]{:S(2)}) collective-permute-start(f32[8,64,128]{2,1,0:T(8,128)S(1)} %multiply_add_fusion.2), channel_id=1, source_target_pairs={{0,8},{8,16},{16,24},{24,32},{32,40},{40,48},{48,56},{56,64},{64,7... | collective-permute-start | bytes 786440 | tf_op jit(solution)/shard_map/while/body/eval_jaxpr/ppermute | solution.py:12
  268.8 9.0 %collective-permute-start = (f32[8,64,128]{2,1,0:T(8,128)S(1)}, f32[8,64,128]{2,1,0:T(8,128)S(1)}, u32[]{:S(2)}, u32[]{:S(2)}) collective-permute-start(f32[8,64,128]{2,1,0:T(8,128)S(1)} %multiply_add_fusion.2), channel_id=1, source_target_pairs={{0,8},{8,16},{16,24},{24,32},{32,40},{40,48},{48,56},{56,64},{64,7... | collective-permute-start | bytes 786440 | tf_op jit(solution)/shard_map/while/body/eval_jaxpr/ppermute | solution.py:12
  277.9 7.5 %collective-permute-start = (f32[8,64,128]{2,1,0:T(8,128)S(1)}, f32[8,64,128]{2,1,0:T(8,128)S(1)}, u32[]{:S(2)}, u32[]{:S(2)}) collective-permute-start(f32[8,64,128]{2,1,0:T(8,128)S(1)} %multiply_add_fusion.2), channel_id=1, source_target_pairs={{0,8},{8,16},{16,24},{24,32},{32,40},{40,48},{48,56},{56,64},{64,7... | collective-permute-start | bytes 786440 | tf_op jit(solution)/shard_map/while/body/eval_jaxpr/ppermute | solution.py:12
  293.0 8.1 %collective-permute-start = (f32[8,64,128]{2,1,0:T(8,128)S(1)}, f32[8,64,128]{2,1,0:T(8,128)S(1)}, u32[]{:S(2)}, u32[]{:S(2)}) collective-permute-start(f32[8,64,128]{2,1,0:T(8,128)S(1)} %multiply_add_fusion.2), channel_id=1, source_target_pairs={{0,8},{8,16},{16,24},{24,32},{32,40},{40,48},{48,56},{56,64},{64,7... | collective-permute-start | bytes 786440 | tf_op jit(solution)/shard_map/while/body/eval_jaxpr/ppermute | solution.py:12
  301.3 9.1 %collective-permute-start = (f32[8,64,128]{2,1,0:T(8,128)S(1)}, f32[8,64,128]{2,1,0:T(8,128)S(1)}, u32[]{:S(2)}, u32[]{:S(2)}) collective-permute-start(f32[8,64,128]{2,1,0:T(8,128)S(1)} %multiply_add_fusion.2), channel_id=1, source_target_pairs={{0,8},{8,16},{16,24},{24,32},{32,40},{40,48},{48,56},{56,64},{64,7... | collective-permute-start | bytes 786440 | tf_op jit(solution)/shard_map/while/body/eval_jaxpr/ppermute | solution.py:12
  310.5 9.6 %collective-permute-start = (f32[8,64,128]{2,1,0:T(8,128)S(1)}, f32[8,64,128]{2,1,0:T(8,128)S(1)}, u32[]{:S(2)}, u32[]{:S(2)}) collective-permute-start(f32[8,64,128]{2,1,0:T(8,128)S(1)} %multiply_add_fusion.2), channel_id=1, source_target_pairs={{0,8},{8,16},{16,24},{24,32},{32,40},{40,48},{48,56},{56,64},{64,7... | collective-permute-start | bytes 786440 | tf_op jit(solution)/shard_map/while/body/eval_jaxpr/ppermute | solution.py:12
  320.3 9.0 %collective-permute-start = (f32[8,64,128]{2,1,0:T(8,128)S(1)}, f32[8,64,128]{2,1,0:T(8,128)S(1)}, u32[]{:S(2)}, u32[]{:S(2)}) collective-permute-start(f32[8,64,128]{2,1,0:T(8,128)S(1)} %multiply_add_fusion.2), channel_id=1, source_target_pairs={{0,8},{8,16},{16,24},{24,32},{32,40},{40,48},{48,56},{56,64},{64,7... | collective-permute-start | bytes 786440 | tf_op jit(solution)/shard_map/while/body/eval_jaxpr/ppermute | solution.py:12
  329.5 8.1 %collective-permute-start = (f32[8,64,128]{2,1,0:T(8,128)S(1)}, f32[8,64,128]{2,1,0:T(8,128)S(1)}, u32[]{:S(2)}, u32[]{:S(2)}) collective-permute-start(f32[8,64,128]{2,1,0:T(8,128)S(1)} %multiply_add_fusion.2), channel_id=1, source_target_pairs={{0,8},{8,16},{16,24},{24,32},{32,40},{40,48},{48,56},{56,64},{64,7... | collective-permute-start | bytes 786440 | tf_op jit(solution)/shard_map/while/body/eval_jaxpr/ppermute | solution.py:12
  337.7 11.4 %collective-permute-start = (f32[8,64,128]{2,1,0:T(8,128)S(1)}, f32[8,64,128]{2,1,0:T(8,128)S(1)}, u32[]{:S(2)}, u32[]{:S(2)}) collective-permute-start(f32[8,64,128]{2,1,0:T(8,128)S(1)} %multiply_add_fusion.2), channel_id=1, source_target_pairs={{0,8},{8,16},{16,24},{24,32},{32,40},{40,48},{48,56},{56,64},{64,7... | collective-permute-start | bytes 786440 | tf_op jit(solution)/shard_map/while/body/eval_jaxpr/ppermute | solution.py:12
  356.8 8.5 %collective-permute-start = (f32[8,64,128]{2,1,0:T(8,128)S(1)}, f32[8,64,128]{2,1,0:T(8,128)S(1)}, u32[]{:S(2)}, u32[]{:S(2)}) collective-permute-start(f32[8,64,128]{2,1,0:T(8,128)S(1)} %multiply_add_fusion.2), channel_id=1, source_target_pairs={{0,8},{8,16},{16,24},{24,32},{32,40},{40,48},{48,56},{56,64},{64,7... | collective-permute-start | bytes 786440 | tf_op jit(solution)/shard_map/while/body/eval_jaxpr/ppermute | solution.py:12
  365.5 8.6 %collective-permute-start = (f32[8,64,128]{2,1,0:T(8,128)S(1)}, f32[8,64,128]{2,1,0:T(8,128)S(1)}, u32[]{:S(2)}, u32[]{:S(2)}) collective-permute-start(f32[8,64,128]{2,1,0:T(8,128)S(1)} %multiply_add_fusion.2), channel_id=1, source_target_pairs={{0,8},{8,16},{16,24},{24,32},{32,40},{40,48},{48,56},{56,64},{64,7... | collective-permute-start | bytes 786440 | tf_op jit(solution)/shard_map/while/body/eval_jaxpr/ppermute | solution.py:12
  374.2 8.6 %collective-permute-start = (f32[8,64,128]{2,1,0:T(8,128)S(1)}, f32[8,64,128]{2,1,0:T(8,128)S(1)}, u32[]{:S(2)}, u32[]{:S(2)}) collective-permute-start(f32[8,64,128]{2,1,0:T(8,128)S(1)} %multiply_add_fusion.2), channel_id=1, source_target_pairs={{0,8},{8,16},{16,24},{24,32},{32,40},{40,48},{48,56},{56,64},{64,7... | collective-permute-start | bytes 786440 | tf_op jit(solution)/shard_map/while/body/eval_jaxpr/ppermute | solution.py:12
  383.0 8.3 %collective-permute-start = (f32[8,64,128]{2,1,0:T(8,128)S(1)}, f32[8,64,128]{2,1,0:T(8,128)S(1)}, u32[]{:S(2)}, u32[]{:S(2)}) collective-permute-start(f32[8,64,128]{2,1,0:T(8,128)S(1)} %multiply_add_fusion.2), channel_id=1, source_target_pairs={{0,8},{8,16},{16,24},{24,32},{32,40},{40,48},{48,56},{56,64},{64,7... | collective-permute-start | bytes 786440 | tf_op jit(solution)/shard_map/while/body/eval_jaxpr/ppermute | solution.py:12
  391.5 9.3 %collective-permute-start = (f32[8,64,128]{2,1,0:T(8,128)S(1)}, f32[8,64,128]{2,1,0:T(8,128)S(1)}, u32[]{:S(2)}, u32[]{:S(2)}) collective-permute-start(f32[8,64,128]{2,1,0:T(8,128)S(1)} %multiply_add_fusion.2), channel_id=1, source_target_pairs={{0,8},{8,16},{16,24},{24,32},{32,40},{40,48},{48,56},{56,64},{64,7... | collective-permute-start | bytes 786440 | tf_op jit(solution)/shard_map/while/body/eval_jaxpr/ppermute | solution.py:12
  400.9 10.9 %collective-permute-start = (f32[8,64,128]{2,1,0:T(8,128)S(1)}, f32[8,64,128]{2,1,0:T(8,128)S(1)}, u32[]{:S(2)}, u32[]{:S(2)}) collective-permute-start(f32[8,64,128]{2,1,0:T(8,128)S(1)} %multiply_add_fusion.2), channel_id=1, source_target_pairs={{0,8},{8,16},{16,24},{24,32},{32,40},{40,48},{48,56},{56,64},{64,7... | collective-permute-start | bytes 786440 | tf_op jit(solution)/shard_map/while/body/eval_jaxpr/ppermute | solution.py:12
  411.9 11.8 %collective-permute-start = (f32[8,64,128]{2,1,0:T(8,128)S(1)}, f32[8,64,128]{2,1,0:T(8,128)S(1)}, u32[]{:S(2)}, u32[]{:S(2)}) collective-permute-start(f32[8,64,128]{2,1,0:T(8,128)S(1)} %multiply_add_fusion.2), channel_id=1, source_target_pairs={{0,8},{8,16},{16,24},{24,32},{32,40},{40,48},{48,56},{56,64},{64,7... | collective-permute-start | bytes 786440 | tf_op jit(solution)/shard_map/while/body/eval_jaxpr/ppermute | solution.py:12
  423.8 10.4 %collective-permute-start = (f32[8,64,128]{2,1,0:T(8,128)S(1)}, f32[8,64,128]{2,1,0:T(8,128)S(1)}, u32[]{:S(2)}, u32[]{:S(2)}) collective-permute-start(f32[8,64,128]{2,1,0:T(8,128)S(1)} %multiply_add_fusion.2), channel_id=1, source_target_pairs={{0,8},{8,16},{16,24},{24,32},{32,40},{40,48},{48,56},{56,64},{64,7... | collective-permute-start | bytes 786440 | tf_op jit(solution)/shard_map/while/body/eval_jaxpr/ppermute | solution.py:12
  434.4 8.7 %collective-permute-start = (f32[8,64,128]{2,1,0:T(8,128)S(1)}, f32[8,64,128]{2,1,0:T(8,128)S(1)}, u32[]{:S(2)}, u32[]{:S(2)}) collective-permute-start(f32[8,64,128]{2,1,0:T(8,128)S(1)} %multiply_add_fusion.2), channel_id=1, source_target_pairs={{0,8},{8,16},{16,24},{24,32},{32,40},{40,48},{48,56},{56,64},{64,7... | collective-permute-start | bytes 786440 | tf_op jit(solution)/shard_map/while/body/eval_jaxpr/ppermute | solution.py:12
  450.7 8.5 %collective-permute-start = (f32[8,64,128]{2,1,0:T(8,128)S(1)}, f32[8,64,128]{2,1,0:T(8,128)S(1)}, u32[]{:S(2)}, u32[]{:S(2)}) collective-permute-start(f32[8,64,128]{2,1,0:T(8,128)S(1)} %multiply_add_fusion.2), channel_id=1, source_target_pairs={{0,8},{8,16},{16,24},{24,32},{32,40},{40,48},{48,56},{56,64},{64,7... | collective-permute-start | bytes 786440 | tf_op jit(solution)/shard_map/while/body/eval_jaxpr/ppermute | solution.py:12
  459.3 13.7 %collective-permute-start = (f32[8,64,128]{2,1,0:T(8,128)S(1)}, f32[8,64,128]{2,1,0:T(8,128)S(1)}, u32[]{:S(2)}, u32[]{:S(2)}) collective-permute-start(f32[8,64,128]{2,1,0:T(8,128)S(1)} %multiply_add_fusion.2), channel_id=1, source_target_pairs={{0,8},{8,16},{16,24},{24,32},{32,40},{40,48},{48,56},{56,64},{64,7... | collective-permute-start | bytes 786440 | tf_op jit(solution)/shard_map/while/body/eval_jaxpr/ppermute | solution.py:12
  473.2 9.0 %collective-permute-start = (f32[8,64,128]{2,1,0:T(8,128)S(1)}, f32[8,64,128]{2,1,0:T(8,128)S(1)}, u32[]{:S(2)}, u32[]{:S(2)}) collective-permute-start(f32[8,64,128]{2,1,0:T(8,128)S(1)} %multiply_add_fusion.2), channel_id=1, source_target_pairs={{0,8},{8,16},{16,24},{24,32},{32,40},{40,48},{48,56},{56,64},{64,7... | collective-permute-start | bytes 786440 | tf_op jit(solution)/shard_map/while/body/eval_jaxpr/ppermute | solution.py:12
  482.3 8.7 %collective-permute-start = (f32[8,64,128]{2,1,0:T(8,128)S(1)}, f32[8,64,128]{2,1,0:T(8,128)S(1)}, u32[]{:S(2)}, u32[]{:S(2)}) collective-permute-start(f32[8,64,128]{2,1,0:T(8,128)S(1)} %multiply_add_fusion.2), channel_id=1, source_target_pairs={{0,8},{8,16},{16,24},{24,32},{32,40},{40,48},{48,56},{56,64},{64,7... | collective-permute-start | bytes 786440 | tf_op jit(solution)/shard_map/while/body/eval_jaxpr/ppermute | solution.py:12
  491.1 8.5 %collective-permute-start = (f32[8,64,128]{2,1,0:T(8,128)S(1)}, f32[8,64,128]{2,1,0:T(8,128)S(1)}, u32[]{:S(2)}, u32[]{:S(2)}) collective-permute-start(f32[8,64,128]{2,1,0:T(8,128)S(1)} %multiply_add_fusion.2), channel_id=1, source_target_pairs={{0,8},{8,16},{16,24},{24,32},{32,40},{40,48},{48,56},{56,64},{64,7... | collective-permute-start | bytes 786440 | tf_op jit(solution)/shard_map/while/body/eval_jaxpr/ppermute | solution.py:12
  499.8 9.7 %collective-permute-start = (f32[8,64,128]{2,1,0:T(8,128)S(1)}, f32[8,64,128]{2,1,0:T(8,128)S(1)}, u32[]{:S(2)}, u32[]{:S(2)}) collective-permute-start(f32[8,64,128]{2,1,0:T(8,128)S(1)} %multiply_add_fusion.2), channel_id=1, source_target_pairs={{0,8},{8,16},{16,24},{24,32},{32,40},{40,48},{48,56},{56,64},{64,7... | collective-permute-start | bytes 786440 | tf_op jit(solution)/shard_map/while/body/eval_jaxpr/ppermute | solution.py:12
  509.7 10.5 %collective-permute-start = (f32[8,64,128]{2,1,0:T(8,128)S(1)}, f32[8,64,128]{2,1,0:T(8,128)S(1)}, u32[]{:S(2)}, u32[]{:S(2)}) collective-permute-start(f32[8,64,128]{2,1,0:T(8,128)S(1)} %multiply_add_fusion.2), channel_id=1, source_target_pairs={{0,8},{8,16},{16,24},{24,32},{32,40},{40,48},{48,56},{56,64},{64,7... | collective-permute-start | bytes 786440 | tf_op jit(solution)/shard_map/while/body/eval_jaxpr/ppermute | solution.py:12
  520.3 11.0 %collective-permute-start = (f32[8,64,128]{2,1,0:T(8,128)S(1)}, f32[8,64,128]{2,1,0:T(8,128)S(1)}, u32[]{:S(2)}, u32[]{:S(2)}) collective-permute-start(f32[8,64,128]{2,1,0:T(8,128)S(1)} %multiply_add_fusion.2), channel_id=1, source_target_pairs={{0,8},{8,16},{16,24},{24,32},{32,40},{40,48},{48,56},{56,64},{64,7... | collective-permute-start | bytes 786440 | tf_op jit(solution)/shard_map/while/body/eval_jaxpr/ppermute | solution.py:12
  531.5 12.9 %collective-permute-start = (f32[8,64,128]{2,1,0:T(8,128)S(1)}, f32[8,64,128]{2,1,0:T(8,128)S(1)}, u32[]{:S(2)}, u32[]{:S(2)}) collective-permute-start(f32[8,64,128]{2,1,0:T(8,128)S(1)} %multiply_add_fusion.2), channel_id=1, source_target_pairs={{0,8},{8,16},{16,24},{24,32},{32,40},{40,48},{48,56},{56,64},{64,7... | collective-permute-start | bytes 786440 | tf_op jit(solution)/shard_map/while/body/eval_jaxpr/ppermute | solution.py:12
  (12 other events, 367.8 us)
Sparse Core Ops, SparseCore 0:
  9.9 77.8 all-gather.5
  90.4 98.9 all-gather.3
  191.9 85.3 all-gather.7
  605.7 73.3 reduce-scatter.1
where the time goes:
time: 691 us; the launch traced here: 688 us
  waiting for transfers between devices  379 us (55%)
  starting transfers between devices  164 us (24%)
  blocking collectives  45.7 us (7%)
  local copies, waits for them, and re-layouts  42.3 us (6%)
  matrix products  27.4 us (4%)
  other arithmetic  14.1 us (2%)
  between operations  13.4 us (2%)
    ppermute x33, starting transfers between devices, passed_along(): return lax.ppermute(value, axis, pairs)  164 us
    ppermute x33, waiting for transfers between devices, passed_along(): return lax.ppermute(value, axis, pairs)  136 us
    all_gather x1, waiting for transfers between devices, local(): lax.all_gather(w_xz, 'seq', axis=0, tiled=True)  93.9 us
    all_gather x1, waiting for transfers between devices, local(): lax.all_gather(w_bc, 'seq', axis=0, tiled=True)  74.2 us
    reduce_scatter x1, waiting for transfers between devices, local(): lax.psum_scatter(partial_out, 'head', scatter_dimension=1, tiled=True)  73.5 us
    psum x1, blocking collectives, local(): total_sq = lax.psum(jnp.sum(gated * gated, axis=1), 'head')  45.7 us
    dynamic_update_slice x4, local copies, waits for them, and re-layouts, local(): local_state, parts = lax.scan(block_step, jnp.zeros_like(state_in), inputs)  24.1 us
  transfers between devices with their start and end apart: 37, of which 36 were waited for; matrix products, arithmetic and copies ran while one was open for 11% of the time, Pallas kernels for 0%

commit v1 on v0

--- a/solution.py
+++ b/solution.py
@@ -21,27 +21,21 @@
     return jax.nn.silu(total).astype(jnp.bfloat16)
 
 
-def block_step(state, inputs):
-    xval, bval, cval, logdec = inputs
-    cum = jnp.cumsum(logdec, axis=0)
-    span = cum.shape[0]
-    places = jnp.arange(span)
-    lower = places[:, None] >= places[None, :]
-    cumt = cum.T
-    diff = cumt[:, :, None] - cumt[:, None, :]
-    decay = jnp.where(lower[None], jnp.exp(jnp.where(lower[None], diff, 0.0)), 0.0)
-    scores = jnp.dot(cval, bval.T, preferred_element_type=jnp.float32)
-    weights = (decay * scores[None]).astype(jnp.bfloat16)
-    inner = jnp.einsum("hts,shp->thp", weights, xval, preferred_element_type=jnp.float32)
-    carried = jnp.einsum(
-        "tn,hpn->thp", cval.astype(jnp.float32), state, precision=lax.Precision.HIGHEST
-    )
-    carried = carried * jnp.exp(cum)[:, :, None]
-    tail_decay = jnp.exp(cum[-1][None, :] - cum)
-    decayed_b = (tail_decay.T[:, :, None] * bval.astype(jnp.float32)[None]).astype(jnp.bfloat16)
-    added = jnp.einsum("hsn,shp->hpn", decayed_b, xval, preferred_element_type=jnp.float32)
-    new_state = jnp.exp(cum[-1])[:, None, None] * state + added
-    return (new_state, inner + carried)
+def entering_state(decay, end_state, state_in):
+    count = lax.axis_size("seq")
+    me = lax.axis_index("seq")
+    first = me == 0
+    got_a, got_s = passed_along((decay, end_state), "seq", 1)
+    acc_a = jnp.where(first, jnp.zeros_like(decay), got_a)
+    acc_s = jnp.where(first, state_in, got_s)
+    step = 1
+    while step < count:
+        far_a, far_s = passed_along((acc_a, acc_s), "seq", step)
+        has = me >= step
+        acc_s = jnp.where(has, acc_a[:, None, None] * far_s + acc_s, acc_s)
+        acc_a = jnp.where(has, acc_a * far_a, acc_a)
+        step *= 2
+    return acc_s
 
 
 def local(
@@ -83,24 +77,42 @@
     c_val = bc_conv[:, nstate:]
     logdec = -decay_code.astype(jnp.float32) / (16.0 * rows * seq_count)
     blocks = rows // Q
-    inputs = (
-        x_conv.reshape(blocks, Q, heads, head_dim),
-        b_val.reshape(blocks, Q, nstate),
-        c_val.reshape(blocks, Q, nstate),
-        logdec.reshape(blocks, Q, heads),
-    )
-    local_state, parts = lax.scan(block_step, jnp.zeros_like(state_in), inputs)
-    parts = parts.reshape(rows, heads, head_dim)
+    xb = x_conv.reshape(blocks, Q, heads, head_dim)
+    bb = b_val.reshape(blocks, Q, nstate)
+    cb = c_val.reshape(blocks, Q, nstate)
+    cum = jnp.cumsum(logdec.reshape(blocks, Q, heads), axis=1)
+
+    tail_decay = jnp.exp(cum[:, -1:, :] - cum)
+    decayed_b = (
+        jnp.transpose(tail_decay, (0, 2, 1))[..., None] * bb.astype(jnp.float32)[:, None]
+    ).astype(jnp.bfloat16)
+    added = jnp.einsum("bhsn,bshp->bhpn", decayed_b, xb, preferred_element_type=jnp.float32)
+    block_decay = jnp.exp(cum[:, -1, :])
+    before = [None]
+    running = added[0]
+    for b in range(1, blocks):
+        before.append(running)
+        running = block_decay[b][:, None, None] * running + added[b]
     cum_range = jnp.cumsum(logdec, axis=0)
     range_decay = jnp.exp(cum_range[-1])
+    incoming = entering_state(range_decay, running, state_in)
 
-    def link(step, incoming):
-        outgoing = range_decay[:, None, None] * incoming + local_state
-        received = passed_along(outgoing, "seq", 1)
-        return jnp.where(first, state_in, received)
+    places = jnp.arange(Q)
+    lower = places[:, None] >= places[None, :]
+    cumt = jnp.transpose(cum, (0, 2, 1))
+    diff = cumt[:, :, :, None] - cumt[:, :, None, :]
+    decay = jnp.where(lower, jnp.exp(jnp.where(lower, diff, 0.0)), 0.0)
+    scores = jnp.einsum("btn,bsn->bts", cb, bb, preferred_element_type=jnp.float32)
+    weights = (decay * scores[:, None]).astype(jnp.bfloat16)
+    parts = jnp.einsum("bhts,bshp->bthp", weights, xb, preferred_element_type=jnp.float32)
+    pieces_out = [parts[0]]
+    for b in range(1, blocks):
+        carried = jnp.einsum(
+            "tn,hpn->thp", cb[b].astype(jnp.float32), before[b], precision=lax.Precision.HIGHEST
+        )
+        pieces_out.append(parts[b] + carried * jnp.exp(cum[b])[:, :, None])
+    parts = jnp.concatenate(pieces_out, axis=0)
 
-    opening = jnp.where(first, state_in, jnp.zeros_like(state_in))
-    incoming = lax.fori_loop(0, seq_count - 1, link, opening)
     correction = jnp.einsum(
         "tn,hpn->thp", c_val.astype(jnp.float32), incoming, precision=lax.Precision.HIGHEST
     )

time: 691 us -> 391 us (0.57)
  waiting for transfers between devices: 379 us -> 246 us
  starting transfers between devices: 164 us -> 57.6 us
  blocking collectives: 45.7 us -> 16.9 us
  local copies, waits for them, and re-layouts: 42.3 us -> 16.5 us
    ppermute x33 -> x13, waiting for transfers between devices: 136 us -> 27.7 us  [passed_along(): return lax.ppermute(value, axis, pairs)]
    ppermute x33 -> x13, starting transfers between devices: 164 us -> 57.5 us  [passed_along(): return lax.ppermute(value, axis, pairs)]
    psum x1, blocking collectives: 45.7 us -> 16.9 us  [local(): total_sq = lax.psum(jnp.sum(gated * gated, axis=1), 'head')]
    dynamic_update_slice x4 -> x0, local copies, waits for them, and re-layouts: 24.1 us -> none  [local(): local_state, parts = lax.scan(block_step, jnp.zeros_like(state_in), inputs)]
    reduce_scatter x1, waiting for transfers between devices: 73.5 us -> 56.2 us  [local(): lax.psum_scatter(partial_out, 'head', scatter_dimension=1, tiled=True)]
    all_gather x1, waiting for transfers between devices: 74.2 us -> 67.2 us  [local(): lax.all_gather(w_bc, 'seq', axis=0, tiled=True)]
  transfers between devices with their start and end apart: 37 -> 17, of which waited for: 36 -> 10; matrix products, arithmetic and copies ran while one was open for 11% -> 12% of each run, Pallas kernels for 0% -> 0%
where the time goes in v1:
time: 391 us
  waiting for transfers between devices  246 us (63%)
  starting transfers between devices  57.6 us (15%)
  matrix products  26.6 us (7%)
  blocking collectives  16.9 us (4%)
  local copies, waits for them, and re-layouts  16.5 us (4%)
  between operations  13.7 us (4%)
  other arithmetic  12.8 us (3%)
    all_gather x1, waiting for transfers between devices, local(): lax.all_gather(w_xz, 'seq', axis=0, tiled=True)  93.9 us
    all_gather x1, waiting for transfers between devices, local(): lax.all_gather(w_bc, 'seq', axis=0, tiled=True)  67.2 us
    ppermute x13, starting transfers between devices, passed_along(): return lax.ppermute(value, axis, pairs)  57.5 us
    reduce_scatter x1, waiting for transfers between devices, local(): lax.psum_scatter(partial_out, 'head', scatter_dimension=1, tiled=True)  56.2 us
    ppermute x13, waiting for transfers between devices, passed_along(): return lax.ppermute(value, axis, pairs)  27.7 us
    psum x1, blocking collectives, local(): total_sq = lax.psum(jnp.sum(gated * gated, axis=1), 'head')  16.9 us
    unnamed x31, local copies, waits for them, and re-layouts  9.4 us
    dot_general x1, matrix products, local(): jnp.dot(tokens, pieces[0].reshape(count, 2 * inner), preferred_element_ty...  9.3 us
  transfers between devices with their start and end apart: 17, of which 10 were waited for; matrix products, arithmetic and copies ran while one was open for 12% of the time, Pallas kernels for 0%

profile of v1, /device:TPU:1, one launch (start us, length us, event | category | flops | bytes accessed | tf_op | source)
XLA Modules:
  0.0 390.6 jit_solution(13135936368089963105)
XLA Ops:
  8.8 1.1 reduce-window.16
  11.6 4.9 %collective-permute-start.2 = (f32[8]{0:T(128)}, f32[8]{0:T(128)}, u32[]{:S(2)}, u32[]{:S(2)}) collective-permute-start(f32[8]{0:T(128)} %fusion.32), channel_id=1, source_target_pairs={{0,8},{8,16},{16,24},{24,32},{32,40},{40,48},{48,56},{56,64},{64,7... | collective-permute-start | bytes 104 | tf_op jit(solution)/shard_map/ppermute | solution.py:12
  16.6 1.2 reduce-window.14
  20.6 67.2 %all-gather.6.cloned.1.call-done = bf16[4096,256]{1,0:T(8,128)(2,1)} async-done(((bf16[128,256]{1,0:T(8,128)(2,1)}), bf16[4096,256]{1,0:T(8,128)(2,1)}) %all-gather.6.cloned.1.call-update) | async-done | bytes 2097168 | tf_op jit(solution)/shard_map/all_gather | solution.py:62
  87.8 4.1 %convolution_convert_fusion.1 = bf16[512,256]{1,0:T(8,128)(2,1)S(1)} fusion(bf16[512,4096]{1,0:T(8,128)(2,1)} %param.12, bf16[4096,256]{1,0:T(8,128)(2,1)} %all-gather.6.cloned.1.call-done), kind=kOutput, calls=%fused_computation.17 | convolution fusion | flops 1073872896 | bytes 6553600 | tf_op jit(solution)/shard_map/dot_general | solution.py:66
  91.9 2.4 collective-permute-start.1
  95.5 93.9 %all-gather.4.cloned.1.call-done = bf16[4096,2,512]{2,1,0:T(2,128)(2,1)} async-done(((bf16[128,2,512]{2,1,0:T(2,128)(2,1)}), bf16[4096,2,512]{2,1,0:T(2,128)(2,1)}) %all-gather.4.cloned.1.call-update) | async-done | bytes 8388624 | tf_op jit(solution)/shard_map/all_gather | solution.py:61
  189.4 9.3 %copy.35 = bf16[512,8,2,512]{3,1,2,0:T(8,128)(2,1)} copy(bf16[512,8,2,512]{3,2,1,0:T(2,128)(2,1)} %bitcast.69) | data formatting | bytes 16777216
  198.7 9.3 %convolution_convert_fusion = bf16[512,1024]{1,0:T(8,128)(2,1)S(1)} fusion(bf16[512,4096]{1,0:T(8,128)(2,1)} %param.12, bf16[4096,1024]{1,0:T(8,128)(2,1)} %bitcast.70), kind=kOutput, calls=%fused_computation.8 | convolution fusion | flops 4295491584 | bytes 13631488 | tf_op jit(solution)/shard_map/dot_general | solution.py:65
  208.1 1.3 collective-permute-start
  212.8 1.9 fusion.14
  215.4 3.8 collective-permute-start.7
  220.8 4.5 %collective-permute-done.7 = f32[8,64,128]{2,1,0:T(8,128)S(1)} collective-permute-done((f32[8,64,128]{2,1,0:T(8,128)S(1)}, f32[8,64,128]{2,1,0:T(8,128)S(1)}, u32[]{:S(2)}, u32[]{:S(2)}) %collective-permute-start.7) | collective-permute-done | bytes 262176 | tf_op jit(solution)/shard_map/ppermute | solution.py:12
  226.2 3.3 collective-permute-start.8
  229.5 3.2 collective-permute-start.3
  233.5 5.8 %collective-permute-start.4 = (f32[8]{0:T(128)S(1)}, f32[8]{0:T(128)S(1)}, u32[]{:S(2)}, u32[]{:S(2)}) collective-permute-start(f32[8]{0:T(128)S(1)} %broadcast_select_fusion.4), channel_id=1, source_target_pairs={{0,16},{8,24},{16,32},{24,40},{32,48},{40,56},{48,64},{56,72},{64,... | collective-permute-start | bytes 104 | tf_op jit(solution)/shard_map/ppermute | solution.py:12
  239.5 4.8 %collective-permute-start.9 = (f32[8,64,128]{2,1,0:T(8,128)S(1)}, f32[8,64,128]{2,1,0:T(8,128)S(1)}, u32[]{:S(2)}, u32[]{:S(2)}) collective-permute-start(f32[8,64,128]{2,1,0:T(8,128)S(1)} %add_select_fusion.4), channel_id=1, source_target_pairs={{0,16},{8,24},{16,32},{24,40},{32,48},{40,56},{48,64},{56,72},{64,... | collective-permute-start | bytes 786440 | tf_op jit(solution)/shard_map/ppermute | solution.py:12
  244.3 6.0 %collective-permute-start.5 = (f32[8]{0:T(128)S(1)}, f32[8]{0:T(128)S(1)}, u32[]{:S(2)}, u32[]{:S(2)}) collective-permute-start(f32[8]{0:T(128)S(1)} %broadcast_select_fusion.5), channel_id=1, source_target_pairs={{0,32},{8,40},{16,48},{24,56},{32,64},{40,72},{48,80},{56,88},{64,... | collective-permute-start | bytes 104 | tf_op jit(solution)/shard_map/ppermute | solution.py:12
  250.4 7.9 %collective-permute-done.5 = f32[8]{0:T(128)S(1)} collective-permute-done((f32[8]{0:T(128)S(1)}, f32[8]{0:T(128)S(1)}, u32[]{:S(2)}, u32[]{:S(2)}) %collective-permute-start.5) | collective-permute-done | bytes 64 | tf_op jit(solution)/shard_map/ppermute | solution.py:12
  258.2 9.1 %collective-permute-start.6 = (f32[8]{0:T(128)S(1)}, f32[8]{0:T(128)S(1)}, u32[]{:S(2)}, u32[]{:S(2)}) collective-permute-start(f32[8]{0:T(128)S(1)} %broadcast_select_fusion.6), channel_id=1, source_target_pairs={{0,64},{8,72},{16,80},{24,88},{32,96},{40,104},{48,112},{56,120},{... | collective-permute-start | bytes 104 | tf_op jit(solution)/shard_map/ppermute | solution.py:12
  267.5 1.3 collective-permute-start.10
  269.9 9.3 %collective-permute-done.10 = f32[8,64,128]{2,1,0:T(8,128)S(1)} collective-permute-done((f32[8,64,128]{2,1,0:T(8,128)S(1)}, f32[8,64,128]{2,1,0:T(8,128)S(1)}, u32[]{:S(2)}, u32[]{:S(2)}) %collective-permute-start.10) | collective-permute-done | bytes 262176 | tf_op jit(solution)/shard_map/ppermute | solution.py:12
  279.3 4.5 %collective-permute-start.11 = (f32[8,64,128]{2,1,0:T(8,128)S(1)}, f32[8,64,128]{2,1,0:T(8,128)S(1)}, u32[]{:S(2)}, u32[]{:S(2)}) collective-permute-start(f32[8,64,128]{2,1,0:T(8,128)S(1)} %add_select_fusion.2), channel_id=1, source_target_pairs={{0,64},{8,72},{16,80},{24,88},{32,96},{40,104},{48,112},{56,120},{... | collective-permute-start | bytes 786440 | tf_op jit(solution)/shard_map/ppermute | solution.py:12
  283.9 1.3 fusion.6
  285.2 2.2 collective-permute-done.11
  287.5 6.9 %collective-permute-start.12 = (f32[8,64,128]{2,1,0:T(8,128)S(1)}, f32[8,64,128]{2,1,0:T(8,128)S(1)}, u32[]{:S(2)}, u32[]{:S(2)}) collective-permute-start(f32[8,64,128]{2,1,0:T(8,128)S(1)} %add_select_fusion.1), channel_id=1, source_target_pairs={{0,128},{8,136},{16,144},{24,152},{32,160},{40,168},{48,176},{56,1... | collective-permute-start | bytes 786440 | tf_op jit(solution)/shard_map/ppermute | solution.py:12
  294.9 2.8 collective-permute-done.12
  298.8 2.1 multiply_reduce_fusion
  301.0 16.9 %psum.7 = f32[512]{0:T(512)S(1)} all-reduce(f32[512]{0:T(512)S(1)} %get-tuple-element.5), channel_id=1, replica_groups=mesh['seq'=32,'head'=8] {'head'}, use_global_device_ids=true, to_apply=%region_5.6 | all-reduce | flops 512 | bytes 4096 | tf_op jit(solution)/shard_map/psum | solution.py:122
  317.9 7.8 %fusion.20 = f32[512,4096]{1,0:T(8,128)} fusion(bf16[512,4096]{1,0:T(8,128)(2,1)} %all-gather.8.cloned.1.call-done, f32[512,512]{1,0:T(8,128)S(1)} %get-tuple-element.6, f32[512]{0:T(512)S(1)} %copy-done.3, f32[512]{0:T(512)S(1)} %add_rsqrt_fusion), kind=kOutput, calls=%fused_computation.36 | convolution fusion | flops 2148270080 | bytes 13635584 | tf_op jit(solution)/shard_map/dot_general | solution.py:125
  325.7 56.2 %reduce-scatter.2.cloned.1.call-done = f32[512,512]{1,0:T(8,128)} async-done(((f32[512,4096]{1,0:T(8,128)}), f32[512,512]{1,0:T(8,128)}) %reduce-scatter.2.cloned.1.call-update) | async-done | bytes 1048592 | tf_op jit(solution)/shard_map/reduce_scatter | solution.py:128
  381.9 2.1 convert_element_type.59
  (97 shorter events, 18.2 us)
Async XLA Ops:
  6.5 81.2 %all-gather.6.cloned.1.call-start = ((), (), s32[]{:S(2)}) async-start(), calls=%async_computation.2 | async-start | bytes 2162688 | tf_op jit(solution)/shard_map/all_gather | solution.py:62
  7.3 182.1 %all-gather.4.cloned.1.call-start = ((), (), s32[]{:S(2)}) async-start(), calls=%async_computation.1 | async-start | bytes 8650752 | tf_op jit(solution)/shard_map/all_gather | solution.py:61
  8.0 87.1 %copy-start.14 = (bf16[3,256]{1,0:T(4,128)(2,1)S(1)}, bf16[3,256]{1,0:T(4,128)(2,1)}, u32[]{:S(2)}) copy-start(bf16[3,256]{1,0:T(4,128)(2,1)} %param.18) | copy-start | bytes 4612
  8.0 309.9 %all-gather.8.cloned.1.call-start = ((), (), s32[]{:S(2)}) async-start(), calls=%async_computation.3 | async-start | bytes 4325376 | tf_op jit(solution)/shard_map/all_gather | solution.py:126
  11.6 218.0 %collective-permute-start.2 = (f32[8]{0:T(128)}, f32[8]{0:T(128)}, u32[]{:S(2)}, u32[]{:S(2)}) collective-permute-start(f32[8]{0:T(128)} %fusion.32), channel_id=1, source_target_pairs={{0,8},{8,16},{16,24},{24,32},{32,40},{40,48},{48,56},{56,64},{64,7... | collective-permute-start | bytes 104 | tf_op jit(solution)/shard_map/ppermute | solution.py:12
  16.5 365.4 %reduce-scatter.2.cloned.1.call-start = ((), (), s32[]{:S(2)}) async-start(), calls=%async_computation.4 | async-start | bytes 9437184 | tf_op jit(solution)/shard_map/reduce_scatter | solution.py:128
  18.0 0.8 copy-start.2
  19.7 191.3 %copy-start.4 = (f32[1,512]{1,0:T(1,128)}, f32[1,512]{1,0:T(1,128)S(1)}, u32[]{:S(2)}) copy-start(f32[1,512]{1,0:T(1,128)S(1)} %get-tuple-element.15) | copy-start | bytes 6148
  19.7 191.3 %copy-start.6 = (f32[1,512]{1,0:T(1,128)}, f32[1,512]{1,0:T(1,128)S(1)}, u32[]{:S(2)}) copy-start(f32[1,512]{1,0:T(1,128)S(1)} %get-tuple-element.16) | copy-start | bytes 6148
  19.7 191.3 %copy-start.8 = (f32[1,512]{1,0:T(1,128)}, f32[1,512]{1,0:T(1,128)S(1)}, u32[]{:S(2)}) copy-start(f32[1,512]{1,0:T(1,128)S(1)} %get-tuple-element.17) | copy-start | bytes 6148
  19.7 191.3 %copy-start.10 = (f32[1,512]{1,0:T(1,128)}, f32[1,512]{1,0:T(1,128)S(1)}, u32[]{:S(2)}) copy-start(f32[1,512]{1,0:T(1,128)S(1)} %get-tuple-element.18) | copy-start | bytes 6148
  91.9 3.2 collective-permute-start.1
  198.7 12.1 %copy-start.13 = (bf16[3,512]{1,0:T(4,128)(2,1)S(1)}, bf16[3,512]{1,0:T(4,128)(2,1)}, u32[]{:S(2)}) copy-start(bf16[3,512]{1,0:T(4,128)(2,1)} %param.17) | copy-start | bytes 9220
  208.0 2.8 copy-start
  208.1 2.7 collective-permute-start
  212.8 71.1 %copy-start.12 = (f32[2,8,256]{2,1,0:T(8,128)S(1)}, f32[2,8,256]{2,1,0:T(8,128)}, u32[]{:S(2)}) copy-start(f32[2,8,256]{2,1,0:T(8,128)} %get-tuple-element.10) | copy-start | bytes 49156
  215.4 9.8 %collective-permute-start.7 = (f32[8,64,128]{2,1,0:T(8,128)S(1)}, f32[8,64,128]{2,1,0:T(8,128)S(1)}, u32[]{:S(2)}, u32[]{:S(2)}) collective-permute-start(f32[8,64,128]{2,1,0:T(8,128)S(1)} %fusion.26), channel_id=1, source_target_pairs={{0,8},{8,16},{16,24},{24,32},{32,40},{40,48},{48,56},{56,64},{64,7... | collective-permute-start | bytes 786440 | tf_op jit(solution)/shard_map/ppermute | solution.py:12
  226.2 13.1 %collective-permute-start.8 = (f32[8,64,128]{2,1,0:T(8,128)S(1)}, f32[8,64,128]{2,1,0:T(8,128)S(1)}, u32[]{:S(2)}, u32[]{:S(2)}) collective-permute-start(f32[8,64,128]{2,1,0:T(8,128)S(1)} %broadcast_select_fusion), channel_id=1, source_target_pairs={{0,8},{8,16},{16,24},{24,32},{32,40},{40,48},{48,56},{56,64},{64,7... | collective-permute-start | bytes 786440 | tf_op jit(solution)/shard_map/ppermute | solution.py:12
  229.5 3.9 %collective-permute-start.3 = (f32[8]{0:T(128)S(1)}, f32[8]{0:T(128)S(1)}, u32[]{:S(2)}, u32[]{:S(2)}) collective-permute-start(f32[8]{0:T(128)S(1)} %broadcast_select_fusion.3), channel_id=1, source_target_pairs={{0,8},{8,16},{16,24},{24,32},{32,40},{40,48},{48,56},{56,64},{64,7... | collective-permute-start | bytes 104 | tf_op jit(solution)/shard_map/ppermute | solution.py:12
  233.5 10.8 %collective-permute-start.4 = (f32[8]{0:T(128)S(1)}, f32[8]{0:T(128)S(1)}, u32[]{:S(2)}, u32[]{:S(2)}) collective-permute-start(f32[8]{0:T(128)S(1)} %broadcast_select_fusion.4), channel_id=1, source_target_pairs={{0,16},{8,24},{16,32},{24,40},{32,48},{40,56},{48,64},{56,72},{64,... | collective-permute-start | bytes 104 | tf_op jit(solution)/shard_map/ppermute | solution.py:12
  239.5 27.9 %collective-permute-start.9 = (f32[8,64,128]{2,1,0:T(8,128)S(1)}, f32[8,64,128]{2,1,0:T(8,128)S(1)}, u32[]{:S(2)}, u32[]{:S(2)}) collective-permute-start(f32[8,64,128]{2,1,0:T(8,128)S(1)} %add_select_fusion.4), channel_id=1, source_target_pairs={{0,16},{8,24},{16,32},{24,40},{32,48},{40,56},{48,64},{56,72},{64,... | collective-permute-start | bytes 786440 | tf_op jit(solution)/shard_map/ppermute | solution.py:12
  244.3 13.9 %collective-permute-start.5 = (f32[8]{0:T(128)S(1)}, f32[8]{0:T(128)S(1)}, u32[]{:S(2)}, u32[]{:S(2)}) collective-permute-start(f32[8]{0:T(128)S(1)} %broadcast_select_fusion.5), channel_id=1, source_target_pairs={{0,32},{8,40},{16,48},{24,56},{32,64},{40,72},{48,80},{56,88},{64,... | collective-permute-start | bytes 104 | tf_op jit(solution)/shard_map/ppermute | solution.py:12
  258.2 10.6 %collective-permute-start.6 = (f32[8]{0:T(128)S(1)}, f32[8]{0:T(128)S(1)}, u32[]{:S(2)}, u32[]{:S(2)}) collective-permute-start(f32[8]{0:T(128)S(1)} %broadcast_select_fusion.6), channel_id=1, source_target_pairs={{0,64},{8,72},{16,80},{24,88},{32,96},{40,104},{48,112},{56,120},{... | collective-permute-start | bytes 104 | tf_op jit(solution)/shard_map/ppermute | solution.py:12
  267.5 11.8 %collective-permute-start.10 = (f32[8,64,128]{2,1,0:T(8,128)S(1)}, f32[8,64,128]{2,1,0:T(8,128)S(1)}, u32[]{:S(2)}, u32[]{:S(2)}) collective-permute-start(f32[8,64,128]{2,1,0:T(8,128)S(1)} %add_select_fusion.3), channel_id=1, source_target_pairs={{0,32},{8,40},{16,48},{24,56},{32,64},{40,72},{48,80},{56,88},{64,... | collective-permute-start | bytes 786440 | tf_op jit(solution)/shard_map/ppermute | solution.py:12
  279.3 8.1 %collective-permute-start.11 = (f32[8,64,128]{2,1,0:T(8,128)S(1)}, f32[8,64,128]{2,1,0:T(8,128)S(1)}, u32[]{:S(2)}, u32[]{:S(2)}) collective-permute-start(f32[8,64,128]{2,1,0:T(8,128)S(1)} %add_select_fusion.2), channel_id=1, source_target_pairs={{0,64},{8,72},{16,80},{24,88},{32,96},{40,104},{48,112},{56,120},{... | collective-permute-start | bytes 786440 | tf_op jit(solution)/shard_map/ppermute | solution.py:12
  283.9 13.9 %copy-start.1 = (f32[512,8]{0,1:T(8,128)S(1)}, f32[512,8]{0,1:T(8,128)}, u32[]{:S(2)}) copy-start(f32[512,8]{0,1:T(8,128)} %get-tuple-element.7) | copy-start | bytes 49156
  285.1 13.7 %copy-start.5 = (f32[1,512]{1,0:T(1,128)S(1)}, f32[1,512]{1,0:T(1,128)}, u32[]{:S(2)}) copy-start(f32[1,512]{1,0:T(1,128)} %copy-done.4) | copy-start | bytes 6148
  285.1 13.7 %copy-start.7 = (f32[1,512]{1,0:T(1,128)S(1)}, f32[1,512]{1,0:T(1,128)}, u32[]{:S(2)}) copy-start(f32[1,512]{1,0:T(1,128)} %copy-done.6) | copy-start | bytes 6148
  285.2 13.7 %copy-start.9 = (f32[1,512]{1,0:T(1,128)S(1)}, f32[1,512]{1,0:T(1,128)}, u32[]{:S(2)}) copy-start(f32[1,512]{1,0:T(1,128)} %copy-done.8) | copy-start | bytes 6148
  285.2 13.7 %copy-start.11 = (f32[1,512]{1,0:T(1,128)S(1)}, f32[1,512]{1,0:T(1,128)}, u32[]{:S(2)}) copy-start(f32[1,512]{1,0:T(1,128)} %copy-done.10) | copy-start | bytes 6148
  287.5 10.2 %collective-permute-start.12 = (f32[8,64,128]{2,1,0:T(8,128)S(1)}, f32[8,64,128]{2,1,0:T(8,128)S(1)}, u32[]{:S(2)}, u32[]{:S(2)}) collective-permute-start(f32[8,64,128]{2,1,0:T(8,128)S(1)} %add_select_fusion.1), channel_id=1, source_target_pairs={{0,128},{8,136},{16,144},{24,152},{32,160},{40,168},{48,176},{56,1... | collective-permute-start | bytes 786440 | tf_op jit(solution)/shard_map/ppermute | solution.py:12
  298.4 19.4 %copy-start.3 = (f32[512]{0:T(512)S(1)}, f32[512]{0:T(512)}, u32[]{:S(2)}) copy-start(f32[512]{0:T(512)} %param.22) | copy-start | bytes 6148
Sparse Core Ops, SparseCore 0:
  9.9 77.7 all-gather.5
  90.4 98.9 all-gather.3
  191.9 97.9 all-gather.7
  325.8 56.0 reduce-scatter.1

commit v2 on v1

--- a/solution.py
+++ b/solution.py
@@ -25,15 +25,20 @@
     count = lax.axis_size("seq")
     me = lax.axis_index("seq")
     first = me == 0
-    got_a, got_s = passed_along((decay, end_state), "seq", 1)
-    acc_a = jnp.where(first, jnp.zeros_like(decay), got_a)
-    acc_s = jnp.where(first, state_in, got_s)
+    lanes = end_state.shape[2]
+
+    def pack(a, s):
+        return jnp.concatenate([s, jnp.broadcast_to(a[:, None, None], (a.shape[0], 1, lanes))], axis=1)
+
+    got = passed_along(pack(decay, end_state), "seq", 1)
+    acc_a = jnp.where(first, jnp.zeros_like(decay), got[:, -1, 0])
+    acc_s = jnp.where(first, state_in, got[:, :-1])
     step = 1
     while step < count:
-        far_a, far_s = passed_along((acc_a, acc_s), "seq", step)
+        far = passed_along(pack(acc_a, acc_s), "seq", step)
         has = me >= step
-        acc_s = jnp.where(has, acc_a[:, None, None] * far_s + acc_s, acc_s)
-        acc_a = jnp.where(has, acc_a * far_a, acc_a)
+        acc_s = jnp.where(has, acc_a[:, None, None] * far[:, :-1] + acc_s, acc_s)
+        acc_a = jnp.where(has, acc_a * far[:, -1, 0], acc_a)
         step *= 2
     return acc_s
 
@@ -57,13 +62,17 @@
     inner = heads * head_dim
     seq_count = lax.axis_size("seq")
     first = lax.axis_index("seq") == 0
-    pieces = (
-        lax.all_gather(w_xz, "seq", axis=0, tiled=True),
-        lax.all_gather(w_bc, "seq", axis=0, tiled=True),
-    )
-    count = pieces[0].shape[0]
-    xz = jnp.dot(tokens, pieces[0].reshape(count, 2 * inner), preferred_element_type=jnp.float32)
-    bc_sum = jnp.dot(tokens, pieces[1], preferred_element_type=jnp.float32)
+    w_x = w_xz[:, 0, :]
+    w_z = w_xz[:, 1, :]
+    w_out_t = jnp.transpose(w_out)
+    widths = (w_x.shape[1], w_z.shape[1], w_bc.shape[1], w_out_t.shape[1])
+    packed = jnp.concatenate([w_x, w_z, w_bc, w_out_t], axis=1)
+    gathered = lax.all_gather(packed, "seq", axis=0, tiled=True)
+    proj = widths[0] + widths[1] + widths[2]
+    xzbc = jnp.dot(tokens, gathered[:, :proj], preferred_element_type=jnp.float32)
+    w_out_cols = gathered[:, proj:]
+    xz = xzbc[:, : 2 * inner]
+    bc_sum = xzbc[:, 2 * inner :]
     x_pre = xz[:, :inner].astype(jnp.bfloat16)
     z_val = xz[:, inner:].astype(jnp.bfloat16)
     bc_pre = bc_sum.astype(jnp.bfloat16)
@@ -122,8 +131,8 @@
     total_sq = lax.psum(jnp.sum(gated * gated, axis=1), "head")
     meansq = total_sq / (inner * lax.axis_size("head"))
     normed = (gated * lax.rsqrt(meansq[:, None] + 1e-05) * norm_gain[None, :]).astype(jnp.bfloat16)
-    partial_out = jnp.dot(
-        normed, lax.all_gather(w_out, "seq", axis=1, tiled=True), preferred_element_type=jnp.float32
+    partial_out = lax.dot_general(
+        normed, w_out_cols, (((1,), (1,)), ((), ())), preferred_element_type=jnp.float32
     )
     result = lax.psum_scatter(partial_out, "head", scatter_dimension=1, tiled=True)
     return result.astype(jnp.bfloat16)

time: 391 us -> 341 us (0.87)
  waiting for transfers between devices: 246 us -> 210 us
  starting transfers between devices: 57.6 us -> 42.4 us
  other arithmetic: 12.8 us -> 20.5 us
  local copies, waits for them, and re-layouts: 16.5 us -> 10.3 us
    all_gather x3 -> x1, waiting for transfers between devices: 161 us -> 133 us  [local(): gathered = lax.all_gather(packed, 'seq', axis=0, tiled=True)]
    ppermute x13 -> x8, starting transfers between devices: 57.5 us -> 42.4 us  [passed_along(): return lax.ppermute(value, axis, pairs)]
    unnamed x31 -> x39, local copies, waits for them, and re-layouts: 9.4 us -> 1.39 us
    select_n x10 -> x12, other arithmetic: 1.41 us -> 7.29 us  [the longest x4 3.26 us: entering_state(): acc_s = jnp.where(has, acc_a[:, None, None] * far[:, :-1] + acc_s, acc_s)]
    reduce_scatter x1, waiting for transfers between devices: 56.2 us -> 52.1 us  [local(): lax.psum_scatter(partial_out, 'head', scatter_dimension=1, tiled=True)]
    ppermute x13 -> x8, waiting for transfers between devices: 27.7 us -> 24.6 us  [passed_along(): return lax.ppermute(value, axis, pairs)]
    dot_general x3 -> x2, matrix products: 21.2 us -> 18.3 us  [the longest x1 10.5 us: local(): jnp.dot(tokens, gathered[:, :proj], preferred_element_type=jnp.float32)]
  transfers between devices with their start and end apart: 17 -> 10, of which waited for: 10 -> 8; matrix products, arithmetic and copies ran while one was open for 12% -> 4% of each run, Pallas kernels for 0% -> 0%
where the time goes in v2:
time: 341 us; the launch traced here: 339 us
  waiting for transfers between devices  210 us (62%)
  starting transfers between devices  42.4 us (12%)
  matrix products  22.9 us (7%)
  other arithmetic  20.5 us (6%)
  blocking collectives  19.7 us (6%)
  between operations  13.9 us (4%)
  local copies, waits for them, and re-layouts  10.3 us (3%)
    all_gather x1, waiting for transfers between devices, local(): gathered = lax.all_gather(packed, 'seq', axis=0, tiled=True)  133 us
    reduce_scatter x1, waiting for transfers between devices, local(): lax.psum_scatter(partial_out, 'head', scatter_dimension=1, tiled=True)  52.1 us
    ppermute x8, starting transfers between devices, passed_along(): return lax.ppermute(value, axis, pairs)  42.4 us
    ppermute x8, waiting for transfers between devices, passed_along(): return lax.ppermute(value, axis, pairs)  24.6 us
    psum x1, blocking collectives, local(): total_sq = lax.psum(jnp.sum(gated * gated, axis=1), 'head')  19.7 us
    dot_general x1, matrix products, local(): jnp.dot(tokens, gathered[:, :proj], preferred_element_type=jnp.float32)  10.5 us
    dot_general x1, matrix products, local(): lax.dot_general(normed, w_out_cols, (((1,), (1,)), ((), ())), preferred_e...  7.87 us
  transfers between devices with their start and end apart: 10, of which 8 were waited for; matrix products, arithmetic and copies ran while one was open for 4% of the time, Pallas kernels for 0%

profile of v2, /device:TPU:1, one launch (start us, length us, event | category | flops | bytes accessed | tf_op | source)
XLA Modules:
  0.0 339.5 jit_solution(3522186953847482299)
XLA Ops:
  6.5 0.9 copy.33
  7.5 1.5 fusion.52
  9.4 1.7 pad_maximum_fusion
  11.9 1.1 reduce-window.16
  13.0 1.1 reduce-window.14
  18.4 133.0 %all-gather.2.cloned.1.call-done = bf16[4096,1792]{0,1:T(8,128)(2,1)} async-done(((bf16[128,1792]{0,1:T(8,128)(2,1)}), bf16[4096,1792]{0,1:T(8,128)(2,1)}) %all-gather.2.cloned.1.call-update) | async-done | bytes 14680080 | tf_op jit(solution)/shard_map/all_gather | solution.py:70
  151.4 10.5 %fusion.7 = bf16[512,1280]{1,0:T(8,128)(2,1)S(1)} fusion(bf16[512,4096]{1,0:T(8,128)(2,1)} %param.12, bf16[4096,1792]{0,1:T(8,128)(2,1)} %all-gather.2.cloned.1.call-done), kind=kOutput, calls=%fused_computation.6 | convolution fusion | flops 5369364480 | bytes 15990784 | tf_op jit(solution)/shard_map/dot_general | solution.py:72
  161.9 2.5 collective-permute-start.1
  165.2 3.5 %collective-permute-start = (bf16[3,512]{1,0:T(4,128)(2,1)S(1)}, bf16[3,512]{1,0:T(4,128)(2,1)S(1)}, u32[]{:S(2)}, u32[]{:S(2)}) collective-permute-start(bf16[3,512]{1,0:T(4,128)(2,1)S(1)} %slice.216), channel_id=1, source_target_pairs={{0,8},{8,16},{16,24},{24,32},{32,40},{40,48},{48,56},{56,64},{64,7... | collective-permute-start | bytes 9224 | tf_op jit(solution)/shard_map/ppermute | solution.py:12
  172.5 2.0 fusion.24
  175.9 2.6 collective-permute-start.2
  178.5 3.6 %collective-permute-done.2 = f32[8,65,128]{2,1,0:T(8,128)S(1)} collective-permute-done((f32[8,65,128]{2,1,0:T(8,128)S(1)}, f32[8,65,128]{2,1,0:T(8,128)S(1)}, u32[]{:S(2)}, u32[]{:S(2)}) %collective-permute-start.2) | collective-permute-done | bytes 266272 | tf_op jit(solution)/shard_map/ppermute | solution.py:12
  182.2 1.0 slice_select_fusion
  183.3 4.0 %collective-permute-start.3 = (f32[8,65,128]{2,1,0:T(8,128)S(1)}, f32[8,65,128]{2,1,0:T(8,128)}, u32[]{:S(2)}, u32[]{:S(2)}) collective-permute-start(f32[8,65,128]{2,1,0:T(8,128)S(1)} %pad_maximum_fusion.2), channel_id=1, source_target_pairs={{0,8},{8,16},{16,24},{24,32},{32,40},{40,48},{48,56},{56,64},{64,7... | collective-permute-start | bytes 798728 | tf_op jit(solution)/shard_map/ppermute | solution.py:12
  187.4 2.9 collective-permute-done.3
  191.2 1.1 add_select_fusion.4
  192.4 4.9 %collective-permute-start.4 = (f32[8,65,128]{2,1,0:T(8,128)S(1)}, f32[8,65,128]{2,1,0:T(8,128)}, u32[]{:S(2)}, u32[]{:S(2)}) collective-permute-start(f32[8,65,128]{2,1,0:T(8,128)S(1)} %pad_maximum_fusion.3), channel_id=1, source_target_pairs={{0,16},{8,24},{16,32},{24,40},{32,48},{40,56},{48,64},{56,72},{64,... | collective-permute-start | bytes 798728 | tf_op jit(solution)/shard_map/ppermute | solution.py:12
  198.0 2.3 collective-permute-done.4
  201.2 1.1 add_select_fusion.3
  202.4 13.9 %collective-permute-start.5 = (f32[8,65,128]{2,1,0:T(8,128)S(1)}, f32[8,65,128]{2,1,0:T(8,128)}, u32[]{:S(2)}, u32[]{:S(2)}) collective-permute-start(f32[8,65,128]{2,1,0:T(8,128)S(1)} %pad_maximum_fusion.4), channel_id=1, source_target_pairs={{0,32},{8,40},{16,48},{24,56},{32,64},{40,72},{48,80},{56,88},{64,... | collective-permute-start | bytes 798728 | tf_op jit(solution)/shard_map/ppermute | solution.py:12
  216.7 5.7 %collective-permute-done.5 = f32[8,65,128]{2,1,0:T(8,128)} collective-permute-done((f32[8,65,128]{2,1,0:T(8,128)S(1)}, f32[8,65,128]{2,1,0:T(8,128)}, u32[]{:S(2)}, u32[]{:S(2)}) %collective-permute-start.5) | collective-permute-done | bytes 266272 | tf_op jit(solution)/shard_map/ppermute | solution.py:12
  222.4 1.1 add_select_fusion.2
  224.5 5.7 %collective-permute-start.6 = (f32[8,65,128]{2,1,0:T(8,128)S(1)}, f32[8,65,128]{2,1,0:T(8,128)S(1)}, u32[]{:S(2)}, u32[]{:S(2)}) collective-permute-start(f32[8,65,128]{2,1,0:T(8,128)S(1)} %pad_maximum_fusion.5), channel_id=1, source_target_pairs={{0,64},{8,72},{16,80},{24,88},{32,96},{40,104},{48,112},{56,120},{... | collective-permute-start | bytes 798728 | tf_op jit(solution)/shard_map/ppermute | solution.py:12
  230.2 1.3 fusion.16
  231.5 4.3 %collective-permute-done.6 = f32[8,65,128]{2,1,0:T(8,128)S(1)} collective-permute-done((f32[8,65,128]{2,1,0:T(8,128)S(1)}, f32[8,65,128]{2,1,0:T(8,128)S(1)}, u32[]{:S(2)}, u32[]{:S(2)}) %collective-permute-start.6) | collective-permute-done | bytes 266272 | tf_op jit(solution)/shard_map/ppermute | solution.py:12
  236.1 5.2 %collective-permute-start.7 = (f32[8,65,128]{2,1,0:T(8,128)S(1)}, f32[8,65,128]{2,1,0:T(8,128)S(1)}, u32[]{:S(2)}, u32[]{:S(2)}) collective-permute-start(f32[8,65,128]{2,1,0:T(8,128)S(1)} %pad_maximum_fusion.6), channel_id=1, source_target_pairs={{0,128},{8,136},{16,144},{24,152},{32,160},{40,168},{48,176},{56,1... | collective-permute-start | bytes 798728 | tf_op jit(solution)/shard_map/ppermute | solution.py:12
  241.8 5.8 %collective-permute-done.7 = f32[8,65,128]{2,1,0:T(8,128)S(1)} collective-permute-done((f32[8,65,128]{2,1,0:T(8,128)S(1)}, f32[8,65,128]{2,1,0:T(8,128)S(1)}, u32[]{:S(2)}, u32[]{:S(2)}) %collective-permute-start.7) | collective-permute-done | bytes 266272 | tf_op jit(solution)/shard_map/ppermute | solution.py:12
  248.7 2.1 multiply_reduce_fusion
  250.8 19.7 %psum.7 = f32[512]{0:T(512)S(1)} all-reduce(f32[512]{0:T(512)S(1)} %get-tuple-element.7), channel_id=1, replica_groups=mesh['seq'=32,'head'=8] {'head'}, use_global_device_ids=true, to_apply=%region_5.6 | all-reduce | flops 512 | bytes 4096 | tf_op jit(solution)/shard_map/psum | solution.py:131
  270.5 7.9 %fusion.2 = f32[512,4096]{1,0:T(8,128)} fusion(bf16[4096,1792]{0,1:T(8,128)(2,1)} %all-gather.2.cloned.1.call-done, f32[512,512]{1,0:T(8,128)S(1)} %get-tuple-element.8, f32[512]{0:T(512)S(1)} %copy-done.5, f32[512]{0:T(512)S(1)} %add_rsqrt_fusion), kind=kOutput, calls=%fused_computation.2 | convolution fusion | flops 2148270080 | bytes 13635584 | tf_op jit(solution)/shard_map/dot_general | solution.py:134
  278.4 52.1 %reduce-scatter.2.cloned.1.call-done = f32[512,512]{1,0:T(8,128)} async-done(((f32[512,4096]{1,0:T(8,128)}), f32[512,512]{1,0:T(8,128)}) %reduce-scatter.2.cloned.1.call-update) | async-done | bytes 1048592 | tf_op jit(solution)/shard_map/reduce_scatter | solution.py:137
  330.5 2.1 convert_element_type.56
  (105 shorter events, 17.4 us)
Async XLA Ops:
  6.5 144.9 %all-gather.2.cloned.1.call-start = ((), (), s32[]{:S(2)}) async-start(), calls=%async_computation.1 | async-start | bytes 15138816 | tf_op jit(solution)/shard_map/all_gather | solution.py:70
  11.1 319.5 %reduce-scatter.2.cloned.1.call-start = ((), (), s32[]{:S(2)}) async-start(), calls=%async_computation.2 | async-start | bytes 9437184 | tf_op jit(solution)/shard_map/reduce_scatter | solution.py:137
  14.6 3.1 copy-start.4
  17.0 153.7 %copy-start.6 = (f32[1,512]{1,0:T(1,128)}, f32[1,512]{1,0:T(1,128)S(1)}, u32[]{:S(2)}) copy-start(f32[1,512]{1,0:T(1,128)S(1)} %get-tuple-element.32) | copy-start | bytes 6148
  17.0 153.7 %copy-start.8 = (f32[1,512]{1,0:T(1,128)}, f32[1,512]{1,0:T(1,128)S(1)}, u32[]{:S(2)}) copy-start(f32[1,512]{1,0:T(1,128)S(1)} %get-tuple-element.33) | copy-start | bytes 6148
  17.0 153.7 %copy-start.10 = (f32[1,512]{1,0:T(1,128)}, f32[1,512]{1,0:T(1,128)S(1)}, u32[]{:S(2)}) copy-start(f32[1,512]{1,0:T(1,128)S(1)} %get-tuple-element.34) | copy-start | bytes 6148
  17.0 153.7 %copy-start.12 = (f32[1,512]{1,0:T(1,128)}, f32[1,512]{1,0:T(1,128)S(1)}, u32[]{:S(2)}) copy-start(f32[1,512]{1,0:T(1,128)S(1)} %get-tuple-element.35) | copy-start | bytes 6148
  18.4 150.3 %copy-start.16 = (bf16[3,256]{1,0:T(4,128)(2,1)S(1)}, bf16[3,256]{1,0:T(4,128)(2,1)}, u32[]{:S(2)}) copy-start(bf16[3,256]{1,0:T(4,128)(2,1)} %param.18) | copy-start | bytes 4612
  161.9 6.9 %copy-start = (bf16[512,1280]{1,0:T(8,128)(2,1)}, bf16[512,1280]{1,0:T(8,128)(2,1)S(1)}, u32[]{:S(2)}) copy-start(bf16[512,1280]{1,0:T(8,128)(2,1)S(1)} %fusion.7) | copy-start | bytes 3932164
  161.9 8.6 %copy-start.15 = (bf16[3,512]{1,0:T(4,128)(2,1)S(1)}, bf16[3,512]{1,0:T(4,128)(2,1)}, u32[]{:S(2)}) copy-start(bf16[3,512]{1,0:T(4,128)(2,1)} %param.17) | copy-start | bytes 9220
  161.9 6.8 %collective-permute-start.1 = (bf16[3,256]{1,0:T(4,128)(2,1)S(1)}, bf16[3,256]{1,0:T(4,128)(2,1)S(1)}, u32[]{:S(2)}, u32[]{:S(2)}) collective-permute-start(bf16[3,256]{1,0:T(4,128)(2,1)S(1)} %slice.224), channel_id=1, source_target_pairs={{0,8},{8,16},{16,24},{24,32},{32,40},{40,48},{48,56},{56,64},{64,7... | collective-permute-start | bytes 4616 | tf_op jit(solution)/shard_map/ppermute | solution.py:12
  165.2 5.3 %collective-permute-start = (bf16[3,512]{1,0:T(4,128)(2,1)S(1)}, bf16[3,512]{1,0:T(4,128)(2,1)S(1)}, u32[]{:S(2)}, u32[]{:S(2)}) collective-permute-start(bf16[3,512]{1,0:T(4,128)(2,1)S(1)} %slice.216), channel_id=1, source_target_pairs={{0,8},{8,16},{16,24},{24,32},{32,40},{40,48},{48,56},{56,64},{64,7... | collective-permute-start | bytes 9224 | tf_op jit(solution)/shard_map/ppermute | solution.py:12
  172.5 43.8 %copy-start.17 = (f32[8]{0:T(128)S(1)}, f32[8]{0:T(128)}, u32[]{:S(2)}) copy-start(f32[8]{0:T(128)} %param.20) | copy-start | bytes 100
  172.5 44.0 %copy-start.1 = (bf16[512,128]{1,0:T(8,128)(2,1)S(1)}, bf16[512,128]{1,0:T(8,128)(2,1)}, u32[]{:S(2)}) copy-start(bf16[512,128]{1,0:T(8,128)(2,1)} %get-tuple-element.27) | copy-start | bytes 393220
  174.5 55.7 %copy-start.14 = (f32[2,8,256]{2,1,0:T(8,128)S(1)}, f32[2,8,256]{2,1,0:T(8,128)}, u32[]{:S(2)}) copy-start(f32[2,8,256]{2,1,0:T(8,128)} %get-tuple-element.22) | copy-start | bytes 49156
  175.9 6.2 %collective-permute-start.2 = (f32[8,65,128]{2,1,0:T(8,128)S(1)}, f32[8,65,128]{2,1,0:T(8,128)S(1)}, u32[]{:S(2)}, u32[]{:S(2)}) collective-permute-start(f32[8,65,128]{2,1,0:T(8,128)S(1)} %pad_maximum_fusion.1), channel_id=1, source_target_pairs={{0,8},{8,16},{16,24},{24,32},{32,40},{40,48},{48,56},{56,64},{64,7... | collective-permute-start | bytes 798728 | tf_op jit(solution)/shard_map/ppermute | solution.py:12
  182.1 1.2 copy-start.2
  183.3 7.0 %collective-permute-start.3 = (f32[8,65,128]{2,1,0:T(8,128)S(1)}, f32[8,65,128]{2,1,0:T(8,128)}, u32[]{:S(2)}, u32[]{:S(2)}) collective-permute-start(f32[8,65,128]{2,1,0:T(8,128)S(1)} %pad_maximum_fusion.2), channel_id=1, source_target_pairs={{0,8},{8,16},{16,24},{24,32},{32,40},{40,48},{48,56},{56,64},{64,7... | collective-permute-start | bytes 798728 | tf_op jit(solution)/shard_map/ppermute | solution.py:12
  192.4 7.9 %collective-permute-start.4 = (f32[8,65,128]{2,1,0:T(8,128)S(1)}, f32[8,65,128]{2,1,0:T(8,128)}, u32[]{:S(2)}, u32[]{:S(2)}) collective-permute-start(f32[8,65,128]{2,1,0:T(8,128)S(1)} %pad_maximum_fusion.3), channel_id=1, source_target_pairs={{0,16},{8,24},{16,32},{24,40},{32,48},{40,56},{48,64},{56,72},{64,... | collective-permute-start | bytes 798728 | tf_op jit(solution)/shard_map/ppermute | solution.py:12
  202.4 20.0 %collective-permute-start.5 = (f32[8,65,128]{2,1,0:T(8,128)S(1)}, f32[8,65,128]{2,1,0:T(8,128)}, u32[]{:S(2)}, u32[]{:S(2)}) collective-permute-start(f32[8,65,128]{2,1,0:T(8,128)S(1)} %pad_maximum_fusion.4), channel_id=1, source_target_pairs={{0,32},{8,40},{16,48},{24,56},{32,64},{40,72},{48,80},{56,88},{64,... | collective-permute-start | bytes 798728 | tf_op jit(solution)/shard_map/ppermute | solution.py:12
  224.5 11.3 %collective-permute-start.6 = (f32[8,65,128]{2,1,0:T(8,128)S(1)}, f32[8,65,128]{2,1,0:T(8,128)S(1)}, u32[]{:S(2)}, u32[]{:S(2)}) collective-permute-start(f32[8,65,128]{2,1,0:T(8,128)S(1)} %pad_maximum_fusion.5), channel_id=1, source_target_pairs={{0,64},{8,72},{16,80},{24,88},{32,96},{40,104},{48,112},{56,120},{... | collective-permute-start | bytes 798728 | tf_op jit(solution)/shard_map/ppermute | solution.py:12
  230.2 17.4 %copy-start.3 = (f32[512,8]{0,1:T(8,128)S(1)}, f32[512,8]{0,1:T(8,128)}, u32[]{:S(2)}) copy-start(f32[512,8]{0,1:T(8,128)} %get-tuple-element.19) | copy-start | bytes 49156
  235.9 12.8 %copy-start.7 = (f32[1,512]{1,0:T(1,128)S(1)}, f32[1,512]{1,0:T(1,128)}, u32[]{:S(2)}) copy-start(f32[1,512]{1,0:T(1,128)} %copy-done.6) | copy-start | bytes 6148
  235.9 12.8 %copy-start.9 = (f32[1,512]{1,0:T(1,128)S(1)}, f32[1,512]{1,0:T(1,128)}, u32[]{:S(2)}) copy-start(f32[1,512]{1,0:T(1,128)} %copy-done.8) | copy-start | bytes 6148
  235.9 12.8 %copy-start.11 = (f32[1,512]{1,0:T(1,128)S(1)}, f32[1,512]{1,0:T(1,128)}, u32[]{:S(2)}) copy-start(f32[1,512]{1,0:T(1,128)} %copy-done.10) | copy-start | bytes 6148
  235.9 12.8 %copy-start.13 = (f32[1,512]{1,0:T(1,128)S(1)}, f32[1,512]{1,0:T(1,128)}, u32[]{:S(2)}) copy-start(f32[1,512]{1,0:T(1,128)} %copy-done.12) | copy-start | bytes 6148
  236.1 11.5 %collective-permute-start.7 = (f32[8,65,128]{2,1,0:T(8,128)S(1)}, f32[8,65,128]{2,1,0:T(8,128)S(1)}, u32[]{:S(2)}, u32[]{:S(2)}) collective-permute-start(f32[8,65,128]{2,1,0:T(8,128)S(1)} %pad_maximum_fusion.6), channel_id=1, source_target_pairs={{0,128},{8,136},{16,144},{24,152},{32,160},{40,168},{48,176},{56,1... | collective-permute-start | bytes 798728 | tf_op jit(solution)/shard_map/ppermute | solution.py:12
  248.3 22.2 %copy-start.5 = (f32[512]{0:T(512)S(1)}, f32[512]{0:T(512)}, u32[]{:S(2)}) copy-start(f32[512]{0:T(512)} %param.22) | copy-start | bytes 6148
Sparse Core Ops, SparseCore 0:
  11.2 140.1 all-gather.1
  278.5 51.9 reduce-scatter.1

commit v3 on v2

--- a/solution.py
+++ b/solution.py
@@ -21,26 +21,43 @@
     return jax.nn.silu(total).astype(jnp.bfloat16)
 
 
+def compose(later, earlier):
+    return later[0] * earlier[0], later[0][:, None, None] * earlier[1] + later[1]
+
+
 def entering_state(decay, end_state, state_in):
     count = lax.axis_size("seq")
     me = lax.axis_index("seq")
-    first = me == 0
     lanes = end_state.shape[2]
+    ones = jnp.ones_like(decay)
+    zeros = jnp.zeros_like(end_state)
 
     def pack(a, s):
         return jnp.concatenate([s, jnp.broadcast_to(a[:, None, None], (a.shape[0], 1, lanes))], axis=1)
 
-    got = passed_along(pack(decay, end_state), "seq", 1)
-    acc_a = jnp.where(first, jnp.zeros_like(decay), got[:, -1, 0])
-    acc_s = jnp.where(first, state_in, got[:, :-1])
-    step = 1
-    while step < count:
-        far = passed_along(pack(acc_a, acc_s), "seq", step)
-        has = me >= step
-        acc_s = jnp.where(has, acc_a[:, None, None] * far[:, :-1] + acc_s, acc_s)
-        acc_a = jnp.where(has, acc_a * far[:, -1, 0], acc_a)
-        step *= 2
-    return acc_s
+    def unpack(m):
+        return m[:, -1, 0], m[:, :-1]
+
+    message = pack(decay, end_state)
+    width = min(4, count)
+    got = [unpack(passed_along(message, "seq", k)) for k in range(1, width + 1)]
+    acc = (ones, zeros)
+    for k in range(width, 0, -1):
+        src = me - k
+        ga = jnp.where(src >= 0, got[k - 1][0], jnp.where(src == -1, 0.0, 1.0))
+        gs = jnp.where(src >= 0, got[k - 1][1], jnp.where(src == -1, state_in, zeros))
+        acc = compose((ga, gs), acc)
+    span = width
+    while span < count:
+        radix = min(4, -(-count // span))
+        message = pack(*acc)
+        got = [unpack(passed_along(message, "seq", m * span)) for m in range(1, radix)]
+        for m in range(1, radix):
+            valid = me - m * span >= 0
+            piece = (jnp.where(valid, got[m - 1][0], ones), jnp.where(valid, got[m - 1][1], zeros))
+            acc = compose(acc, piece)
+        span *= radix
+    return acc[1]
 
 
 def local(
@@ -128,14 +145,14 @@
     parts = (parts + correction * jnp.exp(cum_range)[:, :, None]).reshape(rows, inner)
     y_val = parts / nstate + jnp.repeat(skip_gain, head_dim)[None, :] * x_conv.astype(jnp.float32)
     gated = y_val * jax.nn.silu(z_val.astype(jnp.float32))
+    scaled = (gated * norm_gain[None, :]).astype(jnp.bfloat16)
+    partial_out = lax.dot_general(
+        scaled, w_out_cols, (((1,), (1,)), ((), ())), preferred_element_type=jnp.float32
+    )
+    result = lax.psum_scatter(partial_out, "head", scatter_dimension=1, tiled=True)
     total_sq = lax.psum(jnp.sum(gated * gated, axis=1), "head")
     meansq = total_sq / (inner * lax.axis_size("head"))
-    normed = (gated * lax.rsqrt(meansq[:, None] + 1e-05) * norm_gain[None, :]).astype(jnp.bfloat16)
-    partial_out = lax.dot_general(
-        normed, w_out_cols, (((1,), (1,)), ((), ())), preferred_element_type=jnp.float32
-    )
-    result = lax.psum_scatter(partial_out, "head", scatter_dimension=1, tiled=True)
-    return result.astype(jnp.bfloat16)
+    return (result * lax.rsqrt(meansq[:, None] + 1e-05)).astype(jnp.bfloat16)
 
 
 def solution(mesh):

time: 341 us -> 354 us (1.038)
  waiting for transfers between devices: 210 us -> 228 us
  blocking collectives: 19.7 us -> 14.1 us
  other arithmetic: 20.5 us -> 15.9 us
  starting transfers between devices: 42.4 us -> 46.9 us
    ppermute x8 -> x10, waiting for transfers between devices: 24.6 us -> 55.7 us  [passed_along(): return lax.ppermute(value, axis, pairs)]
    reduce_scatter x1, waiting for transfers between devices: 52.1 us -> 39.5 us  [local(): lax.psum_scatter(partial_out, 'head', scatter_dimension=1, tiled=True)]
    select_n x12 -> x1, other arithmetic: 7.29 us -> 0.15 us  [entering_state(): jnp.where(valid, got[m - 1][0], ones)]
    psum x1, blocking collectives: 19.7 us -> 14.1 us  [local(): total_sq = lax.psum(jnp.sum(gated * gated, axis=1), 'head')]
    ppermute x8 -> x10, starting transfers between devices: 42.4 us -> 46.9 us  [passed_along(): return lax.ppermute(value, axis, pairs)]
  transfers between devices with their start and end apart: 10 -> 12, of which waited for: 8 -> 7; matrix products, arithmetic and copies ran while one was open for 4% -> 4% of each run, Pallas kernels for 0% -> 0%
where the time goes in v3:
time: 354 us
  waiting for transfers between devices  228 us (64%)
  starting transfers between devices  46.9 us (13%)
  matrix products  24.5 us (7%)
  other arithmetic  15.9 us (4%)
  blocking collectives  14.1 us (4%)
  between operations  13.9 us (4%)
  local copies, waits for them, and re-layouts  10.7 us (3%)
    all_gather x1, waiting for transfers between devices, local(): gathered = lax.all_gather(packed, 'seq', axis=0, tiled=True)  132 us
    ppermute x10, waiting for transfers between devices, passed_along(): return lax.ppermute(value, axis, pairs)  55.7 us
    ppermute x10, starting transfers between devices, passed_along(): return lax.ppermute(value, axis, pairs)  46.9 us
    reduce_scatter x1, waiting for transfers between devices, local(): lax.psum_scatter(partial_out, 'head', scatter_dimension=1, tiled=True)  39.5 us
    psum x1, blocking collectives, local(): total_sq = lax.psum(jnp.sum(gated * gated, axis=1), 'head')  14.1 us
    dot_general x1, matrix products, local(): jnp.dot(tokens, gathered[:, :proj], preferred_element_type=jnp.float32)  10.5 us
    dot_general x1, matrix products, local(): lax.dot_general(scaled, w_out_cols, (((1,), (1,)), ((), ())), preferred_e...  7.82 us
  transfers between devices with their start and end apart: 12, of which 7 were waited for; matrix products, arithmetic and copies ran while one was open for 4% of the time, Pallas kernels for 0%

profile of v3, /device:TPU:1, one launch (start us, length us, event | category | flops | bytes accessed | tf_op | source)
XLA Modules:
  0.0 353.6 jit_solution(4038845594887935803)
XLA Ops:
  6.5 0.9 copy.33
  7.5 1.5 fusion.72
  9.4 1.7 pad_maximum_fusion
  11.9 1.1 reduce-window.16
  13.0 1.1 reduce-window.14
  19.0 132.4 %all-gather.2.cloned.1.call-done = bf16[4096,1792]{0,1:T(8,128)(2,1)} async-done(((bf16[128,1792]{0,1:T(8,128)(2,1)}), bf16[4096,1792]{0,1:T(8,128)(2,1)}) %all-gather.2.cloned.1.call-update) | async-done | bytes 14680080 | tf_op jit(solution)/shard_map/all_gather | solution.py:87
  151.4 10.5 %fusion.7 = bf16[512,1280]{1,0:T(8,128)(2,1)S(1)} fusion(bf16[512,4096]{1,0:T(8,128)(2,1)} %param.12, bf16[4096,1792]{0,1:T(8,128)(2,1)} %all-gather.2.cloned.1.call-done), kind=kOutput, calls=%fused_computation.6 | convolution fusion | flops 5369364480 | bytes 15990784 | tf_op jit(solution)/shard_map/dot_general | solution.py:89
  161.9 2.5 collective-permute-start.1
  165.2 3.5 collective-permute-start
  172.5 1.9 fusion.24
  175.8 4.5 %collective-permute-start.5 = (f32[8,65,128]{2,1,0:T(8,128)S(1)}, f32[8,65,128]{2,1,0:T(8,128)S(1)}, u32[]{:S(2)}, u32[]{:S(2)}) collective-permute-start(f32[8,65,128]{2,1,0:T(8,128)S(1)} %pad_maximum_fusion.1), channel_id=1, source_target_pairs={{0,32},{8,40},{16,48},{24,56},{32,64},{40,72},{48,80},{56,88},{64,... | collective-permute-start | bytes 798728 | tf_op jit(solution)/shard_map/ppermute | solution.py:12
  180.3 3.0 collective-permute-start.4
  183.3 3.4 collective-permute-start.3
  186.7 3.9 %collective-permute-start.2 = (f32[8,65,128]{2,1,0:T(8,128)S(1)}, f32[8,65,128]{2,1,0:T(8,128)}, u32[]{:S(2)}, u32[]{:S(2)}) collective-permute-start(f32[8,65,128]{2,1,0:T(8,128)S(1)} %pad_maximum_fusion.1), channel_id=1, source_target_pairs={{0,8},{8,16},{16,24},{24,32},{32,40},{40,48},{48,56},{56,64},{64,7... | collective-permute-start | bytes 798728 | tf_op jit(solution)/shard_map/ppermute | solution.py:12
  191.5 1.1 fusion.75
  192.6 10.8 %collective-permute-done.4 = f32[8,65,128]{2,1,0:T(8,128)S(1)} collective-permute-done((f32[8,65,128]{2,1,0:T(8,128)S(1)}, f32[8,65,128]{2,1,0:T(8,128)S(1)}, u32[]{:S(2)}, u32[]{:S(2)}) %collective-permute-start.4) | collective-permute-done | bytes 266272 | tf_op jit(solution)/shard_map/ppermute | solution.py:12
  203.4 14.3 %collective-permute-done.3 = f32[8,65,128]{2,1,0:T(8,128)} collective-permute-done((f32[8,65,128]{2,1,0:T(8,128)S(1)}, f32[8,65,128]{2,1,0:T(8,128)}, u32[]{:S(2)}, u32[]{:S(2)}) %collective-permute-start.3) | collective-permute-done | bytes 266272 | tf_op jit(solution)/shard_map/ppermute | solution.py:12
  217.8 11.6 %collective-permute-done.2 = f32[8,65,128]{2,1,0:T(8,128)} collective-permute-done((f32[8,65,128]{2,1,0:T(8,128)S(1)}, f32[8,65,128]{2,1,0:T(8,128)}, u32[]{:S(2)}, u32[]{:S(2)}) %collective-permute-start.2) | collective-permute-done | bytes 266272 | tf_op jit(solution)/shard_map/ppermute | solution.py:12
  229.3 0.9 fusion.69
  230.3 1.3 fusion.43
  231.7 9.2 %collective-permute-start.8 = (f32[8,65,128]{2,1,0:T(8,128)S(1)}, f32[8,65,128]{2,1,0:T(8,128)S(1)}, u32[]{:S(2)}, u32[]{:S(2)}) collective-permute-start(f32[8,65,128]{2,1,0:T(8,128)S(1)} %pad_maximum_fusion.2), channel_id=1, source_target_pairs={{0,96},{8,104},{16,112},{24,120},{32,128},{40,136},{48,144},{56,15... | collective-permute-start | bytes 798728 | tf_op jit(solution)/shard_map/ppermute | solution.py:12
  240.8 3.4 collective-permute-start.7
  244.2 5.0 %collective-permute-start.6 = (f32[8,65,128]{2,1,0:T(8,128)S(1)}, f32[8,65,128]{2,1,0:T(8,128)S(1)}, u32[]{:S(2)}, u32[]{:S(2)}) collective-permute-start(f32[8,65,128]{2,1,0:T(8,128)S(1)} %pad_maximum_fusion.2), channel_id=1, source_target_pairs={{0,32},{8,40},{16,48},{24,56},{32,64},{40,72},{48,80},{56,88},{64,... | collective-permute-start | bytes 798728 | tf_op jit(solution)/shard_map/ppermute | solution.py:12
  249.3 2.0 fusion.16
  251.3 14.8 %collective-permute-done.6 = f32[8,65,128]{2,1,0:T(8,128)S(1)} collective-permute-done((f32[8,65,128]{2,1,0:T(8,128)S(1)}, f32[8,65,128]{2,1,0:T(8,128)S(1)}, u32[]{:S(2)}, u32[]{:S(2)}) %collective-permute-start.6) | collective-permute-done | bytes 266272 | tf_op jit(solution)/shard_map/ppermute | solution.py:12
  266.7 8.5 %collective-permute-start.9 = (f32[8,65,128]{2,1,0:T(8,128)S(1)}, f32[8,65,128]{2,1,0:T(8,128)S(1)}, u32[]{:S(2)}, u32[]{:S(2)}) collective-permute-start(f32[8,65,128]{2,1,0:T(8,128)S(1)} %pad_maximum_fusion.3), channel_id=1, source_target_pairs={{0,128},{8,136},{16,144},{24,152},{32,160},{40,168},{48,176},{56,1... | collective-permute-start | bytes 798728 | tf_op jit(solution)/shard_map/ppermute | solution.py:12
  275.7 4.2 %collective-permute-done.9 = f32[8,65,128]{2,1,0:T(8,128)S(1)} collective-permute-done((f32[8,65,128]{2,1,0:T(8,128)S(1)}, f32[8,65,128]{2,1,0:T(8,128)S(1)}, u32[]{:S(2)}, u32[]{:S(2)}) %collective-permute-start.9) | collective-permute-done | bytes 266272 | tf_op jit(solution)/shard_map/ppermute | solution.py:12
  280.9 2.1 multiply_reduce_fusion
  283.1 7.8 %fusion.2 = f32[512,4096]{1,0:T(8,128)} fusion(bf16[4096,1792]{0,1:T(8,128)(2,1)} %all-gather.2.cloned.1.call-done, f32[512,512]{1,0:T(8,128)S(1)} %get-tuple-element.11, f32[512]{0:T(512)S(1)} %copy-done.2), kind=kOutput, calls=%fused_computation.2 | convolution fusion | flops 2148007936 | bytes 13633536 | tf_op jit(solution)/shard_map/dot_general | solution.py:149
  290.9 14.1 %psum.7 = f32[512]{0:T(512)S(1)} all-reduce(f32[512]{0:T(512)S(1)} %get-tuple-element.10), channel_id=1, replica_groups=mesh['seq'=32,'head'=8] {'head'}, use_global_device_ids=true, to_apply=%region_6.7 | all-reduce | flops 512 | bytes 4096 | tf_op jit(solution)/shard_map/psum | solution.py:153
  305.1 39.5 %reduce-scatter.2.cloned.1.call-done = f32[512,512]{1,0:T(8,128)} async-done(((f32[512,4096]{1,0:T(8,128)}), f32[512,512]{1,0:T(8,128)}) %reduce-scatter.2.cloned.1.call-update) | async-done | bytes 1048592 | tf_op jit(solution)/shard_map/reduce_scatter | solution.py:152
  344.6 2.2 multiply_convert_fusion.6
  (89 shorter events, 14.8 us)
Async XLA Ops:
  6.5 144.9 %all-gather.2.cloned.1.call-start = ((), (), s32[]{:S(2)}) async-start(), calls=%async_computation.1 | async-start | bytes 15138816 | tf_op jit(solution)/shard_map/all_gather | solution.py:87
  11.1 333.5 %reduce-scatter.2.cloned.1.call-start = ((), (), s32[]{:S(2)}) async-start(), calls=%async_computation.2 | async-start | bytes 9437184 | tf_op jit(solution)/shard_map/reduce_scatter | solution.py:152
  17.6 153.1 %copy-start.4 = (f32[1,512]{1,0:T(1,128)}, f32[1,512]{1,0:T(1,128)S(1)}, u32[]{:S(2)}) copy-start(f32[1,512]{1,0:T(1,128)S(1)} %get-tuple-element.30) | copy-start | bytes 6148
  17.6 153.1 %copy-start.6 = (f32[1,512]{1,0:T(1,128)}, f32[1,512]{1,0:T(1,128)S(1)}, u32[]{:S(2)}) copy-start(f32[1,512]{1,0:T(1,128)S(1)} %get-tuple-element.31) | copy-start | bytes 6148
  17.6 153.1 %copy-start.8 = (f32[1,512]{1,0:T(1,128)}, f32[1,512]{1,0:T(1,128)S(1)}, u32[]{:S(2)}) copy-start(f32[1,512]{1,0:T(1,128)S(1)} %get-tuple-element.32) | copy-start | bytes 6148
  17.6 153.1 %copy-start.10 = (f32[1,512]{1,0:T(1,128)}, f32[1,512]{1,0:T(1,128)S(1)}, u32[]{:S(2)}) copy-start(f32[1,512]{1,0:T(1,128)S(1)} %get-tuple-element.33) | copy-start | bytes 6148
  19.0 149.7 %copy-start.13 = (bf16[3,256]{1,0:T(4,128)(2,1)S(1)}, bf16[3,256]{1,0:T(4,128)(2,1)}, u32[]{:S(2)}) copy-start(bf16[3,256]{1,0:T(4,128)(2,1)} %param.18) | copy-start | bytes 4612
  161.9 6.9 %copy-start = (bf16[512,1280]{1,0:T(8,128)(2,1)}, bf16[512,1280]{1,0:T(8,128)(2,1)S(1)}, u32[]{:S(2)}) copy-start(bf16[512,1280]{1,0:T(8,128)(2,1)S(1)} %fusion.7) | copy-start | bytes 3932164
  161.9 8.7 %copy-start.12 = (bf16[3,512]{1,0:T(4,128)(2,1)S(1)}, bf16[3,512]{1,0:T(4,128)(2,1)}, u32[]{:S(2)}) copy-start(bf16[3,512]{1,0:T(4,128)(2,1)} %param.17) | copy-start | bytes 9220
  161.9 6.8 %collective-permute-start.1 = (bf16[3,256]{1,0:T(4,128)(2,1)S(1)}, bf16[3,256]{1,0:T(4,128)(2,1)S(1)}, u32[]{:S(2)}, u32[]{:S(2)}) collective-permute-start(bf16[3,256]{1,0:T(4,128)(2,1)S(1)} %slice.240), channel_id=1, source_target_pairs={{0,8},{8,16},{16,24},{24,32},{32,40},{40,48},{48,56},{56,64},{64,7... | collective-permute-start | bytes 4616 | tf_op jit(solution)/shard_map/ppermute | solution.py:12
  165.2 5.3 %collective-permute-start = (bf16[3,512]{1,0:T(4,128)(2,1)S(1)}, bf16[3,512]{1,0:T(4,128)(2,1)S(1)}, u32[]{:S(2)}, u32[]{:S(2)}) collective-permute-start(bf16[3,512]{1,0:T(4,128)(2,1)S(1)} %slice.232), channel_id=1, source_target_pairs={{0,8},{8,16},{16,24},{24,32},{32,40},{40,48},{48,56},{56,64},{64,7... | collective-permute-start | bytes 9224 | tf_op jit(solution)/shard_map/ppermute | solution.py:12
  175.8 16.8 %collective-permute-start.5 = (f32[8,65,128]{2,1,0:T(8,128)S(1)}, f32[8,65,128]{2,1,0:T(8,128)S(1)}, u32[]{:S(2)}, u32[]{:S(2)}) collective-permute-start(f32[8,65,128]{2,1,0:T(8,128)S(1)} %pad_maximum_fusion.1), channel_id=1, source_target_pairs={{0,32},{8,40},{16,48},{24,56},{32,64},{40,72},{48,80},{56,88},{64,... | collective-permute-start | bytes 798728 | tf_op jit(solution)/shard_map/ppermute | solution.py:12
  180.3 23.1 %collective-permute-start.4 = (f32[8,65,128]{2,1,0:T(8,128)S(1)}, f32[8,65,128]{2,1,0:T(8,128)S(1)}, u32[]{:S(2)}, u32[]{:S(2)}) collective-permute-start(f32[8,65,128]{2,1,0:T(8,128)S(1)} %pad_maximum_fusion.1), channel_id=1, source_target_pairs={{0,24},{8,32},{16,40},{24,48},{32,56},{40,64},{48,72},{56,80},{64,... | collective-permute-start | bytes 798728 | tf_op jit(solution)/shard_map/ppermute | solution.py:12
  183.3 34.5 %collective-permute-start.3 = (f32[8,65,128]{2,1,0:T(8,128)S(1)}, f32[8,65,128]{2,1,0:T(8,128)}, u32[]{:S(2)}, u32[]{:S(2)}) collective-permute-start(f32[8,65,128]{2,1,0:T(8,128)S(1)} %pad_maximum_fusion.1), channel_id=1, source_target_pairs={{0,16},{8,24},{16,32},{24,40},{32,48},{40,56},{48,64},{56,72},{64,... | collective-permute-start | bytes 798728 | tf_op jit(solution)/shard_map/ppermute | solution.py:12
  186.7 42.6 %collective-permute-start.2 = (f32[8,65,128]{2,1,0:T(8,128)S(1)}, f32[8,65,128]{2,1,0:T(8,128)}, u32[]{:S(2)}, u32[]{:S(2)}) collective-permute-start(f32[8,65,128]{2,1,0:T(8,128)S(1)} %pad_maximum_fusion.1), channel_id=1, source_target_pairs={{0,8},{8,16},{16,24},{24,32},{32,40},{40,48},{48,56},{56,64},{64,7... | collective-permute-start | bytes 798728 | tf_op jit(solution)/shard_map/ppermute | solution.py:12
  231.7 34.6 %collective-permute-start.8 = (f32[8,65,128]{2,1,0:T(8,128)S(1)}, f32[8,65,128]{2,1,0:T(8,128)S(1)}, u32[]{:S(2)}, u32[]{:S(2)}) collective-permute-start(f32[8,65,128]{2,1,0:T(8,128)S(1)} %pad_maximum_fusion.2), channel_id=1, source_target_pairs={{0,96},{8,104},{16,112},{24,120},{32,128},{40,136},{48,144},{56,15... | collective-permute-start | bytes 798728 | tf_op jit(solution)/shard_map/ppermute | solution.py:12
  240.8 25.4 %collective-permute-start.7 = (f32[8,65,128]{2,1,0:T(8,128)S(1)}, f32[8,65,128]{2,1,0:T(8,128)S(1)}, u32[]{:S(2)}, u32[]{:S(2)}) collective-permute-start(f32[8,65,128]{2,1,0:T(8,128)S(1)} %pad_maximum_fusion.2), channel_id=1, source_target_pairs={{0,64},{8,72},{16,80},{24,88},{32,96},{40,104},{48,112},{56,120},{... | collective-permute-start | bytes 798728 | tf_op jit(solution)/shard_map/ppermute | solution.py:12
  244.2 21.9 %collective-permute-start.6 = (f32[8,65,128]{2,1,0:T(8,128)S(1)}, f32[8,65,128]{2,1,0:T(8,128)S(1)}, u32[]{:S(2)}, u32[]{:S(2)}) collective-permute-start(f32[8,65,128]{2,1,0:T(8,128)S(1)} %pad_maximum_fusion.2), channel_id=1, source_target_pairs={{0,32},{8,40},{16,48},{24,56},{32,64},{40,72},{48,80},{56,88},{64,... | collective-permute-start | bytes 798728 | tf_op jit(solution)/shard_map/ppermute | solution.py:12
  249.3 26.0 %copy-start.3 = (f32[256,8]{0,1:T(8,128)S(1)}, f32[256,8]{0,1:T(8,128)}, u32[]{:S(2)}) copy-start(f32[256,8]{0,1:T(8,128)} %fusion.55) | copy-start | bytes 24580
  249.3 30.6 %copy-start.1 = (f32[512,8]{0,1:T(8,128)S(1)}, f32[512,8]{0,1:T(8,128)}, u32[]{:S(2)}) copy-start(f32[512,8]{0,1:T(8,128)} %get-tuple-element.14) | copy-start | bytes 49156
  266.6 14.3 %copy-start.5 = (f32[1,512]{1,0:T(1,128)S(1)}, f32[1,512]{1,0:T(1,128)}, u32[]{:S(2)}) copy-start(f32[1,512]{1,0:T(1,128)} %copy-done.4) | copy-start | bytes 6148
  266.6 14.3 %copy-start.7 = (f32[1,512]{1,0:T(1,128)S(1)}, f32[1,512]{1,0:T(1,128)}, u32[]{:S(2)}) copy-start(f32[1,512]{1,0:T(1,128)} %copy-done.6) | copy-start | bytes 6148
  266.6 14.3 %copy-start.9 = (f32[1,512]{1,0:T(1,128)S(1)}, f32[1,512]{1,0:T(1,128)}, u32[]{:S(2)}) copy-start(f32[1,512]{1,0:T(1,128)} %copy-done.8) | copy-start | bytes 6148
  266.6 14.3 %copy-start.11 = (f32[1,512]{1,0:T(1,128)S(1)}, f32[1,512]{1,0:T(1,128)}, u32[]{:S(2)}) copy-start(f32[1,512]{1,0:T(1,128)} %copy-done.10) | copy-start | bytes 6148
  266.7 13.2 %collective-permute-start.9 = (f32[8,65,128]{2,1,0:T(8,128)S(1)}, f32[8,65,128]{2,1,0:T(8,128)S(1)}, u32[]{:S(2)}, u32[]{:S(2)}) collective-permute-start(f32[8,65,128]{2,1,0:T(8,128)S(1)} %pad_maximum_fusion.3), channel_id=1, source_target_pairs={{0,128},{8,136},{16,144},{24,152},{32,160},{40,168},{48,176},{56,1... | collective-permute-start | bytes 798728 | tf_op jit(solution)/shard_map/ppermute | solution.py:12
  280.6 2.5 copy-start.2
Sparse Core Ops, SparseCore 0:
  11.2 140.1 all-gather.1
  291.0 53.4 reduce-scatter.1

commit v4 on v2

--- a/solution.py
+++ b/solution.py
@@ -1,6 +1,10 @@
+import functools
+
 import jax
 import jax.numpy as jnp
 from jax import lax
+from jax.experimental import pallas as pl
+from jax.experimental.pallas import tpu as pltpu
 from jax.sharding import PartitionSpec as P
 
 Q = 256
@@ -21,26 +25,76 @@
     return jax.nn.silu(total).astype(jnp.bfloat16)
 
 
+def scan_kernel(count, shifts, msg_ref, sin_ref, out_ref, sbuf, rbuf, send_sem, recv_sem):
+    me = lax.axis_index("seq")
+    hd = lax.axis_index("head")
+    rows = sin_ref.shape[1]
+    barrier = pltpu.get_barrier_semaphore()
+    distinct = sorted(set(shifts))
+    for d in distinct:
+        for peer in ((me + d) % count, (me + count - d) % count):
+            pl.semaphore_signal(barrier, inc=1, device_id=(peer, hd), device_id_type=pl.DeviceIdType.MESH)
+    pl.semaphore_wait(barrier, 2 * len(distinct))
+    copies = []
+    for k, d in enumerate(shifts):
+        if k == 0:
+            sbuf[k] = msg_ref[...]
+        else:
+            sbuf[k] = out_ref[...]
+        copy = pltpu.make_async_remote_copy(
+            src_ref=sbuf.at[k],
+            dst_ref=rbuf.at[k],
+            send_sem=send_sem.at[k],
+            recv_sem=recv_sem.at[k],
+            device_id=((me + d) % count, hd),
+            device_id_type=pl.DeviceIdType.MESH,
+        )
+        copy.start()
+        copies.append(copy)
+        copy.wait_recv()
+        far = rbuf[k]
+        if k == 0:
+            opening = jnp.concatenate(
+                [sin_ref[...], jnp.zeros((far.shape[0], far.shape[1] - rows, far.shape[2]), far.dtype)], axis=1
+            )
+            out_ref[...] = jnp.where(me == 0, opening, far)
+        else:
+            acc = out_ref[...]
+            acc_a = acc[:, rows:, :]
+            acc_a_rows = jnp.tile(acc_a, (1, rows // acc_a.shape[1], 1))
+            new_s = acc_a_rows * far[:, :rows, :] + acc[:, :rows, :]
+            new_a = acc_a * far[:, rows:, :]
+            combined = jnp.concatenate([new_s, new_a], axis=1)
+            out_ref[...] = jnp.where(me >= d, combined, acc)
+    for copy in copies:
+        copy.wait_send()
+
+
 def entering_state(decay, end_state, state_in):
     count = lax.axis_size("seq")
-    me = lax.axis_index("seq")
-    first = me == 0
-    lanes = end_state.shape[2]
-
-    def pack(a, s):
-        return jnp.concatenate([s, jnp.broadcast_to(a[:, None, None], (a.shape[0], 1, lanes))], axis=1)
-
-    got = passed_along(pack(decay, end_state), "seq", 1)
-    acc_a = jnp.where(first, jnp.zeros_like(decay), got[:, -1, 0])
-    acc_s = jnp.where(first, state_in, got[:, :-1])
+    heads, rows, lanes = end_state.shape
+    pad = 8
+    message = jnp.concatenate([end_state, jnp.broadcast_to(decay[:, None, None], (heads, pad, lanes))], axis=1)
+    shifts = [1]
     step = 1
     while step < count:
-        far = passed_along(pack(acc_a, acc_s), "seq", step)
-        has = me >= step
-        acc_s = jnp.where(has, acc_a[:, None, None] * far[:, :-1] + acc_s, acc_s)
-        acc_a = jnp.where(has, acc_a * far[:, -1, 0], acc_a)
+        shifts.append(step)
         step *= 2
-    return acc_s
+    shape = message.shape
+    out = pl.pallas_call(
+        functools.partial(scan_kernel, count, tuple(shifts)),
+        out_shape=jax.ShapeDtypeStruct(shape, jnp.float32),
+        in_specs=[pl.BlockSpec(memory_space=pltpu.VMEM)] * 2,
+        out_specs=pl.BlockSpec(memory_space=pltpu.VMEM),
+        scratch_shapes=[
+            pltpu.VMEM((len(shifts),) + shape, jnp.float32),
+            pltpu.VMEM((len(shifts),) + shape, jnp.float32),
+            pltpu.SemaphoreType.DMA((len(shifts),)),
+            pltpu.SemaphoreType.DMA((len(shifts),)),
+        ],
+        compiler_params=pltpu.CompilerParams(collective_id=0, has_side_effects=True),
+    )(message, state_in)
+    return out[:, :rows, :]
 
 
 def local(
@@ -128,14 +182,14 @@
     parts = (parts + correction * jnp.exp(cum_range)[:, :, None]).reshape(rows, inner)
     y_val = parts / nstate + jnp.repeat(skip_gain, head_dim)[None, :] * x_conv.astype(jnp.float32)
     gated = y_val * jax.nn.silu(z_val.astype(jnp.float32))
+    scaled = (gated * norm_gain[None, :]).astype(jnp.bfloat16)
+    partial_out = lax.dot_general(
+        scaled, w_out_cols, (((1,), (1,)), ((), ())), preferred_element_type=jnp.float32
+    )
+    result = lax.psum_scatter(partial_out, "head", scatter_dimension=1, tiled=True)
     total_sq = lax.psum(jnp.sum(gated * gated, axis=1), "head")
     meansq = total_sq / (inner * lax.axis_size("head"))
-    normed = (gated * lax.rsqrt(meansq[:, None] + 1e-05) * norm_gain[None, :]).astype(jnp.bfloat16)
-    partial_out = lax.dot_general(
-        normed, w_out_cols, (((1,), (1,)), ((), ())), preferred_element_type=jnp.float32
-    )
-    result = lax.psum_scatter(partial_out, "head", scatter_dimension=1, tiled=True)
-    return result.astype(jnp.bfloat16)
+    return (result * lax.rsqrt(meansq[:, None] + 1e-05)).astype(jnp.bfloat16)
 
 
 def solution(mesh):

time: 341 us -> 321 us (0.941)
  Pallas kernels: 0 us -> 56.3 us
  starting transfers between devices: 42.4 us -> 6.25 us
  waiting for transfers between devices: 210 us -> 179 us
  other arithmetic: 20.5 us -> 12.7 us
    pallas_call x0 -> x1, Pallas kernels: none -> 56.3 us  [entering_state(): pl.pallas_call(functools.partial(scan_kernel, count, tuple(shifts)), out_...]
    ppermute x8 -> x2, starting transfers between devices: 42.4 us -> 6.2 us  [passed_along(): return lax.ppermute(value, axis, pairs)]
    ppermute x8 -> x2, waiting for transfers between devices: 24.6 us -> 0.01 us  [passed_along(): return lax.ppermute(value, axis, pairs)]
    select_n x12 -> x0, other arithmetic: 7.29 us -> none  [the longest x4 3.26 us: entering_state(): acc_s = jnp.where(has, acc_a[:, None, None] * far[:, :-1] + acc_s, acc_s)]
    reduce_scatter x1, waiting for transfers between devices: 52.1 us -> 45.7 us  [local(): lax.psum_scatter(partial_out, 'head', scatter_dimension=1, tiled=True)]
  transfers between devices with their start and end apart: 10 -> 4, of which waited for: 8 -> 2; matrix products, arithmetic and copies ran while one was open for 4% -> 3% of each run, Pallas kernels for 0% -> 0%
where the time goes in v4:
time: 321 us
  waiting for transfers between devices  179 us (56%)
  Pallas kernels  56.3 us (18%)
  matrix products  24.6 us (8%)
  blocking collectives  20.2 us (6%)
  between operations  13.7 us (4%)
  other arithmetic  12.7 us (4%)
  local copies, waits for them, and re-layouts  7.52 us (2%)
  starting transfers between devices  6.25 us (2%)
    all_gather x1, waiting for transfers between devices, local(): gathered = lax.all_gather(packed, 'seq', axis=0, tiled=True)  134 us
    pallas_call x1, Pallas kernels, entering_state(): pl.pallas_call(functools.partial(scan_kernel, count, tuple(shifts)), out_...  56.3 us
    reduce_scatter x1, waiting for transfers between devices, local(): lax.psum_scatter(partial_out, 'head', scatter_dimension=1, tiled=True)  45.7 us
    psum x1, blocking collectives, local(): total_sq = lax.psum(jnp.sum(gated * gated, axis=1), 'head')  20.2 us
    dot_general x1, matrix products, local(): jnp.dot(tokens, gathered[:, :proj], preferred_element_type=jnp.float32)  10.5 us
    dot_general x1, matrix products, local(): lax.dot_general(scaled, w_out_cols, (((1,), (1,)), ((), ())), preferred_e...  7.82 us
  transfers between devices with their start and end apart: 4, of which 2 were waited for; matrix products, arithmetic and copies ran while one was open for 3% of the time, Pallas kernels for 0%

profile of v4, /device:TPU:1, one launch (start us, length us, event | category | flops | bytes accessed | tf_op | source)
XLA Modules:
  0.0 320.6 jit_solution(10411955072870258872)
XLA Ops:
  6.5 0.9 copy.33
  7.5 1.5 fusion.45
  9.4 1.7 pad_maximum_fusion
  11.1 0.7 fusion.40
  11.9 1.1 reduce-window.16
  13.0 1.1 reduce-window.14
  14.8 0.5 slice_bitcast_fusion.7
  15.3 0.8 fusion.47
  16.2 0.9 fusion.46
  17.1 0.7 subtract_exponential_fusion
  17.8 133.6 %all-gather.2.cloned.1.call-done = bf16[4096,1792]{0,1:T(8,128)(2,1)} async-done(((bf16[128,1792]{0,1:T(8,128)(2,1)}), bf16[4096,1792]{0,1:T(8,128)(2,1)}) %all-gather.2.cloned.1.call-update) | async-done | bytes 14680080 | tf_op jit(solution)/shard_map/all_gather | solution.py:124
  151.4 10.5 %fusion.7 = bf16[512,1280]{1,0:T(8,128)(2,1)S(1)} fusion(bf16[512,4096]{1,0:T(8,128)(2,1)} %param.12, bf16[4096,1792]{0,1:T(8,128)(2,1)} %all-gather.2.cloned.1.call-done), kind=kOutput, calls=%fused_computation.6 | convolution fusion | flops 5369364480 | bytes 15990784 | tf_op jit(solution)/shard_map/dot_general | solution.py:126
  161.9 2.5 collective-permute-start.1
  164.9 3.7 %collective-permute-start = (bf16[3,512]{1,0:T(4,128)(2,1)S(1)}, bf16[3,512]{1,0:T(4,128)(2,1)S(1)}, u32[]{:S(2)}, u32[]{:S(2)}) collective-permute-start(bf16[3,512]{1,0:T(4,128)(2,1)S(1)} %slice.176), channel_id=1, source_target_pairs={{0,8},{8,16},{16,24},{24,32},{32,40},{40,48},{48,56},{56,64},{64,7... | collective-permute-start | bytes 9224 | tf_op jit(solution)/shard_map/ppermute | solution.py:16
  168.6 0.3 multiply_convert_fusion.10
  169.0 1.0 fusion.48
  170.0 0.7 convert_element_type.51
  170.9 0.6 multiply_convert_fusion.8
  171.6 0.5 reshape.94
  172.1 0.6 copy.35
  172.7 2.3 fusion.16
  175.1 1.0 fusion.24
  176.3 0.4 fusion.19
  176.7 0.7 pad_maximum_fusion.1.msg_ref
  177.5 56.3 %shard_map.118 = f32[8,72,128]{2,1,0:T(8,128)} custom-call(f32[8,72,128]{2,1,0:T(8,128)} %pad_maximum_fusion.1.msg_ref, f32[8,64,128]{2,1,0:T(8,128)} %sin_ref.1), custom_call_target="tpu_custom_call" | custom-call | tf_op jit(solution)/shard_map/pallas_call | solution.py:84
  233.8 1.6 fusion.18
  235.4 0.3 copy.37
  235.7 2.1 multiply_reduce_fusion
  237.8 7.8 %fusion.2 = f32[512,4096]{1,0:T(8,128)} fusion(bf16[4096,1792]{0,1:T(8,128)(2,1)} %all-gather.2.cloned.1.call-done, f32[512,512]{1,0:T(8,128)S(1)} %get-tuple-element.6, f32[512]{0:T(512)S(1)} %copy-done.2), kind=kOutput, calls=%fused_computation.2 | convolution fusion | flops 2148007936 | bytes 13633536 | tf_op jit(solution)/shard_map/dot_general | solution.py:186
  245.7 20.2 %psum.7 = f32[512]{0:T(512)S(1)} all-reduce(f32[512]{0:T(512)S(1)} %get-tuple-element.5), channel_id=1, replica_groups=mesh['seq'=32,'head'=8] {'head'}, use_global_device_ids=true, to_apply=%region_6.7 | all-reduce | flops 512 | bytes 4096 | tf_op jit(solution)/shard_map/psum | solution.py:190
  265.9 45.7 %reduce-scatter.2.cloned.1.call-done = f32[512,512]{1,0:T(8,128)} async-done(((f32[512,4096]{1,0:T(8,128)}), f32[512,512]{1,0:T(8,128)}) %reduce-scatter.2.cloned.1.call-update) | async-done | bytes 1048592 | tf_op jit(solution)/shard_map/reduce_scatter | solution.py:189
  311.6 2.2 multiply_convert_fusion.6
  (50 shorter events, 2.1 us)
Async XLA Ops:
  6.5 144.9 %all-gather.2.cloned.1.call-start = ((), (), s32[]{:S(2)}) async-start(), calls=%async_computation.1 | async-start | bytes 15138816 | tf_op jit(solution)/shard_map/all_gather | solution.py:124
  11.1 300.6 %reduce-scatter.2.cloned.1.call-start = ((), (), s32[]{:S(2)}) async-start(), calls=%async_computation.2 | async-start | bytes 9437184 | tf_op jit(solution)/shard_map/reduce_scatter | solution.py:189
  17.8 146.9 %copy-start.5 = (f32[8]{0:T(128)S(1)}, f32[8]{0:T(128)}, u32[]{:S(2)}) copy-start(f32[8]{0:T(128)} %param.20) | copy-start | bytes 100
  17.8 150.8 %copy-start.4 = (bf16[3,256]{1,0:T(4,128)(2,1)S(1)}, bf16[3,256]{1,0:T(4,128)(2,1)}, u32[]{:S(2)}) copy-start(bf16[3,256]{1,0:T(4,128)(2,1)} %param.18) | copy-start | bytes 4612
  161.9 6.8 %copy-start = (bf16[512,1280]{1,0:T(8,128)(2,1)}, bf16[512,1280]{1,0:T(8,128)(2,1)S(1)}, u32[]{:S(2)}) copy-start(bf16[512,1280]{1,0:T(8,128)(2,1)S(1)} %fusion.7) | copy-start | bytes 3932164
  161.9 8.9 %copy-start.3 = (bf16[3,512]{1,0:T(4,128)(2,1)S(1)}, bf16[3,512]{1,0:T(4,128)(2,1)}, u32[]{:S(2)}) copy-start(bf16[3,512]{1,0:T(4,128)(2,1)} %param.17) | copy-start | bytes 9220
  161.9 6.6 %collective-permute-start.1 = (bf16[3,256]{1,0:T(4,128)(2,1)S(1)}, bf16[3,256]{1,0:T(4,128)(2,1)S(1)}, u32[]{:S(2)}, u32[]{:S(2)}) collective-permute-start(bf16[3,256]{1,0:T(4,128)(2,1)S(1)} %slice.184), channel_id=1, source_target_pairs={{0,8},{8,16},{16,24},{24,32},{32,40},{40,48},{48,56},{56,64},{64,7... | collective-permute-start | bytes 4616 | tf_op jit(solution)/shard_map/ppermute | solution.py:16
  164.9 5.9 %collective-permute-start = (bf16[3,512]{1,0:T(4,128)(2,1)S(1)}, bf16[3,512]{1,0:T(4,128)(2,1)S(1)}, u32[]{:S(2)}, u32[]{:S(2)}) collective-permute-start(bf16[3,512]{1,0:T(4,128)(2,1)S(1)} %slice.176), channel_id=1, source_target_pairs={{0,8},{8,16},{16,24},{24,32},{32,40},{40,48},{48,56},{56,64},{64,7... | collective-permute-start | bytes 9224 | tf_op jit(solution)/shard_map/ppermute | solution.py:16
  172.7 2.4 copy-start.1
  172.7 3.4 %copy-start.6 = (f32[8]{0:T(128)S(1)}, f32[8]{0:T(128)}, u32[]{:S(2)}) copy-start(f32[8]{0:T(128)} %slice_bitcast_fusion.7) | copy-start | bytes 100
  235.4 2.5 copy-start.2
Sparse Core Ops, SparseCore 0:
  11.2 140.1 all-gather.1
  245.8 65.7 reduce-scatter.1

commit v5 on v4

--- a/solution.py
+++ b/solution.py
@@ -25,10 +25,9 @@
     return jax.nn.silu(total).astype(jnp.bfloat16)
 
 
-def scan_kernel(count, shifts, msg_ref, sin_ref, out_ref, sbuf, rbuf, send_sem, recv_sem):
+def scan_kernel(count, shifts, msg_ref, dec_ref, sin_ref, out_ref, dec_acc, s_send, a_send, s_recv, a_recv, send_sem, recv_sem):
     me = lax.axis_index("seq")
     hd = lax.axis_index("head")
-    rows = sin_ref.shape[1]
     barrier = pltpu.get_barrier_semaphore()
     distinct = sorted(set(shifts))
     for d in distinct:
@@ -38,34 +37,39 @@
     copies = []
     for k, d in enumerate(shifts):
         if k == 0:
-            sbuf[k] = msg_ref[...]
+            s_send[k] = msg_ref[...].astype(s_send.dtype)
+            a_send[k] = dec_ref[...]
         else:
-            sbuf[k] = out_ref[...]
-        copy = pltpu.make_async_remote_copy(
-            src_ref=sbuf.at[k],
-            dst_ref=rbuf.at[k],
-            send_sem=send_sem.at[k],
-            recv_sem=recv_sem.at[k],
-            device_id=((me + d) % count, hd),
-            device_id_type=pl.DeviceIdType.MESH,
-        )
-        copy.start()
-        copies.append(copy)
-        copy.wait_recv()
-        far = rbuf[k]
+            s_send[k] = out_ref[...].astype(s_send.dtype)
+            a_send[k] = dec_acc[...]
+        target = ((me + d) % count, hd)
+        pair = []
+        for index, (src, dst) in enumerate(((s_send, s_recv), (a_send, a_recv))):
+            copy = pltpu.make_async_remote_copy(
+                src_ref=src.at[k],
+                dst_ref=dst.at[k],
+                send_sem=send_sem.at[index, k],
+                recv_sem=recv_sem.at[index, k],
+                device_id=target,
+                device_id_type=pl.DeviceIdType.MESH,
+            )
+            copy.start()
+            pair.append(copy)
+        copies.extend(pair)
+        for copy in pair:
+            copy.wait_recv()
+        far_s = s_recv[k].astype(jnp.float32)
+        far_a = a_recv[k]
         if k == 0:
-            opening = jnp.concatenate(
-                [sin_ref[...], jnp.zeros((far.shape[0], far.shape[1] - rows, far.shape[2]), far.dtype)], axis=1
-            )
-            out_ref[...] = jnp.where(me == 0, opening, far)
+            out_ref[...] = jnp.where(me == 0, sin_ref[...], far_s)
+            dec_acc[...] = jnp.where(me == 0, jnp.zeros_like(far_a), far_a)
         else:
-            acc = out_ref[...]
-            acc_a = acc[:, rows:, :]
+            acc_s = out_ref[...]
+            acc_a = dec_acc[...]
+            rows = acc_s.shape[1]
             acc_a_rows = jnp.tile(acc_a, (1, rows // acc_a.shape[1], 1))
-            new_s = acc_a_rows * far[:, :rows, :] + acc[:, :rows, :]
-            new_a = acc_a * far[:, rows:, :]
-            combined = jnp.concatenate([new_s, new_a], axis=1)
-            out_ref[...] = jnp.where(me >= d, combined, acc)
+            out_ref[...] = jnp.where(me >= d, acc_a_rows * far_s + acc_s, acc_s)
+            dec_acc[...] = jnp.where(me >= d, acc_a * far_a, acc_a)
     for copy in copies:
         copy.wait_send()
 
@@ -73,28 +77,29 @@
 def entering_state(decay, end_state, state_in):
     count = lax.axis_size("seq")
     heads, rows, lanes = end_state.shape
-    pad = 8
-    message = jnp.concatenate([end_state, jnp.broadcast_to(decay[:, None, None], (heads, pad, lanes))], axis=1)
+    decay_rows = jnp.broadcast_to(decay[:, None, None], (heads, 8, lanes))
     shifts = [1]
     step = 1
     while step < count:
         shifts.append(step)
         step *= 2
-    shape = message.shape
-    out = pl.pallas_call(
+    steps = len(shifts)
+    return pl.pallas_call(
         functools.partial(scan_kernel, count, tuple(shifts)),
-        out_shape=jax.ShapeDtypeStruct(shape, jnp.float32),
-        in_specs=[pl.BlockSpec(memory_space=pltpu.VMEM)] * 2,
+        out_shape=jax.ShapeDtypeStruct(end_state.shape, jnp.float32),
+        in_specs=[pl.BlockSpec(memory_space=pltpu.VMEM)] * 3,
         out_specs=pl.BlockSpec(memory_space=pltpu.VMEM),
         scratch_shapes=[
-            pltpu.VMEM((len(shifts),) + shape, jnp.float32),
-            pltpu.VMEM((len(shifts),) + shape, jnp.float32),
-            pltpu.SemaphoreType.DMA((len(shifts),)),
-            pltpu.SemaphoreType.DMA((len(shifts),)),
+            pltpu.VMEM(decay_rows.shape, jnp.float32),
+            pltpu.VMEM((steps,) + end_state.shape, jnp.bfloat16),
+            pltpu.VMEM((steps,) + decay_rows.shape, jnp.float32),
+            pltpu.VMEM((steps,) + end_state.shape, jnp.bfloat16),
+            pltpu.VMEM((steps,) + decay_rows.shape, jnp.float32),
+            pltpu.SemaphoreType.DMA((2, steps)),
+            pltpu.SemaphoreType.DMA((2, steps)),
         ],
         compiler_params=pltpu.CompilerParams(collective_id=0, has_side_effects=True),
-    )(message, state_in)
-    return out[:, :rows, :]
+    )(end_state, decay_rows, state_in)
 
 
 def local(
@@ -118,13 +123,10 @@
     first = lax.axis_index("seq") == 0
     w_x = w_xz[:, 0, :]
     w_z = w_xz[:, 1, :]
-    w_out_t = jnp.transpose(w_out)
-    widths = (w_x.shape[1], w_z.shape[1], w_bc.shape[1], w_out_t.shape[1])
-    packed = jnp.concatenate([w_x, w_z, w_bc, w_out_t], axis=1)
+    packed = jnp.concatenate([w_x, w_z, w_bc], axis=1)
     gathered = lax.all_gather(packed, "seq", axis=0, tiled=True)
-    proj = widths[0] + widths[1] + widths[2]
-    xzbc = jnp.dot(tokens, gathered[:, :proj], preferred_element_type=jnp.float32)
-    w_out_cols = gathered[:, proj:]
+    w_out_cols = lax.all_gather(jnp.transpose(w_out), "seq", axis=0, tiled=True)
+    xzbc = jnp.dot(tokens, gathered, preferred_element_type=jnp.float32)
     xz = xzbc[:, : 2 * inner]
     bc_sum = xzbc[:, 2 * inner :]
     x_pre = xz[:, :inner].astype(jnp.bfloat16)

time: 321 us -> 285 us (0.89)
  waiting for transfers between devices: 179 us -> 160 us
  Pallas kernels: 56.3 us -> 45.7 us
  blocking collectives: 20.2 us -> 15.4 us
    all_gather x1, waiting for transfers between devices: 134 us -> 105 us  [local(): gathered = lax.all_gather(packed, 'seq', axis=0, tiled=True)]
    all_gather x0 -> x1, waiting for transfers between devices: none -> 13.9 us  [local(): w_out_cols = lax.all_gather(jnp.transpose(w_out), 'seq', axis=0, tiled=True)]
    pallas_call x1, Pallas kernels: 56.3 us -> 45.7 us  [entering_state(): pl.pallas_call(functools.partial(scan_kernel, count, tuple(shifts)), out_...]
    reduce_scatter x1, waiting for transfers between devices: 45.7 us -> 40.1 us  [local(): lax.psum_scatter(partial_out, 'head', scatter_dimension=1, tiled=True)]
    psum x1, blocking collectives: 20.2 us -> 15.4 us  [local(): total_sq = lax.psum(jnp.sum(gated * gated, axis=1), 'head')]
  transfers between devices with their start and end apart: 4 -> 5, of which waited for: 2 -> 3; matrix products, arithmetic and copies ran while one was open for 3% -> 11% of each run, Pallas kernels for 0% -> 16%
where the time goes in v5:
time: 285 us; the launch traced here: 284 us
  waiting for transfers between devices  160 us (56%)
  Pallas kernels  45.7 us (16%)
  matrix products  24.4 us (9%)
  blocking collectives  15.4 us (5%)
  between operations  13.4 us (5%)
  other arithmetic  13.2 us (5%)
  local copies, waits for them, and re-layouts  6.98 us (2%)
  starting transfers between devices  4.95 us (2%)
    all_gather x1, waiting for transfers between devices, local(): gathered = lax.all_gather(packed, 'seq', axis=0, tiled=True)  105 us
    pallas_call x1, Pallas kernels, entering_state(): pl.pallas_call(functools.partial(scan_kernel, count, tuple(shifts)), out_...  45.7 us
    reduce_scatter x1, waiting for transfers between devices, local(): lax.psum_scatter(partial_out, 'head', scatter_dimension=1, tiled=True)  40.1 us
    psum x1, blocking collectives, local(): total_sq = lax.psum(jnp.sum(gated * gated, axis=1), 'head')  15.4 us
    all_gather x1, waiting for transfers between devices, local(): w_out_cols = lax.all_gather(jnp.transpose(w_out), 'seq', axis=0, tiled=True)  13.9 us
    dot_general x1, matrix products, local(): xzbc = jnp.dot(tokens, gathered, preferred_element_type=jnp.float32)  10.4 us
    dot_general x1, matrix products, local(): lax.dot_general(scaled, w_out_cols, (((1,), (1,)), ((), ())), preferred_e...  7.76 us
  transfers between devices with their start and end apart: 5, of which 3 were waited for; matrix products, arithmetic and copies ran while one was open for 11% of the time, Pallas kernels for 16%

profile of v5, /device:TPU:1, one launch (start us, length us, event | category | flops | bytes accessed | tf_op | source)
XLA Modules:
  0.0 284.0 jit_solution(12928123840676625899)
XLA Ops:
  6.5 1.5 fusion.36
  8.1 1.6 pad_maximum_fusion
  9.8 0.7 all-gather.5.cloned.1.call-update
  10.5 0.7 fusion.31
  11.3 1.1 reduce-window.14
  12.8 1.1 reduce-window.16
  14.2 0.6 slice_bitcast_fusion.7
  14.8 0.8 fusion.38
  15.6 0.9 fusion.37
  16.6 0.7 subtract_exponential_fusion
  17.3 105.1 %all-gather.3.cloned.1.call-done = bf16[4096,1280]{1,0:T(8,128)(2,1)} async-done(((bf16[128,1280]{1,0:T(8,128)(2,1)}), bf16[4096,1280]{1,0:T(8,128)(2,1)}) %all-gather.3.cloned.1.call-update) | async-done | bytes 10485776 | tf_op jit(solution)/shard_map/all_gather | solution.py:127
  122.4 10.4 %fusion = bf16[512,1280]{1,0:T(8,128)(2,1)S(1)} fusion(bf16[512,4096]{1,0:T(8,128)(2,1)} %param.12, bf16[4096,1280]{1,0:T(8,128)(2,1)} %all-gather.3.cloned.1.call-done), kind=kOutput, calls=%fused_computation.2 | convolution fusion | flops 5369364480 | bytes 15990784 | tf_op jit(solution)/shard_map/dot_general | solution.py:129
  132.8 1.5 collective-permute-start.1
  134.8 3.3 %collective-permute-start = (bf16[3,512]{1,0:T(4,128)(2,1)S(1)}, bf16[3,512]{1,0:T(4,128)(2,1)S(1)}, u32[]{:S(2)}, u32[]{:S(2)}) collective-permute-start(bf16[3,512]{1,0:T(4,128)(2,1)S(1)} %slice.163), channel_id=1, source_target_pairs={{0,8},{8,16},{16,24},{24,32},{32,40},{40,48},{48,56},{56,64},{64,7... | collective-permute-start | bytes 9224 | tf_op jit(solution)/shard_map/ppermute | solution.py:16
  138.6 1.0 fusion.39
  139.6 0.7 convert_element_type.51
  140.5 0.6 multiply_convert_fusion.8
  141.2 0.5 reshape.94
  141.7 0.6 copy.31
  142.3 1.9 fusion.15
  144.3 1.5 fusion.26.msg_ref
  145.8 0.7 broadcast_in_dim.18.dec_ref
  146.4 45.7 %shard_map.118 = f32[8,64,128]{2,1,0:T(8,128)} custom-call(f32[8,64,128]{2,1,0:T(8,128)} %fusion.26.msg_ref, f32[8,8,128]{2,1,0:T(8,128)} %broadcast_in_dim.18.dec_ref, f32[8,64,128]{2,1,0:T(8,128)} %sin_ref.1), custom_call_target="tpu_custom_call" | custom-call | tf_op jit(solution)/shard_map/pallas_call | solution.py:87
  192.2 2.3 fusion.7
  194.5 0.4 fusion.10
  195.0 0.6 fusion.9
  195.9 2.1 multiply_reduce_fusion
  198.1 13.9 %all-gather.5.cloned.1.call-done = bf16[4096,512]{0,1:T(8,128)(2,1)} async-done(((bf16[128,512]{0,1:T(8,128)(2,1)}), bf16[4096,512]{0,1:T(8,128)(2,1)}) %all-gather.5.cloned.1.call-update) | async-done | bytes 4194320 | tf_op jit(solution)/shard_map/all_gather | solution.py:128
  212.0 7.8 %fusion.21 = f32[512,4096]{1,0:T(8,128)} fusion(bf16[4096,512]{0,1:T(8,128)(2,1)} %all-gather.5.cloned.1.call-done, f32[512,512]{1,0:T(8,128)S(1)} %get-tuple-element.6, f32[512]{0:T(512)S(1)} %copy-done.2), kind=kOutput, calls=%fused_computation.37 | convolution fusion | flops 2148007936 | bytes 13633536 | tf_op jit(solution)/shard_map/dot_general | solution.py:188
  219.8 15.4 %psum.7 = f32[512]{0:T(512)S(1)} all-reduce(f32[512]{0:T(512)S(1)} %get-tuple-element.5), channel_id=1, replica_groups=mesh['seq'=32,'head'=8] {'head'}, use_global_device_ids=true, to_apply=%region_6.7 | all-reduce | flops 512 | bytes 4096 | tf_op jit(solution)/shard_map/psum | solution.py:192
  235.2 40.1 %reduce-scatter.2.cloned.1.call-done = f32[512,512]{1,0:T(8,128)} async-done(((f32[512,4096]{1,0:T(8,128)}), f32[512,512]{1,0:T(8,128)}) %reduce-scatter.2.cloned.1.call-update) | async-done | bytes 1048592 | tf_op jit(solution)/shard_map/reduce_scatter | solution.py:191
  275.3 2.2 multiply_convert_fusion.6
  (48 shorter events, 2.3 us)
Async XLA Ops:
  6.5 115.9 %all-gather.3.cloned.1.call-start = ((), (), s32[]{:S(2)}) async-start(), calls=%async_computation.1 | async-start | bytes 10813440 | tf_op jit(solution)/shard_map/all_gather | solution.py:127
  9.7 202.2 %all-gather.5.cloned.1.call-start = ((), (), s32[]{:S(2)}) async-start(), calls=%async_computation.2 | async-start | bytes 4325376 | tf_op jit(solution)/shard_map/all_gather | solution.py:128
  10.5 264.9 %reduce-scatter.2.cloned.1.call-start = ((), (), s32[]{:S(2)}) async-start(), calls=%async_computation.3 | async-start | bytes 9437184 | tf_op jit(solution)/shard_map/reduce_scatter | solution.py:191
  17.3 117.3 %copy-start.5 = (f32[8]{0:T(128)S(1)}, f32[8]{0:T(128)}, u32[]{:S(2)}) copy-start(f32[8]{0:T(128)} %param.20) | copy-start | bytes 100
  17.3 120.9 %copy-start.4 = (bf16[3,256]{1,0:T(4,128)(2,1)S(1)}, bf16[3,256]{1,0:T(4,128)(2,1)}, u32[]{:S(2)}) copy-start(bf16[3,256]{1,0:T(4,128)(2,1)} %param.18) | copy-start | bytes 4612
  132.8 5.4 %copy-start = (bf16[512,1280]{1,0:T(8,128)(2,1)}, bf16[512,1280]{1,0:T(8,128)(2,1)S(1)}, u32[]{:S(2)}) copy-start(bf16[512,1280]{1,0:T(8,128)(2,1)S(1)} %fusion) | copy-start | bytes 3932164
  132.8 7.6 %copy-start.3 = (bf16[3,512]{1,0:T(4,128)(2,1)S(1)}, bf16[3,512]{1,0:T(4,128)(2,1)}, u32[]{:S(2)}) copy-start(bf16[3,512]{1,0:T(4,128)(2,1)} %param.17) | copy-start | bytes 9220
  132.8 5.3 %collective-permute-start.1 = (bf16[3,256]{1,0:T(4,128)(2,1)S(1)}, bf16[3,256]{1,0:T(4,128)(2,1)S(1)}, u32[]{:S(2)}, u32[]{:S(2)}) collective-permute-start(bf16[3,256]{1,0:T(4,128)(2,1)S(1)} %slice.171), channel_id=1, source_target_pairs={{0,8},{8,16},{16,24},{24,32},{32,40},{40,48},{48,56},{56,64},{64,7... | collective-permute-start | bytes 4616 | tf_op jit(solution)/shard_map/ppermute | solution.py:16
  134.8 5.6 %collective-permute-start = (bf16[3,512]{1,0:T(4,128)(2,1)S(1)}, bf16[3,512]{1,0:T(4,128)(2,1)S(1)}, u32[]{:S(2)}, u32[]{:S(2)}) collective-permute-start(bf16[3,512]{1,0:T(4,128)(2,1)S(1)} %slice.163), channel_id=1, source_target_pairs={{0,8},{8,16},{16,24},{24,32},{32,40},{40,48},{48,56},{56,64},{64,7... | collective-permute-start | bytes 9224 | tf_op jit(solution)/shard_map/ppermute | solution.py:16
  192.2 2.8 copy-start.1
  195.6 16.4 %copy-start.2 = (f32[512]{0:T(512)S(1)}, f32[512]{0:T(512)}, u32[]{:S(2)}) copy-start(f32[512]{0:T(512)} %param.22) | copy-start | bytes 6148
Sparse Core Ops, SparseCore 0:
  9.9 112.4 all-gather.2
  124.9 87.0 all-gather.4
  219.9 55.4 reduce-scatter.1

commit v6 on v5

--- a/solution.py
+++ b/solution.py
@@ -16,10 +16,10 @@
     return lax.ppermute(value, axis, pairs)
 
 
-def depthwise(pre, tail, kernel):
-    whole = jnp.concatenate([tail, pre], axis=0).astype(jnp.float32)
-    length = pre.shape[0]
-    total = jnp.zeros((length, pre.shape[1]), jnp.float32)
+def depthwise(whole, kernel):
+    whole = whole.astype(jnp.float32)
+    length = whole.shape[0] - kernel.shape[0] + 1
+    total = jnp.zeros((length, whole.shape[1]), jnp.float32)
     for offset in range(kernel.shape[0]):
         total = total + kernel[offset] * whole[offset : offset + length]
     return jax.nn.silu(total).astype(jnp.bfloat16)
@@ -126,18 +126,16 @@
     packed = jnp.concatenate([w_x, w_z, w_bc], axis=1)
     gathered = lax.all_gather(packed, "seq", axis=0, tiled=True)
     w_out_cols = lax.all_gather(jnp.transpose(w_out), "seq", axis=0, tiled=True)
-    xzbc = jnp.dot(tokens, gathered, preferred_element_type=jnp.float32)
-    xz = xzbc[:, : 2 * inner]
-    bc_sum = xzbc[:, 2 * inner :]
-    x_pre = xz[:, :inner].astype(jnp.bfloat16)
-    z_val = xz[:, inner:].astype(jnp.bfloat16)
-    bc_pre = bc_sum.astype(jnp.bfloat16)
     lag = conv_x.shape[0] - 1
-    before_x, before_bc = passed_along((x_pre[rows - lag :], bc_pre[rows - lag :]), "seq", 1)
-    before_x = jnp.where(first, tail_x, before_x)
-    before_bc = jnp.where(first, tail_bc, before_bc)
-    x_conv = depthwise(x_pre, before_x, conv_x)
-    bc_conv = depthwise(bc_pre, before_bc, conv_bc)
+    earlier = passed_along(tokens[rows - lag :], "seq", 1)
+    extended = jnp.concatenate([earlier, tokens], axis=0)
+    xzbc = jnp.dot(extended, gathered, preferred_element_type=jnp.float32).astype(jnp.bfloat16)
+    opening = lax.broadcasted_iota(jnp.int32, (rows + lag, 1), 0) < lag
+    whole_x = jnp.where(first & opening, jnp.pad(tail_x, ((0, rows), (0, 0))), xzbc[:, :inner])
+    whole_bc = jnp.where(first & opening, jnp.pad(tail_bc, ((0, rows), (0, 0))), xzbc[:, 2 * inner :])
+    z_val = xzbc[lag:, inner : 2 * inner]
+    x_conv = depthwise(whole_x, conv_x)
+    bc_conv = depthwise(whole_bc, conv_bc)
     b_val = bc_conv[:, :nstate]
     c_val = bc_conv[:, nstate:]
     logdec = -decay_code.astype(jnp.float32) / (16.0 * rows * seq_count)
@@ -188,7 +186,9 @@
     partial_out = lax.dot_general(
         scaled, w_out_cols, (((1,), (1,)), ((), ())), preferred_element_type=jnp.float32
     )
-    result = lax.psum_scatter(partial_out, "head", scatter_dimension=1, tiled=True)
+    result = lax.psum_scatter(
+        partial_out.astype(jnp.bfloat16), "head", scatter_dimension=1, tiled=True
+    ).astype(jnp.float32)
     total_sq = lax.psum(jnp.sum(gated * gated, axis=1), "head")
     meansq = total_sq / (inner * lax.axis_size("head"))
     return (result * lax.rsqrt(meansq[:, None] + 1e-05)).astype(jnp.bfloat16)

time: 285 us -> 273 us (0.958)
  waiting for transfers between devices: 160 us -> 153 us
  Pallas kernels: 45.7 us -> 41.8 us
  matrix products: 24.4 us -> 20.6 us
    reduce_scatter x1, waiting for transfers between devices: 40.1 us -> 22.7 us  [local(): lax.psum_scatter(partial_out.astype(jnp.bfloat16), 'head', scatter_dimens...]
    all_gather x1, waiting for transfers between devices: 13.9 us -> 29.1 us  [local(): w_out_cols = lax.all_gather(jnp.transpose(w_out), 'seq', axis=0, tiled=True)]
    all_gather x1, waiting for transfers between devices: 105 us -> 100 us  [local(): gathered = lax.all_gather(packed, 'seq', axis=0, tiled=True)]
    pallas_call x1, Pallas kernels: 45.7 us -> 41.8 us  [entering_state(): pl.pallas_call(functools.partial(scan_kernel, count, tuple(shifts)), out_...]
  transfers between devices with their start and end apart: 5 -> 4, of which waited for: 3 -> 3; matrix products, arithmetic and copies ran while one was open for 11% -> 11% of each run, Pallas kernels for 16% -> 15%
where the time goes in v6:
time: 273 us; the launch traced here: 271 us
  waiting for transfers between devices  153 us (56%)
  Pallas kernels  41.8 us (15%)
  matrix products  20.6 us (8%)
  blocking collectives  17.2 us (6%)
  between operations  13.4 us (5%)
  other arithmetic  12.2 us (4%)
  local copies, waits for them, and re-layouts  8.73 us (3%)
  starting transfers between devices  4.45 us (2%)
    all_gather x1, waiting for transfers between devices, local(): gathered = lax.all_gather(packed, 'seq', axis=0, tiled=True)  100 us
    pallas_call x1, Pallas kernels, entering_state(): pl.pallas_call(functools.partial(scan_kernel, count, tuple(shifts)), out_...  41.8 us
    all_gather x1, waiting for transfers between devices, local(): w_out_cols = lax.all_gather(jnp.transpose(w_out), 'seq', axis=0, tiled=True)  29.1 us
    reduce_scatter x1, waiting for transfers between devices, local(): lax.psum_scatter(partial_out.astype(jnp.bfloat16), 'head', scatter_dimens...  22.7 us
    psum x1, blocking collectives, local(): total_sq = lax.psum(jnp.sum(gated * gated, axis=1), 'head')  17.2 us
    dot_general x1, matrix products, local(): jnp.dot(extended, gathered, preferred_element_type=jnp.float32)  10.6 us
    dot_general x1, matrix products, local(): lax.dot_general(scaled, w_out_cols, (((1,), (1,)), ((), ())), preferred_e...  6.46 us
  transfers between devices with their start and end apart: 4, of which 3 were waited for; matrix products, arithmetic and copies ran while one was open for 11% of the time, Pallas kernels for 15%

profile of v6, /device:TPU:1, one launch (start us, length us, event | category | flops | bytes accessed | tf_op | source)
XLA Modules:
  0.0 270.9 jit_solution(8330279188414351177)
XLA Ops:
  6.5 1.5 fusion.45
  8.1 1.6 pad_maximum_fusion
  9.8 0.7 all-gather.5.cloned.1.call-update
  10.5 0.9 slice.115
  11.4 4.4 %collective-permute-start = (bf16[3,4096]{1,0:T(4,128)(2,1)S(1)}, bf16[3,4096]{1,0:T(4,128)(2,1)S(1)}, u32[]{:S(2)}, u32[]{:S(2)}) collective-permute-start(bf16[3,4096]{1,0:T(4,128)(2,1)S(1)} %slice.115), channel_id=1, source_target_pairs={{0,8},{8,16},{16,24},{24,32},{32,40},{40,48},{48,56},{56,64},{64,7... | collective-permute-start | bytes 73736 | tf_op jit(solution)/shard_map/ppermute | solution.py:16
  15.8 0.7 fusion.40
  16.5 1.1 reduce-window.14
  18.1 1.1 reduce-window.16
  19.7 0.8 fusion.47
  20.6 0.9 fusion.46
  21.5 0.7 broadcast_in_dim.53
  22.4 100.0 %all-gather.3.cloned.1.call-done = bf16[4096,1280]{1,0:T(8,128)(2,1)} async-done(((bf16[128,1280]{1,0:T(8,128)(2,1)}), bf16[4096,1280]{1,0:T(8,128)(2,1)}) %all-gather.3.cloned.1.call-update) | async-done | bytes 10485776 | tf_op jit(solution)/shard_map/all_gather | solution.py:127
  122.4 10.6 %fusion.4 = bf16[515,1280]{1,0:T(8,128)(2,1)S(1)} fusion(bf16[4096,1280]{1,0:T(8,128)(2,1)} %all-gather.3.cloned.1.call-done, bf16[512,4096]{1,0:T(8,128)(2,1)} %param.12, bf16[3,4096]{1,0:T(4,128)(2,1)S(1)} %collective-permute-done), kind=kOutput, calls=%fused_computation.6 | convolution fusion | flops 5409263616 | bytes 16023040 | tf_op jit(solution)/shard_map/dot_general | solution.py:132
  133.2 0.9 copy-done
  134.1 0.6 multiply_convert_fusion.8
  134.8 0.5 reshape.101
  135.3 0.6 copy.31
  135.9 1.1 fusion.32
  137.4 1.0 fusion.21
  138.4 0.8 fusion.33.msg_ref
  139.2 0.7 broadcast_in_dim.52.dec_ref
  139.9 41.8 %shard_map.118 = f32[8,64,128]{2,1,0:T(8,128)} custom-call(f32[8,64,128]{2,1,0:T(8,128)} %fusion.33.msg_ref, f32[8,8,128]{2,1,0:T(8,128)} %broadcast_in_dim.52.dec_ref, f32[8,64,128]{2,1,0:T(8,128)} %sin_ref.1), custom_call_target="tpu_custom_call" | custom-call | tf_op jit(solution)/shard_map/pallas_call | solution.py:87
  182.0 1.2 fusion.13
  183.2 0.4 fusion.16
  183.7 0.6 fusion.15
  184.3 0.3 copy.33
  184.6 2.2 multiply_reduce_fusion
  186.9 29.1 %all-gather.5.cloned.1.call-done = bf16[4096,512]{0,1:T(8,128)(2,1)} async-done(((bf16[128,512]{0,1:T(8,128)(2,1)}), bf16[4096,512]{0,1:T(8,128)(2,1)}) %all-gather.5.cloned.1.call-update) | async-done | bytes 4194320 | tf_op jit(solution)/shard_map/all_gather | solution.py:128
  216.0 6.5 %convolution_convert_fusion = bf16[512,4096]{1,0:T(8,128)(2,1)} fusion(bf16[4096,512]{0,1:T(8,128)(2,1)} %all-gather.5.cloned.1.call-done, f32[512,512]{1,0:T(8,128)S(1)} %get-tuple-element.6, f32[512]{0:T(512)S(1)} %copy-done.4), kind=kOutput, calls=%fused_computation | convolution fusion | flops 2150105088 | bytes 9439232 | tf_op jit(solution)/shard_map/dot_general | solution.py:186
  222.5 17.2 %psum.7 = f32[512]{0:T(512)S(1)} all-reduce(f32[512]{0:T(512)S(1)} %get-tuple-element.5), channel_id=1, replica_groups=mesh['seq'=32,'head'=8] {'head'}, use_global_device_ids=true, to_apply=%region_6.7 | all-reduce | flops 512 | bytes 4096 | tf_op jit(solution)/shard_map/psum | solution.py:192
  239.7 22.7 %reduce-scatter.2.cloned.1.call-done = bf16[512,512]{1,0:T(8,128)(2,1)} async-done(((bf16[512,4096]{1,0:T(8,128)(2,1)}), bf16[512,512]{1,0:T(8,128)(2,1)}) %reduce-scatter.2.cloned.1.call-update) | async-done | bytes 524304 | tf_op jit(solution)/shard_map/reduce_scatter | solution.py:189
  262.4 2.0 multiply_convert_fusion.6
  (40 shorter events, 2.1 us)
Async XLA Ops:
  6.5 115.9 %all-gather.3.cloned.1.call-start = ((), (), s32[]{:S(2)}) async-start(), calls=%async_computation.1 | async-start | bytes 10813440 | tf_op jit(solution)/shard_map/all_gather | solution.py:127
  9.7 206.2 %all-gather.5.cloned.1.call-start = ((), (), s32[]{:S(2)}) async-start(), calls=%async_computation.2 | async-start | bytes 4325376 | tf_op jit(solution)/shard_map/all_gather | solution.py:128
  10.5 251.9 %reduce-scatter.2.cloned.1.call-start = ((), (), s32[]{:S(2)}) async-start(), calls=%async_computation.3 | async-start | bytes 4718592 | tf_op jit(solution)/shard_map/reduce_scatter | solution.py:189
  11.4 11.0 %collective-permute-start = (bf16[3,4096]{1,0:T(4,128)(2,1)S(1)}, bf16[3,4096]{1,0:T(4,128)(2,1)S(1)}, u32[]{:S(2)}, u32[]{:S(2)}) collective-permute-start(bf16[3,4096]{1,0:T(4,128)(2,1)S(1)} %slice.115), channel_id=1, source_target_pairs={{0,8},{8,16},{16,24},{24,32},{32,40},{40,48},{48,56},{56,64},{64,7... | collective-permute-start | bytes 73736 | tf_op jit(solution)/shard_map/ppermute | solution.py:16
  22.3 110.7 %copy-start.2 = (bf16[3,512]{1,0:T(4,128)(2,1)S(1)}, bf16[3,512]{1,0:T(4,128)(2,1)}, u32[]{:S(2)}) copy-start(bf16[3,512]{1,0:T(4,128)(2,1)} %param.17) | copy-start | bytes 9220
  133.1 1.1 copy-start
  133.2 2.7 copy-start.3
  181.9 1.7 copy-start.1
  184.3 31.7 %copy-start.4 = (f32[512]{0:T(512)S(1)}, f32[512]{0:T(512)}, u32[]{:S(2)}) copy-start(f32[512]{0:T(512)} %param.22) | copy-start | bytes 6148
Sparse Core Ops, SparseCore 0:
  9.9 112.4 all-gather.2
  124.9 91.0 all-gather.4
  222.6 39.7 reduce-scatter.1

commit v7 on v6

--- a/solution.py
+++ b/solution.py
@@ -5,13 +5,20 @@
 from jax import lax
 from jax.experimental import pallas as pl
 from jax.experimental.pallas import tpu as pltpu
-from jax.sharding import PartitionSpec as P
+from jax.sharding import Mesh, PartitionSpec as P
 
 Q = 256
 
 
+SEQ = ("sx", "sz")
+
+
+def seq_size():
+    return lax.axis_size("sx") * lax.axis_size("sz")
+
+
 def passed_along(value, axis, by):
-    size = lax.axis_size(axis)
+    size = seq_size() if axis == SEQ else lax.axis_size(axis)
     pairs = [(i, i + by) for i in range(size) if 0 <= i + by < size]
     return lax.ppermute(value, axis, pairs)
 
@@ -25,14 +32,16 @@
     return jax.nn.silu(total).astype(jnp.bfloat16)
 
 
-def scan_kernel(count, shifts, msg_ref, dec_ref, sin_ref, out_ref, dec_acc, s_send, a_send, s_recv, a_recv, send_sem, recv_sem):
-    me = lax.axis_index("seq")
+def scan_kernel(count, minor, shifts, msg_ref, dec_ref, sin_ref, out_ref, dec_acc, s_send, a_send, s_recv, a_recv, send_sem, recv_sem):
+    me = lax.axis_index("sx") * minor + lax.axis_index("sz")
     hd = lax.axis_index("head")
     barrier = pltpu.get_barrier_semaphore()
     distinct = sorted(set(shifts))
     for d in distinct:
         for peer in ((me + d) % count, (me + count - d) % count):
-            pl.semaphore_signal(barrier, inc=1, device_id=(peer, hd), device_id_type=pl.DeviceIdType.MESH)
+            pl.semaphore_signal(
+                barrier, inc=1, device_id=(peer // minor, peer % minor, hd), device_id_type=pl.DeviceIdType.MESH
+            )
     pl.semaphore_wait(barrier, 2 * len(distinct))
     copies = []
     for k, d in enumerate(shifts):
@@ -42,7 +51,7 @@
         else:
             s_send[k] = out_ref[...].astype(s_send.dtype)
             a_send[k] = dec_acc[...]
-        target = ((me + d) % count, hd)
+        target = ((me + d) % count // minor, (me + d) % count % minor, hd)
         pair = []
         for index, (src, dst) in enumerate(((s_send, s_recv), (a_send, a_recv))):
             copy = pltpu.make_async_remote_copy(
@@ -75,7 +84,8 @@
 
 
 def entering_state(decay, end_state, state_in):
-    count = lax.axis_size("seq")
+    count = seq_size()
+    minor = lax.axis_size("sz")
     heads, rows, lanes = end_state.shape
     decay_rows = jnp.broadcast_to(decay[:, None, None], (heads, 8, lanes))
     shifts = [1]
@@ -85,7 +95,7 @@
         step *= 2
     steps = len(shifts)
     return pl.pallas_call(
-        functools.partial(scan_kernel, count, tuple(shifts)),
+        functools.partial(scan_kernel, count, minor, tuple(shifts)),
         out_shape=jax.ShapeDtypeStruct(end_state.shape, jnp.float32),
         in_specs=[pl.BlockSpec(memory_space=pltpu.VMEM)] * 3,
         out_specs=pl.BlockSpec(memory_space=pltpu.VMEM),
@@ -100,6 +110,11 @@
         ],
         compiler_params=pltpu.CompilerParams(collective_id=0, has_side_effects=True),
     )(end_state, decay_rows, state_in)
+
+
+def gather_seq(value):
+    value = lax.all_gather(value, "sz", axis=0, tiled=True)
+    return lax.all_gather(value, "sx", axis=0, tiled=True)
 
 
 def local(
@@ -119,15 +134,15 @@
     rows = tokens.shape[0]
     heads, head_dim, nstate = state_in.shape
     inner = heads * head_dim
-    seq_count = lax.axis_size("seq")
-    first = lax.axis_index("seq") == 0
+    seq_count = seq_size()
+    first = lax.axis_index(SEQ) == 0
     w_x = w_xz[:, 0, :]
     w_z = w_xz[:, 1, :]
     packed = jnp.concatenate([w_x, w_z, w_bc], axis=1)
-    gathered = lax.all_gather(packed, "seq", axis=0, tiled=True)
-    w_out_cols = lax.all_gather(jnp.transpose(w_out), "seq", axis=0, tiled=True)
+    gathered = gather_seq(packed)
+    w_out_cols = gather_seq(jnp.transpose(w_out))
     lag = conv_x.shape[0] - 1
-    earlier = passed_along(tokens[rows - lag :], "seq", 1)
+    earlier = passed_along(tokens[rows - lag :], SEQ, 1)
     extended = jnp.concatenate([earlier, tokens], axis=0)
     xzbc = jnp.dot(extended, gathered, preferred_element_type=jnp.float32).astype(jnp.bfloat16)
     opening = lax.broadcasted_iota(jnp.int32, (rows + lag, 1), 0) < lag
@@ -195,23 +210,27 @@
 
 
 def solution(mesh):
+    devices = mesh.devices
+    majors = [getattr(d, "coords", (0,))[0] for d in devices[:, 0]]
+    minor = majors.count(majors[0])
+    split = Mesh(devices.reshape(devices.shape[0] // minor, minor, devices.shape[1]), ("sx", "sz", "head"))
     return jax.shard_map(
         local,
-        mesh=mesh,
+        mesh=split,
         in_specs=(
-            P("seq", None),
-            P("seq", None, "head"),
-            P("seq", None),
+            P(SEQ, None),
+            P(SEQ, None, "head"),
+            P(SEQ, None),
             P(None, "head"),
             P(),
             P(None, "head"),
             P(),
-            P("seq", "head"),
+            P(SEQ, "head"),
             P("head"),
             P("head", None, None),
             P("head"),
-            P("head", "seq"),
+            P("head", SEQ),
         ),
-        out_specs=P("seq", "head"),
+        out_specs=P(SEQ, "head"),
         check_vma=False,
     )

time: 273 us -> 328 us (1.20)
  waiting for transfers between devices: 153 us -> 210 us
  Pallas kernels: 41.8 us -> 47.2 us
  blocking collectives: 17.2 us -> 13.2 us
    all_gather x2 -> x4, waiting for transfers between devices: 129 us -> 187 us  [the longest x2 113 us: gather_seq(): return lax.all_gather(value, 'sx', axis=0, tiled=True)]
    pallas_call x1, Pallas kernels: 41.8 us -> 47.2 us  [entering_state(): pl.pallas_call(functools.partial(scan_kernel, count, minor, tuple(shifts)...]
    psum x1, blocking collectives: 17.2 us -> 13.2 us  [local(): total_sq = lax.psum(jnp.sum(gated * gated, axis=1), 'head')]
  transfers between devices with their start and end apart: 4 -> 6, of which waited for: 3 -> 5; matrix products, arithmetic and copies ran while one was open for 11% -> 8% of each run, Pallas kernels for 15% -> 15%
where the time goes in v7:
time: 328 us; the launch traced here: 325 us
  waiting for transfers between devices  210 us (64%)
  Pallas kernels  47.2 us (14%)
  matrix products  20.6 us (6%)
  between operations  13.4 us (4%)
  blocking collectives  13.2 us (4%)
  other arithmetic  11.5 us (4%)
  local copies, waits for them, and re-layouts  6.4 us (2%)
    all_gather x2, waiting for transfers between devices, gather_seq(): return lax.all_gather(value, 'sx', axis=0, tiled=True)  113 us
    all_gather x2, waiting for transfers between devices, gather_seq(): value = lax.all_gather(value, 'sz', axis=0, tiled=True)  74.1 us
    pallas_call x1, Pallas kernels, entering_state(): pl.pallas_call(functools.partial(scan_kernel, count, minor, tuple(shifts)...  47.2 us
    reduce_scatter x1, waiting for transfers between devices, local(): lax.psum_scatter(partial_out.astype(jnp.bfloat16), 'head', scatter_dimens...  22.1 us
    psum x1, blocking collectives, local(): total_sq = lax.psum(jnp.sum(gated * gated, axis=1), 'head')  13.2 us
    dot_general x1, matrix products, local(): jnp.dot(extended, gathered, preferred_element_type=jnp.float32)  10.6 us
  transfers between devices with their start and end apart: 6, of which 5 were waited for; matrix products, arithmetic and copies ran while one was open for 8% of the time, Pallas kernels for 15%

profile of v7, /device:TPU:1, one launch (start us, length us, event | category | flops | bytes accessed | tf_op | source)
XLA Modules:
  0.0 325.3 jit_solution(15459349641125274629)
XLA Ops:
  6.6 1.5 fusion.45
  8.2 1.6 pad_maximum_fusion
  9.8 0.7 all-gather.9.cloned.1.call-update
  10.6 42.5 %all-gather.5.cloned.1.call-done = bf16[1024,1280]{1,0:T(8,128)(2,1)} async-done(((bf16[128,1280]{1,0:T(8,128)(2,1)}), bf16[1024,1280]{1,0:T(8,128)(2,1)}) %all-gather.5.cloned.1.call-update) | async-done | bytes 2621456 | tf_op jit(solution)/shard_map/all_gather | solution.py:116
  53.1 0.9 slice.115
  54.0 3.1 collective-permute-start
  57.1 1.2 reduce-window.14
  58.7 1.1 reduce-window.16
  60.2 31.6 %all-gather.9.cloned.1.call-done = bf16[1024,512]{0,1:T(8,128)(2,1)} async-done(((bf16[128,512]{0,1:T(8,128)(2,1)}), bf16[1024,512]{0,1:T(8,128)(2,1)}) %all-gather.9.cloned.1.call-update) | async-done | bytes 1048592 | tf_op jit(solution)/shard_map/all_gather | solution.py:116
  92.4 108.0 %all-gather.7.cloned.1.call-done = bf16[4096,1280]{1,0:T(8,128)(2,1)} async-done(((bf16[1024,1280]{1,0:T(8,128)(2,1)}), bf16[4096,1280]{1,0:T(8,128)(2,1)}) %all-gather.7.cloned.1.call-update) | async-done | bytes 10485776 | tf_op jit(solution)/shard_map/all_gather | solution.py:117
  200.4 10.6 %fusion.4 = bf16[515,1280]{1,0:T(8,128)(2,1)S(1)} fusion(bf16[4096,1280]{1,0:T(8,128)(2,1)} %all-gather.7.cloned.1.call-done, bf16[512,4096]{1,0:T(8,128)(2,1)} %param.12, bf16[3,4096]{1,0:T(4,128)(2,1)S(1)} %collective-permute-done), kind=kOutput, calls=%fused_computation.6 | convolution fusion | flops 5409263616 | bytes 16023040 | tf_op jit(solution)/shard_map/dot_general | solution.py:147
  211.3 0.9 copy-done
  212.1 0.6 multiply_convert_fusion.8
  212.8 0.5 reshape.101
  213.3 0.6 copy.31
  213.9 1.1 fusion.32
  215.1 0.3 multiply_convert_fusion.10
  215.4 1.0 fusion.21
  216.5 0.8 fusion.33.msg_ref
  217.3 0.7 broadcast_in_dim.52.dec_ref
  217.9 47.2 %shard_map.118 = f32[8,64,128]{2,1,0:T(8,128)} custom-call(f32[8,64,128]{2,1,0:T(8,128)} %fusion.33.msg_ref, f32[8,8,128]{2,1,0:T(8,128)} %broadcast_in_dim.52.dec_ref, f32[8,64,128]{2,1,0:T(8,128)} %sin_ref.1), custom_call_target="tpu_custom_call" | custom-call | tf_op jit(solution)/shard_map/pallas_call | solution.py:97
  265.1 0.2 fusion.48
  265.4 1.2 fusion.13
  266.7 0.4 fusion.16
  267.1 0.6 fusion.15
  267.7 0.3 copy.33
  268.0 2.2 multiply_reduce_fusion
  270.3 4.7 %all-gather.11.cloned.1.call-done = bf16[4096,512]{0,1:T(8,128)(2,1)} async-done(((bf16[1024,512]{0,1:T(8,128)(2,1)}), bf16[4096,512]{0,1:T(8,128)(2,1)}) %all-gather.11.cloned.1.call-update) | async-done | bytes 4194320 | tf_op jit(solution)/shard_map/all_gather | solution.py:117
  274.9 6.5 %convolution_convert_fusion = bf16[512,4096]{1,0:T(8,128)(2,1)} fusion(bf16[4096,512]{0,1:T(8,128)(2,1)} %all-gather.11.cloned.1.call-done, f32[512,512]{1,0:T(8,128)S(1)} %get-tuple-element.6, f32[512]{0:T(512)S(1)} %copy-done.8), kind=kOutput, calls=%fused_computation | convolution fusion | flops 2150105088 | bytes 9439232 | tf_op jit(solution)/shard_map/dot_general | solution.py:201
  281.4 13.2 %psum.7 = f32[512]{0:T(512)S(1)} all-reduce(f32[512]{0:T(512)S(1)} %get-tuple-element.5), channel_id=1, replica_groups=mesh['sx'=4,'sz'=8,'head'=8] {'head'}, use_global_device_ids=true, to_apply=%region_6.7 | all-reduce | flops 512 | bytes 4096 | tf_op jit(solution)/shard_map/psum | solution.py:207
  294.7 22.1 %reduce-scatter.2.cloned.1.call-done = bf16[512,512]{1,0:T(8,128)(2,1)} async-done(((bf16[512,4096]{1,0:T(8,128)(2,1)}), bf16[512,512]{1,0:T(8,128)(2,1)}) %reduce-scatter.2.cloned.1.call-update) | async-done | bytes 524304 | tf_op jit(solution)/shard_map/reduce_scatter | solution.py:204
  316.8 2.0 multiply_convert_fusion.6
  (54 shorter events, 1.8 us)
Async XLA Ops:
  6.5 50.6 %copy-start.2 = (s32[512,8]{0,1:T(8,128)S(1)}, s32[512,8]{0,1:T(8,128)}, u32[]{:S(2)}) copy-start(s32[512,8]{0,1:T(8,128)} %param.19) | copy-start | bytes 49156
  6.5 53.6 %copy-start.5 = (f32[4,256]{1,0:T(4,128)S(1)}, f32[4,256]{1,0:T(4,128)}, u32[]{:S(2)}) copy-start(f32[4,256]{1,0:T(4,128)} %param.16) | copy-start | bytes 12292
  6.5 85.6 %copy-start.3 = (f32[4,512]{1,0:T(4,128)S(1)}, f32[4,512]{1,0:T(4,128)}, u32[]{:S(2)}) copy-start(f32[4,512]{1,0:T(4,128)} %param.15) | copy-start | bytes 24580
  6.5 85.7 %copy-start.7 = (f32[8]{0:T(128)S(1)}, f32[8]{0:T(128)}, u32[]{:S(2)}) copy-start(f32[8]{0:T(128)} %param.20) | copy-start | bytes 100
  6.5 46.5 %all-gather.5.cloned.1.call-start = ((), (), s32[]{:S(2)}) async-start(), calls=%async_computation.1 | async-start | bytes 2949120 | tf_op jit(solution)/shard_map/all_gather | solution.py:116
  9.8 82.1 %all-gather.9.cloned.1.call-start = ((), (), s32[]{:S(2)}) async-start(), calls=%async_computation.3 | async-start | bytes 1179648 | tf_op jit(solution)/shard_map/all_gather | solution.py:116
  10.5 189.9 %all-gather.7.cloned.1.call-start = ((), (), s32[]{:S(2)}) async-start(), calls=%async_computation.2 | async-start | bytes 13107200 | tf_op jit(solution)/shard_map/all_gather | solution.py:117
  53.1 221.8 %all-gather.11.cloned.1.call-start = ((), (), s32[]{:S(2)}) async-start(), calls=%async_computation.4 | async-start | bytes 5242880 | tf_op jit(solution)/shard_map/all_gather | solution.py:117
  54.0 38.4 %collective-permute-start = (bf16[3,4096]{1,0:T(4,128)(2,1)S(1)}, bf16[3,4096]{1,0:T(4,128)(2,1)S(1)}, u32[]{:S(2)}, u32[]{:S(2)}) collective-permute-start(bf16[3,4096]{1,0:T(4,128)(2,1)S(1)} %slice.115), channel_id=1, source_target_pairs={{0,8},{8,16},{16,24},{24,32},{32,40},{40,48},{48,56},{56,64},{64,7... | collective-permute-start | bytes 73736 | tf_op jit(solution)/shard_map/ppermute | solution.py:23
  91.9 224.9 %reduce-scatter.2.cloned.1.call-start = ((), (), s32[]{:S(2)}) async-start(), calls=%async_computation.5 | async-start | bytes 4718592 | tf_op jit(solution)/shard_map/reduce_scatter | solution.py:204
  92.4 118.7 %copy-start.4 = (bf16[3,512]{1,0:T(4,128)(2,1)S(1)}, bf16[3,512]{1,0:T(4,128)(2,1)}, u32[]{:S(2)}) copy-start(bf16[3,512]{1,0:T(4,128)(2,1)} %param.17) | copy-start | bytes 9220
  211.1 1.1 copy-start
  211.2 2.7 copy-start.6
  265.4 1.7 copy-start.1
  267.7 7.2 %copy-start.8 = (f32[512]{0:T(512)S(1)}, f32[512]{0:T(512)}, u32[]{:S(2)}) copy-start(f32[512]{0:T(512)} %param.22) | copy-start | bytes 6148
Sparse Core Ops, SparseCore 0:
  9.9 43.1 all-gather.4
  54.8 37.0 all-gather.8
  93.7 106.7 all-gather.6
  202.1 72.8 all-gather.10
  281.6 35.1 reduce-scatter.1

commit v8 on v6

--- a/solution.py
+++ b/solution.py
@@ -102,6 +102,55 @@
     )(end_state, decay_rows, state_in)
 
 
+def gather_kernel(count, src_ref, out_ref, own_sem, send_sem, recv_sem):
+    me = lax.axis_index("seq")
+    hd = lax.axis_index("head")
+    rows = src_ref.shape[0]
+    barrier = pltpu.get_barrier_semaphore()
+    for k in range(1, count):
+        pl.semaphore_signal(
+            barrier, inc=1, device_id=((me + k) % count, hd), device_id_type=pl.DeviceIdType.MESH
+        )
+    pl.semaphore_wait(barrier, count - 1)
+    place = out_ref.at[pl.ds(me * rows, rows)]
+    own = pltpu.make_async_copy(src_ref, place, own_sem)
+    own.start()
+    copies = []
+    for k in range(1, count):
+        copy = pltpu.make_async_remote_copy(
+            src_ref=src_ref,
+            dst_ref=place,
+            send_sem=send_sem.at[k],
+            recv_sem=recv_sem.at[k],
+            device_id=((me + k) % count, hd),
+            device_id_type=pl.DeviceIdType.MESH,
+        )
+        copy.start()
+        copies.append(copy)
+    for copy in copies:
+        copy.wait_recv()
+    for copy in copies:
+        copy.wait_send()
+    own.wait()
+
+
+def gather_seq(value):
+    count = lax.axis_size("seq")
+    rows, cols = value.shape
+    return pl.pallas_call(
+        functools.partial(gather_kernel, count),
+        out_shape=jax.ShapeDtypeStruct((count * rows, cols), value.dtype),
+        in_specs=[pl.BlockSpec(memory_space=pl.ANY)],
+        out_specs=pl.BlockSpec(memory_space=pl.ANY),
+        scratch_shapes=[
+            pltpu.SemaphoreType.DMA(()),
+            pltpu.SemaphoreType.DMA((count,)),
+            pltpu.SemaphoreType.DMA((count,)),
+        ],
+        compiler_params=pltpu.CompilerParams(collective_id=1, has_side_effects=True),
+    )(value)
+
+
 def local(
     tokens,
     w_xz,
@@ -125,7 +174,7 @@
     w_z = w_xz[:, 1, :]
     packed = jnp.concatenate([w_x, w_z, w_bc], axis=1)
     gathered = lax.all_gather(packed, "seq", axis=0, tiled=True)
-    w_out_cols = lax.all_gather(jnp.transpose(w_out), "seq", axis=0, tiled=True)
+    w_out_cols = gather_seq(jnp.transpose(w_out))
     lag = conv_x.shape[0] - 1
     earlier = passed_along(tokens[rows - lag :], "seq", 1)
     extended = jnp.concatenate([earlier, tokens], axis=0)

time: 273 us -> 314 us (1.15)
  Pallas kernels: 41.8 us -> 179 us
  waiting for transfers between devices: 153 us -> 53.5 us
    pallas_call x0 -> x1, Pallas kernels: none -> 132 us  [gather_seq(): pl.pallas_call(functools.partial(gather_kernel, count), out_shape=jax.Sha...]
    all_gather x1, waiting for transfers between devices: 100 us -> 30.9 us  [local(): gathered = lax.all_gather(packed, 'seq', axis=0, tiled=True)]
    all_gather x1 -> x0, waiting for transfers between devices: 29.1 us -> none  [local(): w_out_cols = lax.all_gather(jnp.transpose(w_out), 'seq', axis=0, tiled=True)]
    pallas_call x1, Pallas kernels: 41.8 us -> 47.3 us  [entering_state(): pl.pallas_call(functools.partial(scan_kernel, count, tuple(shifts)), out_...]
  transfers between devices with their start and end apart: 4 -> 3, of which waited for: 3 -> 2; matrix products, arithmetic and copies ran while one was open for 11% -> 3% of each run, Pallas kernels for 15% -> 42%
where the time goes in v8:
time: 314 us; the launch traced here: 312 us
  Pallas kernels  179 us (57%)
  waiting for transfers between devices  53.5 us (17%)
  matrix products  21.5 us (7%)
  blocking collectives  16.4 us (5%)
  between operations  13.7 us (4%)
  other arithmetic  12.7 us (4%)
  local copies, waits for them, and re-layouts  10.1 us (3%)
  starting transfers between devices  4.42 us (1%)
    pallas_call x1, Pallas kernels, gather_seq(): pl.pallas_call(functools.partial(gather_kernel, count), out_shape=jax.Sha...  132 us
    pallas_call x1, Pallas kernels, entering_state(): pl.pallas_call(functools.partial(scan_kernel, count, tuple(shifts)), out_...  47.3 us
    all_gather x1, waiting for transfers between devices, local(): gathered = lax.all_gather(packed, 'seq', axis=0, tiled=True)  30.9 us
    reduce_scatter x1, waiting for transfers between devices, local(): lax.psum_scatter(partial_out.astype(jnp.bfloat16), 'head', scatter_dimens...  22.6 us
    psum x1, blocking collectives, local(): total_sq = lax.psum(jnp.sum(gated * gated, axis=1), 'head')  16.4 us
    dot_general x1, matrix products, local(): jnp.dot(extended, gathered, preferred_element_type=jnp.float32)  10.6 us
  transfers between devices with their start and end apart: 3, of which 2 were waited for; matrix products, arithmetic and copies ran while one was open for 3% of the time, Pallas kernels for 42%

profile of v8, /device:TPU:1, one launch (start us, length us, event | category | flops | bytes accessed | tf_op | source)
XLA Modules:
  0.0 311.7 jit_solution(10639043978573560179)
XLA Ops:
  6.5 1.5 fusion.45
  8.1 1.6 pad_maximum_fusion
  9.8 0.9 slice.115
  10.6 4.4 %collective-permute-start = (bf16[3,4096]{1,0:T(4,128)(2,1)S(1)}, bf16[3,4096]{1,0:T(4,128)(2,1)S(1)}, u32[]{:S(2)}, u32[]{:S(2)}) collective-permute-start(bf16[3,4096]{1,0:T(4,128)(2,1)S(1)} %slice.115), channel_id=1, source_target_pairs={{0,8},{8,16},{16,24},{24,32},{32,40},{40,48},{48,56},{56,64},{64,7... | collective-permute-start | bytes 73736 | tf_op jit(solution)/shard_map/ppermute | solution.py:16
  15.0 0.7 fusion.40
  15.8 1.1 reduce-window.14
  17.3 1.1 reduce-window.16
  19.0 0.6 slice_bitcast_fusion.7
  19.6 0.8 fusion.47
  20.4 0.9 fusion.46
  21.3 0.7 subtract_exponential_fusion
  21.9 0.7 broadcast_in_dim.53
  22.8 1.6 copy.36
  24.4 132.2 %shard_map.119 = bf16[4096,512]{1,0:T(8,128)(2,1)} custom-call(bf16[128,512]{1,0:T(8,128)(2,1)} %bitcast.73), custom_call_target="tpu_custom_call" | custom-call | tf_op jit(solution)/shard_map/pallas_call | solution.py:140
  156.6 30.9 %all-gather.2.cloned.1.call-done = bf16[4096,1280]{1,0:T(8,128)(2,1)} async-done(((bf16[128,1280]{1,0:T(8,128)(2,1)}), bf16[4096,1280]{1,0:T(8,128)(2,1)}) %all-gather.2.cloned.1.call-update) | async-done | bytes 10485776 | tf_op jit(solution)/shard_map/all_gather | solution.py:176
  187.5 10.6 %fusion.4 = bf16[515,1280]{1,0:T(8,128)(2,1)S(1)} fusion(bf16[4096,1280]{1,0:T(8,128)(2,1)} %all-gather.2.cloned.1.call-done, bf16[512,4096]{1,0:T(8,128)(2,1)} %param.12, bf16[3,4096]{1,0:T(4,128)(2,1)S(1)} %collective-permute-done), kind=kOutput, calls=%fused_computation.6 | convolution fusion | flops 5409263616 | bytes 16023040 | tf_op jit(solution)/shard_map/dot_general | solution.py:181
  198.7 0.7 convert_element_type.62
  199.4 1.0 fusion.48
  200.6 0.6 multiply_convert_fusion.8
  201.3 0.5 reshape.101
  201.8 0.6 copy.33
  202.4 2.3 fusion.13
  204.8 1.2 fusion.21
  206.4 0.8 fusion.33.msg_ref
  207.2 0.7 broadcast_in_dim.52.dec_ref
  207.9 47.3 %shard_map.118 = f32[8,64,128]{2,1,0:T(8,128)} custom-call(f32[8,64,128]{2,1,0:T(8,128)} %fusion.33.msg_ref, f32[8,8,128]{2,1,0:T(8,128)} %broadcast_in_dim.52.dec_ref, f32[8,64,128]{2,1,0:T(8,128)} %sin_ref.1), custom_call_target="tpu_custom_call" | custom-call | tf_op jit(solution)/shard_map/pallas_call | solution.py:87
  255.2 1.6 fusion.15
  257.1 2.4 multiply_reduce_fusion
  259.5 4.3 %convolution_convert_fusion = bf16[512,4096]{1,0:T(8,128)(2,1)} fusion(bf16[4096,512]{1,0:T(8,128)(2,1)S(1)} %copy-done, f32[512,512]{1,0:T(8,128)S(1)} %get-tuple-element.6, f32[512]{0:T(512)S(1)} %copy-done.6), kind=kOutput, calls=%fused_computation | convolution fusion | flops 2150105088 | bytes 9439232 | tf_op jit(solution)/shard_map/dot_general | solution.py:235
  263.8 16.4 %psum.7 = f32[512]{0:T(512)S(1)} all-reduce(f32[512]{0:T(512)S(1)} %get-tuple-element.5), channel_id=1, replica_groups=mesh['seq'=32,'head'=8] {'head'}, use_global_device_ids=true, to_apply=%region_6.7 | all-reduce | flops 512 | bytes 4096 | tf_op jit(solution)/shard_map/psum | solution.py:241
  280.2 22.6 %reduce-scatter.2.cloned.1.call-done = bf16[512,512]{1,0:T(8,128)(2,1)} async-done(((bf16[512,4096]{1,0:T(8,128)(2,1)}), bf16[512,512]{1,0:T(8,128)(2,1)}) %reduce-scatter.2.cloned.1.call-update) | async-done | bytes 524304 | tf_op jit(solution)/shard_map/reduce_scatter | solution.py:238
  302.8 2.0 multiply_convert_fusion.6
  (43 shorter events, 2.6 us)
Async XLA Ops:
  6.5 181.0 %all-gather.2.cloned.1.call-start = ((), (), s32[]{:S(2)}) async-start(), calls=%async_computation.1 | async-start | bytes 10813440 | tf_op jit(solution)/shard_map/all_gather | solution.py:176
  9.7 293.1 %reduce-scatter.2.cloned.1.call-start = ((), (), s32[]{:S(2)}) async-start(), calls=%async_computation.2 | async-start | bytes 4718592 | tf_op jit(solution)/shard_map/reduce_scatter | solution.py:238
  10.6 146.0 %collective-permute-start = (bf16[3,4096]{1,0:T(4,128)(2,1)S(1)}, bf16[3,4096]{1,0:T(4,128)(2,1)S(1)}, u32[]{:S(2)}, u32[]{:S(2)}) collective-permute-start(bf16[3,4096]{1,0:T(4,128)(2,1)S(1)} %slice.115), channel_id=1, source_target_pairs={{0,8},{8,16},{16,24},{24,32},{32,40},{40,48},{48,56},{56,64},{64,7... | collective-permute-start | bytes 73736 | tf_op jit(solution)/shard_map/ppermute | solution.py:16
  156.6 41.5 %copy-start.4 = (bf16[3,256]{1,0:T(4,128)(2,1)S(1)}, bf16[3,256]{1,0:T(4,128)(2,1)}, u32[]{:S(2)}) copy-start(bf16[3,256]{1,0:T(4,128)(2,1)} %param.18) | copy-start | bytes 4612
  198.2 2.4 copy-start.1
  198.2 2.3 copy-start.3
  202.4 2.4 copy-start.2
  202.4 4.0 %copy-start.5 = (f32[8]{0:T(128)S(1)}, f32[8]{0:T(128)}, u32[]{:S(2)}) copy-start(f32[8]{0:T(128)} %slice_bitcast_fusion.7) | copy-start | bytes 100
  256.8 2.7 copy-start.6
  257.1 2.4 copy-start
Sparse Core Ops, SparseCore 0:
  9.9 177.5 all-gather.1
  264.0 38.8 reduce-scatter.1

commit v9 on v6

--- a/solution.py
+++ b/solution.py
@@ -102,6 +102,67 @@
     )(end_state, decay_rows, state_in)
 
 
+def ring_kernel(count, src_ref, out_ref, own_sem, send_r, recv_r, send_l, recv_l):
+    me = lax.axis_index("seq")
+    hd = lax.axis_index("head")
+    rows = src_ref.shape[0]
+    right = (me + 1) % count
+    left = (me + count - 1) % count
+    barrier = pltpu.get_barrier_semaphore()
+    for peer in (left, right):
+        pl.semaphore_signal(barrier, inc=1, device_id=(peer, hd), device_id_type=pl.DeviceIdType.MESH)
+    pl.semaphore_wait(barrier, 2)
+    own = pltpu.make_async_copy(src_ref, out_ref.at[pl.ds(me * rows, rows)], own_sem)
+    own.start()
+    to_right = count // 2
+    to_left = count - 1 - to_right
+    copies = []
+    for t in range(max(to_right, to_left)):
+        step = []
+        for steps, sign, peer, sends, recvs in ((to_right, -1, right, send_r, recv_r), (to_left, 1, left, send_l, recv_l)):
+            if t >= steps:
+                continue
+            block = (me + sign * t + count) % count
+            place = out_ref.at[pl.ds(block * rows, rows)]
+            copy = pltpu.make_async_remote_copy(
+                src_ref=src_ref if t == 0 else place,
+                dst_ref=place,
+                send_sem=sends.at[t],
+                recv_sem=recvs.at[t],
+                device_id=(peer, hd),
+                device_id_type=pl.DeviceIdType.MESH,
+            )
+            copy.start()
+            step.append(copy)
+        for copy in step:
+            copy.wait_recv()
+        copies.extend(step)
+    for copy in copies:
+        copy.wait_send()
+    own.wait()
+
+
+def gather_seq(value):
+    count = lax.axis_size("seq")
+    rows, cols = value.shape
+    to_right = count // 2
+    to_left = count - 1 - to_right
+    return pl.pallas_call(
+        functools.partial(ring_kernel, count),
+        out_shape=jax.ShapeDtypeStruct((count * rows, cols), value.dtype),
+        in_specs=[pl.BlockSpec(memory_space=pl.ANY)],
+        out_specs=pl.BlockSpec(memory_space=pl.ANY),
+        scratch_shapes=[
+            pltpu.SemaphoreType.DMA(()),
+            pltpu.SemaphoreType.DMA((to_right,)),
+            pltpu.SemaphoreType.DMA((to_right,)),
+            pltpu.SemaphoreType.DMA((max(to_left, 1),)),
+            pltpu.SemaphoreType.DMA((max(to_left, 1),)),
+        ],
+        compiler_params=pltpu.CompilerParams(collective_id=1, has_side_effects=True),
+    )(value)
+
+
 def local(
     tokens,
     w_xz,
@@ -125,7 +186,7 @@
     w_z = w_xz[:, 1, :]
     packed = jnp.concatenate([w_x, w_z, w_bc], axis=1)
     gathered = lax.all_gather(packed, "seq", axis=0, tiled=True)
-    w_out_cols = lax.all_gather(jnp.transpose(w_out), "seq", axis=0, tiled=True)
+    w_out_cols = gather_seq(jnp.transpose(w_out))
     lag = conv_x.shape[0] - 1
     earlier = passed_along(tokens[rows - lag :], "seq", 1)
     extended = jnp.concatenate([earlier, tokens], axis=0)

time: 273 us -> 277 us (1.015)
  waiting for transfers between devices: 153 us -> 23.1 us
  Pallas kernels: 41.8 us -> 157 us
  blocking collectives: 17.2 us -> 31.1 us
    pallas_call x0 -> x1, Pallas kernels: none -> 125 us  [gather_seq(): pl.pallas_call(functools.partial(ring_kernel, count), out_shape=jax.Shape...]
    all_gather x1, waiting for transfers between devices: 100 us -> 0.02 us  [local(): gathered = lax.all_gather(packed, 'seq', axis=0, tiled=True)]
    all_gather x1 -> x0, waiting for transfers between devices: 29.1 us -> none  [local(): w_out_cols = lax.all_gather(jnp.transpose(w_out), 'seq', axis=0, tiled=True)]
    psum x1, blocking collectives: 17.2 us -> 31.1 us  [local(): total_sq = lax.psum(jnp.sum(gated * gated, axis=1), 'head')]
    pallas_call x1, Pallas kernels: 41.8 us -> 32.7 us  [entering_state(): pl.pallas_call(functools.partial(scan_kernel, count, tuple(shifts)), out_...]
  transfers between devices with their start and end apart: 4 -> 3, of which waited for: 3 -> 1; matrix products, arithmetic and copies ran while one was open for 11% -> 4% of each run, Pallas kernels for 15% -> 46%
where the time goes in v9:
time: 277 us; the launch traced here: 274 us
  Pallas kernels  157 us (57%)
  blocking collectives  31.1 us (11%)
  waiting for transfers between devices  23.1 us (8%)
  matrix products  21.5 us (8%)
  between operations  13.7 us (5%)
  other arithmetic  12.7 us (5%)
  local copies, waits for them, and re-layouts  10.1 us (4%)
  starting transfers between devices  4.42 us (2%)
    pallas_call x1, Pallas kernels, gather_seq(): pl.pallas_call(functools.partial(ring_kernel, count), out_shape=jax.Shape...  125 us
    pallas_call x1, Pallas kernels, entering_state(): pl.pallas_call(functools.partial(scan_kernel, count, tuple(shifts)), out_...  32.7 us
    psum x1, blocking collectives, local(): total_sq = lax.psum(jnp.sum(gated * gated, axis=1), 'head')  31.1 us
    reduce_scatter x1, waiting for transfers between devices, local(): lax.psum_scatter(partial_out.astype(jnp.bfloat16), 'head', scatter_dimens...  23 us
    dot_general x1, matrix products, local(): jnp.dot(extended, gathered, preferred_element_type=jnp.float32)  10.7 us
  transfers between devices with their start and end apart: 3, of which 1 were waited for; matrix products, arithmetic and copies ran while one was open for 4% of the time, Pallas kernels for 46%

profile of v9, /device:TPU:1, one launch (start us, length us, event | category | flops | bytes accessed | tf_op | source)
XLA Modules:
  0.0 273.9 jit_solution(15403802004760598346)
XLA Ops:
  6.5 1.5 fusion.45
  8.1 1.6 pad_maximum_fusion
  9.8 0.9 slice.115
  10.6 4.4 %collective-permute-start = (bf16[3,4096]{1,0:T(4,128)(2,1)S(1)}, bf16[3,4096]{1,0:T(4,128)(2,1)S(1)}, u32[]{:S(2)}, u32[]{:S(2)}) collective-permute-start(bf16[3,4096]{1,0:T(4,128)(2,1)S(1)} %slice.115), channel_id=1, source_target_pairs={{0,8},{8,16},{16,24},{24,32},{32,40},{40,48},{48,56},{56,64},{64,7... | collective-permute-start | bytes 73736 | tf_op jit(solution)/shard_map/ppermute | solution.py:16
  15.0 0.7 fusion.40
  15.8 1.1 reduce-window.14
  17.3 1.1 reduce-window.16
  19.0 0.6 slice_bitcast_fusion.7
  19.6 0.8 fusion.47
  20.4 0.9 fusion.46
  21.3 0.7 subtract_exponential_fusion
  21.9 0.7 broadcast_in_dim.53
  22.8 1.6 copy.36
  24.4 124.7 %shard_map.119 = bf16[4096,512]{1,0:T(8,128)(2,1)} custom-call(bf16[128,512]{1,0:T(8,128)(2,1)} %bitcast.73), custom_call_target="tpu_custom_call" | custom-call | tf_op jit(solution)/shard_map/pallas_call | solution.py:150
  149.2 10.7 %fusion.4 = bf16[515,1280]{1,0:T(8,128)(2,1)S(1)} fusion(bf16[4096,1280]{1,0:T(8,128)(2,1)} %all-gather.2.cloned.1.call-done, bf16[512,4096]{1,0:T(8,128)(2,1)} %param.12, bf16[3,4096]{1,0:T(4,128)(2,1)S(1)} %collective-permute-done), kind=kOutput, calls=%fused_computation.6 | convolution fusion | flops 5409263616 | bytes 16023040 | tf_op jit(solution)/shard_map/dot_general | solution.py:193
  160.4 0.7 convert_element_type.62
  161.1 1.0 fusion.48
  162.3 0.6 multiply_convert_fusion.8
  162.9 0.5 reshape.101
  163.5 0.6 copy.33
  164.1 2.3 fusion.13
  166.5 1.2 fusion.21
  167.7 0.4 fusion.16
  168.1 0.8 fusion.33.msg_ref
  168.9 0.7 broadcast_in_dim.52.dec_ref
  169.6 32.7 %shard_map.118 = f32[8,64,128]{2,1,0:T(8,128)} custom-call(f32[8,64,128]{2,1,0:T(8,128)} %fusion.33.msg_ref, f32[8,8,128]{2,1,0:T(8,128)} %broadcast_in_dim.52.dec_ref, f32[8,64,128]{2,1,0:T(8,128)} %sin_ref.1), custom_call_target="tpu_custom_call" | custom-call | tf_op jit(solution)/shard_map/pallas_call | solution.py:87
  202.3 1.6 fusion.15
  204.3 2.4 multiply_reduce_fusion
  206.7 4.3 %convolution_convert_fusion = bf16[512,4096]{1,0:T(8,128)(2,1)} fusion(bf16[4096,512]{1,0:T(8,128)(2,1)S(1)} %copy-done, f32[512,512]{1,0:T(8,128)S(1)} %get-tuple-element.6, f32[512]{0:T(512)S(1)} %copy-done.6), kind=kOutput, calls=%fused_computation | convolution fusion | flops 2150105088 | bytes 9439232 | tf_op jit(solution)/shard_map/dot_general | solution.py:247
  211.0 31.1 %psum.7 = f32[512]{0:T(512)S(1)} all-reduce(f32[512]{0:T(512)S(1)} %get-tuple-element.5), channel_id=1, replica_groups=mesh['seq'=32,'head'=8] {'head'}, use_global_device_ids=true, to_apply=%region_6.7 | all-reduce | flops 512 | bytes 4096 | tf_op jit(solution)/shard_map/psum | solution.py:253
  242.1 23.0 %reduce-scatter.2.cloned.1.call-done = bf16[512,512]{1,0:T(8,128)(2,1)} async-done(((bf16[512,4096]{1,0:T(8,128)(2,1)}), bf16[512,512]{1,0:T(8,128)(2,1)}) %reduce-scatter.2.cloned.1.call-update) | async-done | bytes 524304 | tf_op jit(solution)/shard_map/reduce_scatter | solution.py:250
  265.1 2.0 multiply_convert_fusion.6
  (43 shorter events, 2.2 us)
Async XLA Ops:
  6.5 142.6 %all-gather.2.cloned.1.call-start = ((), (), s32[]{:S(2)}) async-start(), calls=%async_computation.1 | async-start | bytes 10813440 | tf_op jit(solution)/shard_map/all_gather | solution.py:188
  9.7 255.4 %reduce-scatter.2.cloned.1.call-start = ((), (), s32[]{:S(2)}) async-start(), calls=%async_computation.2 | async-start | bytes 4718592 | tf_op jit(solution)/shard_map/reduce_scatter | solution.py:250
  10.6 138.5 %collective-permute-start = (bf16[3,4096]{1,0:T(4,128)(2,1)S(1)}, bf16[3,4096]{1,0:T(4,128)(2,1)S(1)}, u32[]{:S(2)}, u32[]{:S(2)}) collective-permute-start(bf16[3,4096]{1,0:T(4,128)(2,1)S(1)} %slice.115), channel_id=1, source_target_pairs={{0,8},{8,16},{16,24},{24,32},{32,40},{40,48},{48,56},{56,64},{64,7... | collective-permute-start | bytes 73736 | tf_op jit(solution)/shard_map/ppermute | solution.py:16
  149.1 10.7 %copy-start.4 = (bf16[3,256]{1,0:T(4,128)(2,1)S(1)}, bf16[3,256]{1,0:T(4,128)(2,1)}, u32[]{:S(2)}) copy-start(bf16[3,256]{1,0:T(4,128)(2,1)} %param.18) | copy-start | bytes 4612
  159.8 2.4 copy-start.1
  159.9 2.3 copy-start.3
  164.1 2.4 copy-start.2
  164.1 4.0 %copy-start.5 = (f32[8]{0:T(128)S(1)}, f32[8]{0:T(128)}, u32[]{:S(2)}) copy-start(f32[8]{0:T(128)} %slice_bitcast_fusion.7) | copy-start | bytes 100
  203.9 2.7 copy-start.6
  204.3 2.4 copy-start
Sparse Core Ops, SparseCore 0:
  9.9 137.6 all-gather.1
  211.1 53.9 reduce-scatter.1

commit v10 on v6

--- a/solution.py
+++ b/solution.py
@@ -183,11 +183,11 @@
     y_val = parts / nstate + jnp.repeat(skip_gain, head_dim)[None, :] * x_conv.astype(jnp.float32)
     gated = y_val * jax.nn.silu(z_val.astype(jnp.float32))
     scaled = (gated * norm_gain[None, :]).astype(jnp.bfloat16)
-    partial_out = lax.dot_general(
-        scaled, w_out_cols, (((1,), (1,)), ((), ())), preferred_element_type=jnp.float32
+    partial_t = lax.dot_general(
+        w_out_cols, scaled, (((1,), (1,)), ((), ())), preferred_element_type=jnp.float32
     )
-    result = lax.psum_scatter(
-        partial_out.astype(jnp.bfloat16), "head", scatter_dimension=1, tiled=True
+    result = jnp.transpose(
+        lax.psum_scatter(partial_t.astype(jnp.bfloat16), "head", scatter_dimension=0, tiled=True)
     ).astype(jnp.float32)
     total_sq = lax.psum(jnp.sum(gated * gated, axis=1), "head")
     meansq = total_sq / (inner * lax.axis_size("head"))

time: 273 us -> 273 us (level)
  no operation moved by 1% of the time
where the time goes in v10:
time: 273 us; the launch traced here: 271 us
  waiting for transfers between devices  153 us (56%)
  Pallas kernels  41.8 us (15%)
  matrix products  20.6 us (8%)
  blocking collectives  17.2 us (6%)
  between operations  13.4 us (5%)
  other arithmetic  12.2 us (4%)
  local copies, waits for them, and re-layouts  8.73 us (3%)
  starting transfers between devices  4.45 us (2%)
    all_gather x1, waiting for transfers between devices, local(): gathered = lax.all_gather(packed, 'seq', axis=0, tiled=True)  100 us
    pallas_call x1, Pallas kernels, entering_state(): pl.pallas_call(functools.partial(scan_kernel, count, tuple(shifts)), out_...  41.8 us
    all_gather x1, waiting for transfers between devices, local(): w_out_cols = lax.all_gather(jnp.transpose(w_out), 'seq', axis=0, tiled=True)  29.1 us
    reduce_scatter x1, waiting for transfers between devices, local(): lax.psum_scatter(partial_t.astype(jnp.bfloat16), 'head', scatter_dimensio...  22.7 us
    psum x1, blocking collectives, local(): total_sq = lax.psum(jnp.sum(gated * gated, axis=1), 'head')  17.2 us
    dot_general x1, matrix products, local(): jnp.dot(extended, gathered, preferred_element_type=jnp.float32)  10.6 us
    dot_general x1, matrix products, local(): lax.dot_general(w_out_cols, scaled, (((1,), (1,)), ((), ())), preferred_e...  6.46 us
  transfers between devices with their start and end apart: 4, of which 3 were waited for; matrix products, arithmetic and copies ran while one was open for 11% of the time, Pallas kernels for 15%

profile of v10, /device:TPU:1, one launch (start us, length us, event | category | flops | bytes accessed | tf_op | source)
XLA Modules:
  0.0 270.9 jit_solution(8330279188414351177)
XLA Ops:
  6.5 1.5 fusion.47
  8.1 1.6 pad_maximum_fusion
  9.8 0.7 all-gather.5.cloned.1.call-update
  10.5 0.9 slice.115
  11.4 4.4 %collective-permute-start = (bf16[3,4096]{1,0:T(4,128)(2,1)S(1)}, bf16[3,4096]{1,0:T(4,128)(2,1)S(1)}, u32[]{:S(2)}, u32[]{:S(2)}) collective-permute-start(bf16[3,4096]{1,0:T(4,128)(2,1)S(1)} %slice.115), channel_id=1, source_target_pairs={{0,8},{8,16},{16,24},{24,32},{32,40},{40,48},{48,56},{56,64},{64,7... | collective-permute-start | bytes 73736 | tf_op jit(solution)/shard_map/ppermute | solution.py:16
  15.8 0.7 fusion.42
  16.5 1.1 reduce-window.14
  18.1 1.1 reduce-window.16
  19.7 0.8 fusion.49
  20.6 0.9 fusion.48
  21.5 0.7 broadcast_in_dim.53
  22.4 100.0 %all-gather.3.cloned.1.call-done = bf16[4096,1280]{1,0:T(8,128)(2,1)} async-done(((bf16[128,1280]{1,0:T(8,128)(2,1)}), bf16[4096,1280]{1,0:T(8,128)(2,1)}) %all-gather.3.cloned.1.call-update) | async-done | bytes 10485776 | tf_op jit(solution)/shard_map/all_gather | solution.py:127
  122.4 10.6 %fusion.5 = bf16[515,1280]{1,0:T(8,128)(2,1)S(1)} fusion(bf16[4096,1280]{1,0:T(8,128)(2,1)} %all-gather.3.cloned.1.call-done, bf16[512,4096]{1,0:T(8,128)(2,1)} %param.12, bf16[3,4096]{1,0:T(4,128)(2,1)S(1)} %collective-permute-done), kind=kOutput, calls=%fused_computation.7 | convolution fusion | flops 5409263616 | bytes 16023040 | tf_op jit(solution)/shard_map/dot_general | solution.py:132
  133.2 0.9 copy-done
  134.1 0.6 multiply_convert_fusion.8
  134.8 0.5 reshape.101
  135.3 0.6 copy.31
  135.9 1.1 fusion.34
  137.4 1.0 fusion.22
  138.4 0.8 fusion.35.msg_ref
  139.2 0.7 broadcast_in_dim.52.dec_ref
  139.9 41.8 %shard_map.118 = f32[8,64,128]{2,1,0:T(8,128)} custom-call(f32[8,64,128]{2,1,0:T(8,128)} %fusion.35.msg_ref, f32[8,8,128]{2,1,0:T(8,128)} %broadcast_in_dim.52.dec_ref, f32[8,64,128]{2,1,0:T(8,128)} %sin_ref.1), custom_call_target="tpu_custom_call" | custom-call | tf_op jit(solution)/shard_map/pallas_call | solution.py:87
  182.0 1.2 fusion.14
  183.2 0.4 fusion.17
  183.7 0.6 fusion.16
  184.3 0.3 copy.33
  184.6 2.2 multiply_reduce_fusion
  186.9 29.1 %all-gather.5.cloned.1.call-done = bf16[4096,512]{0,1:T(8,128)(2,1)} async-done(((bf16[128,512]{0,1:T(8,128)(2,1)}), bf16[4096,512]{0,1:T(8,128)(2,1)}) %all-gather.5.cloned.1.call-update) | async-done | bytes 4194320 | tf_op jit(solution)/shard_map/all_gather | solution.py:128
  216.0 6.5 %fusion = bf16[4096,512]{0,1:T(8,128)(2,1)} fusion(bf16[4096,512]{0,1:T(8,128)(2,1)} %all-gather.5.cloned.1.call-done, f32[512,512]{1,0:T(8,128)S(1)} %get-tuple-element.6, f32[512]{0:T(512)S(1)} %copy-done.4), kind=kOutput, calls=%fused_computation.1 | convolution fusion | flops 2150105088 | bytes 9439232 | tf_op jit(solution)/shard_map/dot_general | solution.py:186
  222.5 17.2 %psum.7 = f32[512]{0:T(512)S(1)} all-reduce(f32[512]{0:T(512)S(1)} %get-tuple-element.5), channel_id=1, replica_groups=mesh['seq'=32,'head'=8] {'head'}, use_global_device_ids=true, to_apply=%region_6.7 | all-reduce | flops 512 | bytes 4096 | tf_op jit(solution)/shard_map/psum | solution.py:192
  239.7 22.7 %reduce-scatter.2.cloned.1.call-done = bf16[512,512]{0,1:T(8,128)(2,1)} async-done(((bf16[4096,512]{0,1:T(8,128)(2,1)}), bf16[512,512]{0,1:T(8,128)(2,1)}) %reduce-scatter.2.cloned.1.call-update) | async-done | bytes 524304 | tf_op jit(solution)/shard_map/reduce_scatter | solution.py:190
  262.4 2.0 fusion.29
  (40 shorter events, 2.1 us)
Async XLA Ops:
  6.5 115.9 %all-gather.3.cloned.1.call-start = ((), (), s32[]{:S(2)}) async-start(), calls=%async_computation.1 | async-start | bytes 10813440 | tf_op jit(solution)/shard_map/all_gather | solution.py:127
  9.7 206.2 %all-gather.5.cloned.1.call-start = ((), (), s32[]{:S(2)}) async-start(), calls=%async_computation.2 | async-start | bytes 4325376 | tf_op jit(solution)/shard_map/all_gather | solution.py:128
  10.5 251.9 %reduce-scatter.2.cloned.1.call-start = ((), (), s32[]{:S(2)}) async-start(), calls=%async_computation.3 | async-start | bytes 4718592 | tf_op jit(solution)/shard_map/reduce_scatter | solution.py:190
  11.4 11.0 %collective-permute-start = (bf16[3,4096]{1,0:T(4,128)(2,1)S(1)}, bf16[3,4096]{1,0:T(4,128)(2,1)S(1)}, u32[]{:S(2)}, u32[]{:S(2)}) collective-permute-start(bf16[3,4096]{1,0:T(4,128)(2,1)S(1)} %slice.115), channel_id=1, source_target_pairs={{0,8},{8,16},{16,24},{24,32},{32,40},{40,48},{48,56},{56,64},{64,7... | collective-permute-start | bytes 73736 | tf_op jit(solution)/shard_map/ppermute | solution.py:16
  22.3 110.7 %copy-start.2 = (bf16[3,512]{1,0:T(4,128)(2,1)S(1)}, bf16[3,512]{1,0:T(4,128)(2,1)}, u32[]{:S(2)}) copy-start(bf16[3,512]{1,0:T(4,128)(2,1)} %param.17) | copy-start | bytes 9220
  133.1 1.1 copy-start
  133.2 2.7 copy-start.3
  181.9 1.7 copy-start.1
  184.3 31.7 %copy-start.4 = (f32[512]{0:T(512)S(1)}, f32[512]{0:T(512)}, u32[]{:S(2)}) copy-start(f32[512]{0:T(512)} %param.22) | copy-start | bytes 6148
Sparse Core Ops, SparseCore 0:
  9.9 112.4 all-gather.2
  124.9 91.0 all-gather.4
  222.6 39.7 reduce-scatter.1

commit v11 on v10

--- a/solution.py
+++ b/solution.py
@@ -5,9 +5,16 @@
 from jax import lax
 from jax.experimental import pallas as pl
 from jax.experimental.pallas import tpu as pltpu
-from jax.sharding import PartitionSpec as P
+from jax.sharding import Mesh, PartitionSpec as P
 
 Q = 256
+
+
+HEAD = ("hy", "hc")
+
+
+def head_size():
+    return lax.axis_size("hy") * lax.axis_size("hc")
 
 
 def passed_along(value, axis, by):
@@ -27,12 +34,13 @@
 
 def scan_kernel(count, shifts, msg_ref, dec_ref, sin_ref, out_ref, dec_acc, s_send, a_send, s_recv, a_recv, send_sem, recv_sem):
     me = lax.axis_index("seq")
-    hd = lax.axis_index("head")
+    hy = lax.axis_index("hy")
+    hc = lax.axis_index("hc")
     barrier = pltpu.get_barrier_semaphore()
     distinct = sorted(set(shifts))
     for d in distinct:
         for peer in ((me + d) % count, (me + count - d) % count):
-            pl.semaphore_signal(barrier, inc=1, device_id=(peer, hd), device_id_type=pl.DeviceIdType.MESH)
+            pl.semaphore_signal(barrier, inc=1, device_id=(peer, hy, hc), device_id_type=pl.DeviceIdType.MESH)
     pl.semaphore_wait(barrier, 2 * len(distinct))
     copies = []
     for k, d in enumerate(shifts):
@@ -42,7 +50,7 @@
         else:
             s_send[k] = out_ref[...].astype(s_send.dtype)
             a_send[k] = dec_acc[...]
-        target = ((me + d) % count, hd)
+        target = ((me + d) % count, hy, hc)
         pair = []
         for index, (src, dst) in enumerate(((s_send, s_recv), (a_send, a_recv))):
             copy = pltpu.make_async_remote_copy(
@@ -186,32 +194,42 @@
     partial_t = lax.dot_general(
         w_out_cols, scaled, (((1,), (1,)), ((), ())), preferred_element_type=jnp.float32
     )
+    cores = lax.axis_size("hc")
+    mine = lax.axis_index("hc")
+    split = partial_t.reshape(lax.axis_size("hy"), cores, -1, partial_t.shape[1])
+    other = jnp.where(mine == 0, split[:, 1], split[:, 0])
+    kept = jnp.where(mine == 0, split[:, 0], split[:, 1])
+    got = lax.ppermute(other.astype(jnp.bfloat16), "hc", [(i, (i + 1) % cores) for i in range(cores)])
+    chip_sum = (kept + got.astype(jnp.float32)).astype(jnp.bfloat16)
     result = jnp.transpose(
-        lax.psum_scatter(partial_t.astype(jnp.bfloat16), "head", scatter_dimension=0, tiled=True)
+        lax.psum_scatter(chip_sum, "hy", scatter_dimension=0, tiled=False)
     ).astype(jnp.float32)
-    total_sq = lax.psum(jnp.sum(gated * gated, axis=1), "head")
-    meansq = total_sq / (inner * lax.axis_size("head"))
+    total_sq = lax.psum(jnp.sum(gated * gated, axis=1), HEAD)
+    meansq = total_sq / (inner * head_size())
     return (result * lax.rsqrt(meansq[:, None] + 1e-05)).astype(jnp.bfloat16)
 
 
 def solution(mesh):
+    devices = mesh.devices
+    cores = 2 if devices.shape[1] % 2 == 0 else 1
+    split = Mesh(devices.reshape(devices.shape[0], devices.shape[1] // cores, cores), ("seq", "hy", "hc"))
     return jax.shard_map(
         local,
-        mesh=mesh,
+        mesh=split,
         in_specs=(
             P("seq", None),
-            P("seq", None, "head"),
+            P("seq", None, HEAD),
             P("seq", None),
-            P(None, "head"),
+            P(None, HEAD),
             P(),
-            P(None, "head"),
+            P(None, HEAD),
             P(),
-            P("seq", "head"),
-            P("head"),
-            P("head", None, None),
-            P("head"),
-            P("head", "seq"),
+            P("seq", HEAD),
+            P(HEAD),
+            P(HEAD, None, None),
+            P(HEAD),
+            P(HEAD, "seq"),
         ),
-        out_specs=P("seq", "head"),
+        out_specs=P("seq", HEAD),
         check_vma=False,
     )

time: 273 us -> 296 us (1.084)
  local copies, waits for them, and re-layouts: 8.73 us -> 34.4 us
  waiting for transfers between devices: 153 us -> 136 us
  other arithmetic: 12.2 us -> 20.4 us
  Pallas kernels: 41.8 us -> 47.3 us
  blocking collectives: 17.2 us -> 12.1 us
  matrix products: 20.6 us -> 24.6 us
  starting transfers between devices: 4.45 us -> 7.58 us
    all_gather x1, waiting for transfers between devices: 29.1 us -> 14.8 us  [local(): w_out_cols = lax.all_gather(jnp.transpose(w_out), 'seq', axis=0, tiled=True)]
    reshape x0 -> x1, local copies, waits for them, and re-layouts: none -> 11.7 us  [local(): partial_t.reshape(lax.axis_size('hy'), cores, -1, partial_t.shape[1])]
    slice x1 -> x2, local copies, waits for them, and re-layouts: 0.16 us -> 11.4 us  [the longest x1 11.2 us: local(): kept = jnp.where(mine == 0, split[:, 0], split[:, 1])]
    convert_element_type x0 -> x2, other arithmetic: none -> 5.97 us  [the longest x1 3.68 us: local(): chip_sum = (kept + got.astype(jnp.float32)).astype(jnp.bfloat16)]
    pallas_call x1, Pallas kernels: 41.8 us -> 47.3 us  [entering_state(): pl.pallas_call(functools.partial(scan_kernel, count, tuple(shifts)), out_...]
    psum x1, blocking collectives: 17.2 us -> 12.1 us  [local(): total_sq = lax.psum(jnp.sum(gated * gated, axis=1), HEAD)]
    all_gather x1, waiting for transfers between devices: 100 us -> 96 us  [local(): gathered = lax.all_gather(packed, 'seq', axis=0, tiled=True)]
    ppermute x0 -> x1, waiting for transfers between devices: none -> 3.79 us  [local(): lax.ppermute(other.astype(jnp.bfloat16), 'hc', [(i, (i + 1) % cores) for...]
  transfers between devices with their start and end apart: 4 -> 5, of which waited for: 3 -> 4; matrix products, arithmetic and copies ran while one was open for 11% -> 13% of each run, Pallas kernels for 15% -> 16%
where the time goes in v11:
time: 296 us; the launch traced here: 295 us
  waiting for transfers between devices  136 us (46%)
  Pallas kernels  47.3 us (16%)
  local copies, waits for them, and re-layouts  34.4 us (12%)
  matrix products  24.6 us (8%)
  other arithmetic  20.4 us (7%)
  between operations  13.5 us (5%)
  blocking collectives  12.1 us (4%)
  starting transfers between devices  7.58 us (3%)
    all_gather x1, waiting for transfers between devices, local(): gathered = lax.all_gather(packed, 'seq', axis=0, tiled=True)  96 us
    pallas_call x1, Pallas kernels, entering_state(): pl.pallas_call(functools.partial(scan_kernel, count, tuple(shifts)), out_...  47.3 us
    reduce_scatter x1, waiting for transfers between devices, local(): lax.psum_scatter(chip_sum, 'hy', scatter_dimension=0, tiled=False)  20.3 us
    all_gather x1, waiting for transfers between devices, local(): w_out_cols = lax.all_gather(jnp.transpose(w_out), 'seq', axis=0, tiled=True)  14.8 us
    psum x1, blocking collectives, local(): total_sq = lax.psum(jnp.sum(gated * gated, axis=1), HEAD)  12.1 us
    reshape x1, local copies, waits for them, and re-layouts, local(): partial_t.reshape(lax.axis_size('hy'), cores, -1, partial_t.shape[1])  11.7 us
    slice x1, local copies, waits for them, and re-layouts, local(): kept = jnp.where(mine == 0, split[:, 0], split[:, 1])  11.2 us
    dot_general x1, matrix products, local(): jnp.dot(extended, gathered, preferred_element_type=jnp.float32)  10.6 us
  transfers between devices with their start and end apart: 5, of which 4 were waited for; matrix products, arithmetic and copies ran while one was open for 13% of the time, Pallas kernels for 16%

profile of v11, /device:TPU:1, one launch (start us, length us, event | category | flops | bytes accessed | tf_op | source)
XLA Modules:
  0.0 295.5 jit_solution(7140369470475641617)
XLA Ops:
  6.5 1.5 fusion.50
  8.1 1.6 pad_maximum_fusion
  10.5 0.9 slice.123
  11.4 4.4 %collective-permute-start = (bf16[3,4096]{1,0:T(4,128)(2,1)S(1)}, bf16[3,4096]{1,0:T(4,128)(2,1)S(1)}, u32[]{:S(2)}, u32[]{:S(2)}) collective-permute-start(bf16[3,4096]{1,0:T(4,128)(2,1)S(1)} %slice.123), channel_id=1, source_target_pairs={{0,8},{8,16},{16,24},{24,32},{32,40},{40,48},{48,56},{56,64},{64,7... | collective-permute-start | bytes 73736 | tf_op jit(solution)/shard_map/ppermute | solution.py:23
  15.8 0.7 fusion.44
  16.5 1.1 reduce-window.16
  17.6 1.1 reduce-window.14
  20.1 0.8 fusion.40
  22.1 0.8 fusion.52
  23.5 0.9 fusion.51
  25.1 0.7 broadcast_in_dim.53
  26.4 96.0 %all-gather.3.cloned.1.call-done = bf16[4096,1280]{1,0:T(8,128)(2,1)} async-done(((bf16[128,1280]{1,0:T(8,128)(2,1)}), bf16[4096,1280]{1,0:T(8,128)(2,1)}) %all-gather.3.cloned.1.call-update) | async-done | bytes 10485776 | tf_op jit(solution)/shard_map/all_gather | solution.py:135
  122.4 10.6 %fusion.5 = bf16[515,1280]{1,0:T(8,128)(2,1)S(1)} fusion(bf16[4096,1280]{1,0:T(8,128)(2,1)} %all-gather.3.cloned.1.call-done, bf16[512,4096]{1,0:T(8,128)(2,1)} %param.12, bf16[3,4096]{1,0:T(4,128)(2,1)S(1)} %collective-permute-done), kind=kOutput, calls=%fused_computation.9 | convolution fusion | flops 5409263616 | bytes 16023040 | tf_op jit(solution)/shard_map/dot_general | solution.py:140
  134.2 0.7 convert_element_type.78
  136.9 1.9 fusion.23
  138.9 1.5 fusion.37.msg_ref
  140.4 1.3 broadcast_in_dim.52.dec_ref
  141.7 47.3 %shard_map.118 = f32[8,64,128]{2,1,0:T(8,128)} custom-call(f32[8,64,128]{2,1,0:T(8,128)} %fusion.37.msg_ref, f32[8,8,128]{2,1,0:T(8,128)} %broadcast_in_dim.52.dec_ref, f32[8,64,128]{2,1,0:T(8,128)} %sin_ref.1), custom_call_target="tpu_custom_call" | custom-call | tf_op jit(solution)/shard_map/pallas_call | solution.py:95
  189.0 1.1 fusion.53
  190.2 2.1 fusion.15
  193.9 2.2 multiply_reduce_fusion
  196.1 14.8 %all-gather.5.cloned.1.call-done = bf16[4096,512]{0,1:T(8,128)(2,1)} async-done(((bf16[128,512]{0,1:T(8,128)(2,1)}), bf16[4096,512]{0,1:T(8,128)(2,1)}) %all-gather.5.cloned.1.call-update) | async-done | bytes 4194320 | tf_op jit(solution)/shard_map/all_gather | solution.py:136
  210.9 7.8 %convolution_bitcast_fusion = f32[4096,512]{0,1:T(8,128)} fusion(bf16[4096,512]{0,1:T(8,128)(2,1)} %all-gather.5.cloned.1.call-done, f32[512,512]{1,0:T(8,128)S(1)} %get-tuple-element.6, f32[512]{0:T(512)S(1)} %copy-done.3), kind=kOutput, calls=%fused_computation | convolution fusion | flops 2148007936 | bytes 13633536 | tf_op jit(solution)/shard_map/dot_general | solution.py:194
  218.6 11.7 %reshape.109 = f32[4,2,512,512]{2,1,0,3:T(2,128)} reshape(f32[4096,512]{0,1:T(8,128)} %convolution_bitcast_fusion) | data formatting | bytes 16777216 | tf_op jit(solution)/shard_map/reshape | solution.py:199
  230.3 11.2 %fusion.48 = (f32[4,1,512,512]{2,1,0,3:T(1,128)S(1)}, f32[4,1,512,512]{2,1,0,3:T(1,128)S(1)}) fusion(f32[4,2,512,512]{2,1,0,3:T(2,128)} %reshape.109), kind=kLoop, calls=%fused_computation.91 | loop fusion | bytes 16777216 | tf_op jit(solution)/shard_map/slice | solution.py:201
  241.5 2.3 fusion.9
  243.9 3.1 %collective-permute-start.1 = (bf16[4,512,512]{1,2,0:T(8,128)(2,1)S(1)}, bf16[4,512,512]{1,2,0:T(8,128)(2,1)S(1)}, u32[]{:S(2)}, u32[]{:S(2)}) collective-permute-start(bf16[4,512,512]{1,2,0:T(8,128)(2,1)S(1)} %fusion.9), channel_id=1, source_target_pairs={{0,1},{1,0},{2,3},{3,2},{4,5},{5,4},{6,7},{7,6},{8,9},{9,8},{10,11... | collective-permute-start | bytes 6291464 | tf_op jit(solution)/shard_map/ppermute | solution.py:202
  247.0 3.8 %collective-permute-done.1 = bf16[4,512,512]{1,2,0:T(8,128)(2,1)S(1)} collective-permute-done((bf16[4,512,512]{1,2,0:T(8,128)(2,1)S(1)}, bf16[4,512,512]{1,2,0:T(8,128)(2,1)S(1)}, u32[]{:S(2)}, u32[]{:S(2)}) %collective-permute-start.1) | collective-permute-done | bytes 2097184 | tf_op jit(solution)/shard_map/ppermute | solution.py:202
  250.8 3.7 %fusion.4 = bf16[4,512,512]{1,2,0:T(8,128)(2,1)} fusion(bf16[4,512,512]{1,2,0:T(8,128)(2,1)S(1)} %collective-permute-done.1, f32[4,1,512,512]{2,1,0,3:T(1,128)S(1)} %get-tuple-element.11, f32[4,1,512,512]{2,1,0,3:T(1,128)S(1)} %get-tuple-element.12, pred[]{:T(512)S(6)} %eq.7), kind=kLoop, calls=%fused_computation.6 | loop fusion | flops 4194304 | bytes 12582913 | tf_op jit(solution)/shard_map/convert_element_type | solution.py:203
  254.5 12.1 %psum.7 = f32[512]{0:T(512)S(1)} all-reduce(f32[512]{0:T(512)S(1)} %get-tuple-element.5), channel_id=1, replica_groups=mesh['seq'=32,'hy'=4,'hc'=2] {'hy','hc'}, use_global_device_ids=true, to_apply=%region_6.7 | all-reduce | flops 512 | bytes 4096 | tf_op jit(solution)/shard_map/psum | solution.py:207
  266.6 20.3 %reduce-scatter.2.cloned.1.call-done = bf16[1,512,512]{1,2,0:T(8,128)(2,1)} async-done(((bf16[4,512,512]{1,2,0:T(8,128)(2,1)}), bf16[1,512,512]{1,2,0:T(8,128)(2,1)}) %reduce-scatter.2.cloned.1.call-update) | async-done | bytes 524304 | tf_op jit(solution)/shard_map/reduce_scatter | solution.py:205
  287.0 2.0 fusion.31
  (68 shorter events, 9.8 us)
Async XLA Ops:
  6.5 115.9 %all-gather.3.cloned.1.call-start = ((), (), s32[]{:S(2)}) async-start(), calls=%async_computation.1 | async-start | bytes 10813440 | tf_op jit(solution)/shard_map/all_gather | solution.py:135
  9.7 201.1 %all-gather.5.cloned.1.call-start = ((), (), s32[]{:S(2)}) async-start(), calls=%async_computation.2 | async-start | bytes 4325376 | tf_op jit(solution)/shard_map/all_gather | solution.py:136
  10.5 276.5 %reduce-scatter.2.cloned.1.call-start = ((), (), s32[]{:S(2)}) async-start(), calls=%async_computation.3 | async-start | bytes 2621440 | tf_op jit(solution)/shard_map/reduce_scatter | solution.py:205
  11.4 15.0 %collective-permute-start = (bf16[3,4096]{1,0:T(4,128)(2,1)S(1)}, bf16[3,4096]{1,0:T(4,128)(2,1)S(1)}, u32[]{:S(2)}, u32[]{:S(2)}) collective-permute-start(bf16[3,4096]{1,0:T(4,128)(2,1)S(1)} %slice.123), channel_id=1, source_target_pairs={{0,8},{8,16},{16,24},{24,32},{32,40},{40,48},{48,56},{56,64},{64,7... | collective-permute-start | bytes 73736 | tf_op jit(solution)/shard_map/ppermute | solution.py:23
  24.4 110.7 %copy-start.5 = (f32[1,512]{1,0:T(1,128)}, f32[1,512]{1,0:T(1,128)S(1)}, u32[]{:S(2)}) copy-start(f32[1,512]{1,0:T(1,128)S(1)} %get-tuple-element.19) | copy-start | bytes 6148
  24.4 110.7 %copy-start.7 = (f32[1,512]{1,0:T(1,128)}, f32[1,512]{1,0:T(1,128)S(1)}, u32[]{:S(2)}) copy-start(f32[1,512]{1,0:T(1,128)S(1)} %get-tuple-element.20) | copy-start | bytes 6148
  24.4 110.7 %copy-start.9 = (f32[1,512]{1,0:T(1,128)}, f32[1,512]{1,0:T(1,128)S(1)}, u32[]{:S(2)}) copy-start(f32[1,512]{1,0:T(1,128)S(1)} %get-tuple-element.21) | copy-start | bytes 6148
  24.4 110.7 %copy-start.11 = (f32[1,512]{1,0:T(1,128)}, f32[1,512]{1,0:T(1,128)S(1)}, u32[]{:S(2)}) copy-start(f32[1,512]{1,0:T(1,128)S(1)} %get-tuple-element.22) | copy-start | bytes 6148
  26.4 106.6 %copy-start.15 = (bf16[3,256]{1,0:T(4,128)(2,1)S(1)}, bf16[3,256]{1,0:T(4,128)(2,1)}, u32[]{:S(2)}) copy-start(bf16[3,256]{1,0:T(4,128)(2,1)} %param.18) | copy-start | bytes 4612
  26.4 108.5 %copy-start.14 = (bf16[3,512]{1,0:T(4,128)(2,1)S(1)}, bf16[3,512]{1,0:T(4,128)(2,1)}, u32[]{:S(2)}) copy-start(bf16[3,512]{1,0:T(4,128)(2,1)} %param.17) | copy-start | bytes 9220
  133.1 2.1 copy-start
  190.2 2.3 copy-start.4
  190.2 2.7 copy-start.1
  190.2 2.7 copy-start.2
  192.3 1.5 copy-start.6
  192.3 1.5 copy-start.8
  192.3 1.5 copy-start.10
  192.4 1.5 copy-start.12
  192.4 1.5 copy-start.13
  193.5 17.4 %copy-start.3 = (f32[512]{0:T(512)S(1)}, f32[512]{0:T(512)}, u32[]{:S(2)}) copy-start(f32[512]{0:T(512)} %param.22) | copy-start | bytes 6148
  243.9 6.9 %collective-permute-start.1 = (bf16[4,512,512]{1,2,0:T(8,128)(2,1)S(1)}, bf16[4,512,512]{1,2,0:T(8,128)(2,1)S(1)}, u32[]{:S(2)}, u32[]{:S(2)}) collective-permute-start(bf16[4,512,512]{1,2,0:T(8,128)(2,1)S(1)} %fusion.9), channel_id=1, source_target_pairs={{0,1},{1,0},{2,3},{3,2},{4,5},{5,4},{6,7},{7,6},{8,9},{9,8},{10,11... | collective-permute-start | bytes 6291464 | tf_op jit(solution)/shard_map/ppermute | solution.py:202
Sparse Core Ops, SparseCore 0:
  9.9 112.4 all-gather.2
  124.9 85.9 all-gather.4
  254.6 32.3 reduce-scatter.1

commit v12 on v10

--- a/solution.py
+++ b/solution.py
@@ -66,9 +66,7 @@
         else:
             acc_s = out_ref[...]
             acc_a = dec_acc[...]
-            rows = acc_s.shape[1]
-            acc_a_rows = jnp.tile(acc_a, (1, rows // acc_a.shape[1], 1))
-            out_ref[...] = jnp.where(me >= d, acc_a_rows * far_s + acc_s, acc_s)
+            out_ref[...] = jnp.where(me >= d, acc_a[:, None, :] * far_s + acc_s, acc_s)
             dec_acc[...] = jnp.where(me >= d, acc_a * far_a, acc_a)
     for copy in copies:
         copy.wait_send()
@@ -77,7 +75,7 @@
 def entering_state(decay, end_state, state_in):
     count = lax.axis_size("seq")
     heads, rows, lanes = end_state.shape
-    decay_rows = jnp.broadcast_to(decay[:, None, None], (heads, 8, lanes))
+    decay_rows = jnp.broadcast_to(decay[:, None], (heads, lanes))
     shifts = [1]
     step = 1
     while step < count:

time: 273 us -> 268 us (0.982)
  Pallas kernels: 41.8 us -> 36.8 us
    pallas_call x1, Pallas kernels: 41.8 us -> 36.8 us  [entering_state(): pl.pallas_call(functools.partial(scan_kernel, count, tuple(shifts)), out_...]
  transfers between devices with their start and end apart: 4 -> 4, of which waited for: 3 -> 3; matrix products, arithmetic and copies ran while one was open for 11% -> 11% of each run, Pallas kernels for 15% -> 14%
where the time goes in v12:
time: 268 us; the launch traced here: 265 us
  waiting for transfers between devices  152 us (57%)
  Pallas kernels  36.8 us (14%)
  matrix products  20.6 us (8%)
  blocking collectives  17.1 us (6%)
  between operations  13.4 us (5%)
  other arithmetic  12.2 us (5%)
  local copies, waits for them, and re-layouts  8.71 us (3%)
  starting transfers between devices  4.45 us (2%)
    all_gather x1, waiting for transfers between devices, local(): gathered = lax.all_gather(packed, 'seq', axis=0, tiled=True)  100 us
    pallas_call x1, Pallas kernels, entering_state(): pl.pallas_call(functools.partial(scan_kernel, count, tuple(shifts)), out_...  36.8 us
    all_gather x1, waiting for transfers between devices, local(): w_out_cols = lax.all_gather(jnp.transpose(w_out), 'seq', axis=0, tiled=True)  27.8 us
    reduce_scatter x1, waiting for transfers between devices, local(): lax.psum_scatter(partial_t.astype(jnp.bfloat16), 'head', scatter_dimensio...  23.1 us
    psum x1, blocking collectives, local(): total_sq = lax.psum(jnp.sum(gated * gated, axis=1), 'head')  17.1 us
    dot_general x1, matrix products, local(): jnp.dot(extended, gathered, preferred_element_type=jnp.float32)  10.6 us
    dot_general x1, matrix products, local(): lax.dot_general(w_out_cols, scaled, (((1,), (1,)), ((), ())), preferred_e...  6.46 us
  transfers between devices with their start and end apart: 4, of which 3 were waited for; matrix products, arithmetic and copies ran while one was open for 11% of the time, Pallas kernels for 14%

profile of v12, /device:TPU:1, one launch (start us, length us, event | category | flops | bytes accessed | tf_op | source)
XLA Modules:
  0.0 264.9 jit_solution(16846280332557773367)
XLA Ops:
  6.5 1.5 fusion.47
  8.1 1.6 pad_maximum_fusion
  9.8 0.7 all-gather.5.cloned.1.call-update
  10.5 0.9 slice.115
  11.4 4.4 %collective-permute-start = (bf16[3,4096]{1,0:T(4,128)(2,1)S(1)}, bf16[3,4096]{1,0:T(4,128)(2,1)S(1)}, u32[]{:S(2)}, u32[]{:S(2)}) collective-permute-start(bf16[3,4096]{1,0:T(4,128)(2,1)S(1)} %slice.115), channel_id=1, source_target_pairs={{0,8},{8,16},{16,24},{24,32},{32,40},{40,48},{48,56},{56,64},{64,7... | collective-permute-start | bytes 73736 | tf_op jit(solution)/shard_map/ppermute | solution.py:16
  15.8 0.7 fusion.42
  16.5 1.1 reduce-window.14
  18.1 1.1 reduce-window.16
  19.7 0.8 fusion.49
  20.6 0.9 fusion.48
  21.5 0.7 broadcast_in_dim.53
  22.4 100.0 %all-gather.3.cloned.1.call-done = bf16[4096,1280]{1,0:T(8,128)(2,1)} async-done(((bf16[128,1280]{1,0:T(8,128)(2,1)}), bf16[4096,1280]{1,0:T(8,128)(2,1)}) %all-gather.3.cloned.1.call-update) | async-done | bytes 10485776 | tf_op jit(solution)/shard_map/all_gather | solution.py:125
  122.4 10.6 %fusion.5 = bf16[515,1280]{1,0:T(8,128)(2,1)S(1)} fusion(bf16[4096,1280]{1,0:T(8,128)(2,1)} %all-gather.3.cloned.1.call-done, bf16[512,4096]{1,0:T(8,128)(2,1)} %param.12, bf16[3,4096]{1,0:T(4,128)(2,1)S(1)} %collective-permute-done), kind=kOutput, calls=%fused_computation.7 | convolution fusion | flops 5409263616 | bytes 16023040 | tf_op jit(solution)/shard_map/dot_general | solution.py:130
  133.2 0.9 copy-done
  134.1 0.6 multiply_convert_fusion.8
  134.8 0.5 reshape.101
  135.3 0.6 copy.31
  135.9 1.1 fusion.34
  137.4 1.0 fusion.22
  138.4 0.8 fusion.35.msg_ref
  139.2 0.7 broadcast_in_dim.52.dec_ref
  139.9 36.8 %shard_map.118 = f32[8,64,128]{2,1,0:T(8,128)} custom-call(f32[8,64,128]{2,1,0:T(8,128)} %fusion.35.msg_ref, f32[8,128]{1,0:T(8,128)} %broadcast_in_dim.52.dec_ref, f32[8,64,128]{2,1,0:T(8,128)} %sin_ref.1), custom_call_target="tpu_custom_call" | custom-call | tf_op jit(solution)/shard_map/pallas_call | solution.py:85
  177.0 1.2 fusion.14
  178.3 0.4 fusion.17
  178.7 0.6 fusion.16
  179.3 0.3 copy.33
  179.7 2.2 multiply_reduce_fusion
  181.9 27.8 %all-gather.5.cloned.1.call-done = bf16[4096,512]{0,1:T(8,128)(2,1)} async-done(((bf16[128,512]{0,1:T(8,128)(2,1)}), bf16[4096,512]{0,1:T(8,128)(2,1)}) %all-gather.5.cloned.1.call-update) | async-done | bytes 4194320 | tf_op jit(solution)/shard_map/all_gather | solution.py:126
  209.7 6.5 %fusion = bf16[4096,512]{0,1:T(8,128)(2,1)} fusion(bf16[4096,512]{0,1:T(8,128)(2,1)} %all-gather.5.cloned.1.call-done, f32[512,512]{1,0:T(8,128)S(1)} %get-tuple-element.6, f32[512]{0:T(512)S(1)} %copy-done.4), kind=kOutput, calls=%fused_computation.1 | convolution fusion | flops 2150105088 | bytes 9439232 | tf_op jit(solution)/shard_map/dot_general | solution.py:184
  216.2 17.1 %psum.7 = f32[512]{0:T(512)S(1)} all-reduce(f32[512]{0:T(512)S(1)} %get-tuple-element.5), channel_id=1, replica_groups=mesh['seq'=32,'head'=8] {'head'}, use_global_device_ids=true, to_apply=%region_6.7 | all-reduce | flops 512 | bytes 4096 | tf_op jit(solution)/shard_map/psum | solution.py:190
  233.3 23.1 %reduce-scatter.2.cloned.1.call-done = bf16[512,512]{0,1:T(8,128)(2,1)} async-done(((bf16[4096,512]{0,1:T(8,128)(2,1)}), bf16[512,512]{0,1:T(8,128)(2,1)}) %reduce-scatter.2.cloned.1.call-update) | async-done | bytes 524304 | tf_op jit(solution)/shard_map/reduce_scatter | solution.py:188
  256.3 2.0 fusion.29
  (40 shorter events, 2.1 us)
Async XLA Ops:
  6.5 115.9 %all-gather.3.cloned.1.call-start = ((), (), s32[]{:S(2)}) async-start(), calls=%async_computation.1 | async-start | bytes 10813440 | tf_op jit(solution)/shard_map/all_gather | solution.py:125
  9.7 200.0 %all-gather.5.cloned.1.call-start = ((), (), s32[]{:S(2)}) async-start(), calls=%async_computation.2 | async-start | bytes 4325376 | tf_op jit(solution)/shard_map/all_gather | solution.py:126
  10.5 245.9 %reduce-scatter.2.cloned.1.call-start = ((), (), s32[]{:S(2)}) async-start(), calls=%async_computation.3 | async-start | bytes 4718592 | tf_op jit(solution)/shard_map/reduce_scatter | solution.py:188
  11.4 11.0 %collective-permute-start = (bf16[3,4096]{1,0:T(4,128)(2,1)S(1)}, bf16[3,4096]{1,0:T(4,128)(2,1)S(1)}, u32[]{:S(2)}, u32[]{:S(2)}) collective-permute-start(bf16[3,4096]{1,0:T(4,128)(2,1)S(1)} %slice.115), channel_id=1, source_target_pairs={{0,8},{8,16},{16,24},{24,32},{32,40},{40,48},{48,56},{56,64},{64,7... | collective-permute-start | bytes 73736 | tf_op jit(solution)/shard_map/ppermute | solution.py:16
  22.3 110.7 %copy-start.2 = (bf16[3,512]{1,0:T(4,128)(2,1)S(1)}, bf16[3,512]{1,0:T(4,128)(2,1)}, u32[]{:S(2)}) copy-start(bf16[3,512]{1,0:T(4,128)(2,1)} %param.17) | copy-start | bytes 9220
  133.1 1.1 copy-start
  133.2 2.7 %copy-start.3 = (bf16[3,256]{1,0:T(4,128)(2,1)S(1)}, bf16[3,256]{1,0:T(4,128)(2,1)}, u32[]{:S(2)}) copy-start(bf16[3,256]{1,0:T(4,128)(2,1)} %param.18) | copy-start | bytes 4612
  177.0 1.7 copy-start.1
  179.3 30.4 %copy-start.4 = (f32[512]{0:T(512)S(1)}, f32[512]{0:T(512)}, u32[]{:S(2)}) copy-start(f32[512]{0:T(512)} %param.22) | copy-start | bytes 6148
Sparse Core Ops, SparseCore 0:
  9.9 112.4 all-gather.2
  124.9 84.7 all-gather.4
  216.3 39.9 reduce-scatter.1

commit v13 on v12

--- a/solution.py
+++ b/solution.py
@@ -43,6 +43,8 @@
             s_send[k] = out_ref[...].astype(s_send.dtype)
             a_send[k] = dec_acc[...]
         target = ((me + d) % count, hd)
+        sends = 1 - (me + d) // count
+        receives = (me - d + count) // count
         pair = []
         for index, (src, dst) in enumerate(((s_send, s_recv), (a_send, a_recv))):
             copy = pltpu.make_async_remote_copy(
@@ -53,11 +55,11 @@
                 device_id=target,
                 device_id_type=pl.DeviceIdType.MESH,
             )
-            copy.start()
+            pl.when(sends == 1)(copy.start)
             pair.append(copy)
-        copies.extend(pair)
+        copies.append((sends, pair))
         for copy in pair:
-            copy.wait_recv()
+            pl.when(receives == 1)(copy.wait_recv)
         far_s = s_recv[k].astype(jnp.float32)
         far_a = a_recv[k]
         if k == 0:
@@ -68,8 +70,9 @@
             acc_a = dec_acc[...]
             out_ref[...] = jnp.where(me >= d, acc_a[:, None, :] * far_s + acc_s, acc_s)
             dec_acc[...] = jnp.where(me >= d, acc_a * far_a, acc_a)
-    for copy in copies:
-        copy.wait_send()
+    for sends, pair in copies:
+        for copy in pair:
+            pl.when(sends == 1)(copy.wait_send)
 
 
 def entering_state(decay, end_state, state_in):

time: 268 us -> 268 us (level)
  waiting for transfers between devices: 152 us -> 170 us
  Pallas kernels: 36.8 us -> 20.1 us
    pallas_call x1, Pallas kernels: 36.8 us -> 20.1 us  [entering_state(): pl.pallas_call(functools.partial(scan_kernel, count, tuple(shifts)), out_...]
    all_gather x1, waiting for transfers between devices: 27.8 us -> 43.7 us  [local(): w_out_cols = lax.all_gather(jnp.transpose(w_out), 'seq', axis=0, tiled=True)]
  transfers between devices with their start and end apart: 4 -> 4, of which waited for: 3 -> 3; matrix products, arithmetic and copies ran while one was open for 11% -> 11% of each run, Pallas kernels for 14% -> 8%
where the time goes in v13:
time: 268 us; the launch traced here: 265 us
  waiting for transfers between devices  170 us (63%)
  matrix products  20.6 us (8%)
  Pallas kernels  20.1 us (8%)
  blocking collectives  15.6 us (6%)
  between operations  13.4 us (5%)
  other arithmetic  12.2 us (5%)
  local copies, waits for them, and re-layouts  8.71 us (3%)
  starting transfers between devices  4.45 us (2%)
    all_gather x1, waiting for transfers between devices, local(): gathered = lax.all_gather(packed, 'seq', axis=0, tiled=True)  100 us
    all_gather x1, waiting for transfers between devices, local(): w_out_cols = lax.all_gather(jnp.transpose(w_out), 'seq', axis=0, tiled=True)  43.7 us
    reduce_scatter x1, waiting for transfers between devices, local(): lax.psum_scatter(partial_t.astype(jnp.bfloat16), 'head', scatter_dimensio...  25.4 us
    pallas_call x1, Pallas kernels, entering_state(): pl.pallas_call(functools.partial(scan_kernel, count, tuple(shifts)), out_...  20.1 us
    psum x1, blocking collectives, local(): total_sq = lax.psum(jnp.sum(gated * gated, axis=1), 'head')  15.6 us
    dot_general x1, matrix products, local(): jnp.dot(extended, gathered, preferred_element_type=jnp.float32)  10.6 us
    dot_general x1, matrix products, local(): lax.dot_general(w_out_cols, scaled, (((1,), (1,)), ((), ())), preferred_e...  6.46 us
  transfers between devices with their start and end apart: 4, of which 3 were waited for; matrix products, arithmetic and copies ran while one was open for 11% of the time, Pallas kernels for 8%

profile of v13, /device:TPU:1, one launch (start us, length us, event | category | flops | bytes accessed | tf_op | source)
XLA Modules:
  0.0 264.9 jit_solution(13696582417697499416)
XLA Ops:
  6.5 1.5 fusion.47
  8.1 1.6 pad_maximum_fusion
  9.8 0.7 all-gather.5.cloned.1.call-update
  10.5 0.9 slice.115
  11.4 4.4 %collective-permute-start = (bf16[3,4096]{1,0:T(4,128)(2,1)S(1)}, bf16[3,4096]{1,0:T(4,128)(2,1)S(1)}, u32[]{:S(2)}, u32[]{:S(2)}) collective-permute-start(bf16[3,4096]{1,0:T(4,128)(2,1)S(1)} %slice.115), channel_id=1, source_target_pairs={{0,8},{8,16},{16,24},{24,32},{32,40},{40,48},{48,56},{56,64},{64,7... | collective-permute-start | bytes 73736 | tf_op jit(solution)/shard_map/ppermute | solution.py:16
  15.8 0.7 fusion.42
  16.5 1.1 reduce-window.14
  18.1 1.1 reduce-window.16
  19.7 0.8 fusion.49
  20.6 0.9 fusion.48
  21.5 0.7 broadcast_in_dim.53
  22.4 100.0 %all-gather.3.cloned.1.call-done = bf16[4096,1280]{1,0:T(8,128)(2,1)} async-done(((bf16[128,1280]{1,0:T(8,128)(2,1)}), bf16[4096,1280]{1,0:T(8,128)(2,1)}) %all-gather.3.cloned.1.call-update) | async-done | bytes 10485776 | tf_op jit(solution)/shard_map/all_gather | solution.py:128
  122.4 10.6 %fusion.5 = bf16[515,1280]{1,0:T(8,128)(2,1)S(1)} fusion(bf16[4096,1280]{1,0:T(8,128)(2,1)} %all-gather.3.cloned.1.call-done, bf16[512,4096]{1,0:T(8,128)(2,1)} %param.12, bf16[3,4096]{1,0:T(4,128)(2,1)S(1)} %collective-permute-done), kind=kOutput, calls=%fused_computation.7 | convolution fusion | flops 5409263616 | bytes 16023040 | tf_op jit(solution)/shard_map/dot_general | solution.py:133
  133.2 0.9 copy-done
  134.1 0.6 multiply_convert_fusion.8
  134.8 0.5 reshape.101
  135.3 0.6 copy.31
  135.9 1.1 fusion.34
  137.4 1.0 fusion.22
  138.4 0.8 fusion.35.msg_ref
  139.2 0.7 broadcast_in_dim.52.dec_ref
  139.9 20.1 %shard_map.118 = f32[8,64,128]{2,1,0:T(8,128)} custom-call(f32[8,64,128]{2,1,0:T(8,128)} %fusion.35.msg_ref, f32[8,128]{1,0:T(8,128)} %broadcast_in_dim.52.dec_ref, f32[8,64,128]{2,1,0:T(8,128)} %sin_ref.1), custom_call_target="tpu_custom_call" | custom-call | tf_op jit(solution)/shard_map/pallas_call | solution.py:88
  160.2 1.2 fusion.14
  161.5 0.4 fusion.17
  161.9 0.6 fusion.16
  162.6 0.3 copy.33
  162.9 2.2 multiply_reduce_fusion
  165.1 43.7 %all-gather.5.cloned.1.call-done = bf16[4096,512]{0,1:T(8,128)(2,1)} async-done(((bf16[128,512]{0,1:T(8,128)(2,1)}), bf16[4096,512]{0,1:T(8,128)(2,1)}) %all-gather.5.cloned.1.call-update) | async-done | bytes 4194320 | tf_op jit(solution)/shard_map/all_gather | solution.py:129
  208.8 6.5 %fusion = bf16[4096,512]{0,1:T(8,128)(2,1)} fusion(bf16[4096,512]{0,1:T(8,128)(2,1)} %all-gather.5.cloned.1.call-done, f32[512,512]{1,0:T(8,128)S(1)} %get-tuple-element.6, f32[512]{0:T(512)S(1)} %copy-done.4), kind=kOutput, calls=%fused_computation.1 | convolution fusion | flops 2150105088 | bytes 9439232 | tf_op jit(solution)/shard_map/dot_general | solution.py:187
  215.3 15.6 %psum.7 = f32[512]{0:T(512)S(1)} all-reduce(f32[512]{0:T(512)S(1)} %get-tuple-element.5), channel_id=1, replica_groups=mesh['seq'=32,'head'=8] {'head'}, use_global_device_ids=true, to_apply=%region_6.7 | all-reduce | flops 512 | bytes 4096 | tf_op jit(solution)/shard_map/psum | solution.py:193
  231.0 25.4 %reduce-scatter.2.cloned.1.call-done = bf16[512,512]{0,1:T(8,128)(2,1)} async-done(((bf16[4096,512]{0,1:T(8,128)(2,1)}), bf16[512,512]{0,1:T(8,128)(2,1)}) %reduce-scatter.2.cloned.1.call-update) | async-done | bytes 524304 | tf_op jit(solution)/shard_map/reduce_scatter | solution.py:191
  256.3 2.0 fusion.29
  (40 shorter events, 2.1 us)
Async XLA Ops:
  6.5 115.9 %all-gather.3.cloned.1.call-start = ((), (), s32[]{:S(2)}) async-start(), calls=%async_computation.1 | async-start | bytes 10813440 | tf_op jit(solution)/shard_map/all_gather | solution.py:128
  9.7 199.1 %all-gather.5.cloned.1.call-start = ((), (), s32[]{:S(2)}) async-start(), calls=%async_computation.2 | async-start | bytes 4325376 | tf_op jit(solution)/shard_map/all_gather | solution.py:129
  10.5 245.9 %reduce-scatter.2.cloned.1.call-start = ((), (), s32[]{:S(2)}) async-start(), calls=%async_computation.3 | async-start | bytes 4718592 | tf_op jit(solution)/shard_map/reduce_scatter | solution.py:191
  11.4 11.0 %collective-permute-start = (bf16[3,4096]{1,0:T(4,128)(2,1)S(1)}, bf16[3,4096]{1,0:T(4,128)(2,1)S(1)}, u32[]{:S(2)}, u32[]{:S(2)}) collective-permute-start(bf16[3,4096]{1,0:T(4,128)(2,1)S(1)} %slice.115), channel_id=1, source_target_pairs={{0,8},{8,16},{16,24},{24,32},{32,40},{40,48},{48,56},{56,64},{64,7... | collective-permute-start | bytes 73736 | tf_op jit(solution)/shard_map/ppermute | solution.py:16
  22.3 110.7 %copy-start.2 = (bf16[3,512]{1,0:T(4,128)(2,1)S(1)}, bf16[3,512]{1,0:T(4,128)(2,1)}, u32[]{:S(2)}) copy-start(bf16[3,512]{1,0:T(4,128)(2,1)} %param.17) | copy-start | bytes 9220
  133.1 1.1 copy-start
  133.2 2.7 %copy-start.3 = (bf16[3,256]{1,0:T(4,128)(2,1)S(1)}, bf16[3,256]{1,0:T(4,128)(2,1)}, u32[]{:S(2)}) copy-start(bf16[3,256]{1,0:T(4,128)(2,1)} %param.18) | copy-start | bytes 4612
  160.2 1.7 copy-start.1
  162.6 46.3 %copy-start.4 = (f32[512]{0:T(512)S(1)}, f32[512]{0:T(512)}, u32[]{:S(2)}) copy-start(f32[512]{0:T(512)} %param.22) | copy-start | bytes 6148
Sparse Core Ops, SparseCore 0:
  9.9 112.4 all-gather.2
  124.9 83.9 all-gather.4
  215.4 40.8 reduce-scatter.1

commit v14 on v13

--- a/solution.py
+++ b/solution.py
@@ -124,16 +124,27 @@
     first = lax.axis_index("seq") == 0
     w_x = w_xz[:, 0, :]
     w_z = w_xz[:, 1, :]
-    packed = jnp.concatenate([w_x, w_z, w_bc], axis=1)
+    core = lax.axis_index("head") % 2
+    half = w_bc.shape[1] // 2
+    w_half = jnp.where(core == 0, w_bc[:, :half], w_bc[:, half:])
+    packed = jnp.concatenate([w_x, w_z, w_half], axis=1)
     gathered = lax.all_gather(packed, "seq", axis=0, tiled=True)
     w_out_cols = lax.all_gather(jnp.transpose(w_out), "seq", axis=0, tiled=True)
     lag = conv_x.shape[0] - 1
     earlier = passed_along(tokens[rows - lag :], "seq", 1)
     extended = jnp.concatenate([earlier, tokens], axis=0)
     xzbc = jnp.dot(extended, gathered, preferred_element_type=jnp.float32).astype(jnp.bfloat16)
+    own_half = xzbc[:, 2 * inner :]
+    heads_count = lax.axis_size("head")
+    other_half = lax.ppermute(own_half, "head", [(i, i ^ 1) for i in range(heads_count)])
+    bc_all = jnp.where(
+        core == 0,
+        jnp.concatenate([own_half, other_half], axis=1),
+        jnp.concatenate([other_half, own_half], axis=1),
+    )
     opening = lax.broadcasted_iota(jnp.int32, (rows + lag, 1), 0) < lag
     whole_x = jnp.where(first & opening, jnp.pad(tail_x, ((0, rows), (0, 0))), xzbc[:, :inner])
-    whole_bc = jnp.where(first & opening, jnp.pad(tail_bc, ((0, rows), (0, 0))), xzbc[:, 2 * inner :])
+    whole_bc = jnp.where(first & opening, jnp.pad(tail_bc, ((0, rows), (0, 0))), bc_all)
     z_val = xzbc[lag:, inner : 2 * inner]
     x_conv = depthwise(whole_x, conv_x)
     bc_conv = depthwise(whole_bc, conv_bc)

time: 268 us -> 263 us (0.981)
  waiting for transfers between devices: 170 us -> 167 us
    all_gather x1, waiting for transfers between devices: 100 us -> 94.6 us  [local(): gathered = lax.all_gather(packed, 'seq', axis=0, tiled=True)]
  transfers between devices with their start and end apart: 4 -> 5, of which waited for: 3 -> 3; matrix products, arithmetic and copies ran while one was open for 11% -> 11% of each run, Pallas kernels for 8% -> 8%
where the time goes in v14:
time: 263 us; the launch traced here: 260 us
  waiting for transfers between devices  167 us (63%)
  matrix products  20.3 us (8%)
  Pallas kernels  20.3 us (8%)
  blocking collectives  15.1 us (6%)
  between operations  13.4 us (5%)
  other arithmetic  11.2 us (4%)
  local copies, waits for them, and re-layouts  7.84 us (3%)
  starting transfers between devices  5.81 us (2%)
    all_gather x1, waiting for transfers between devices, local(): gathered = lax.all_gather(packed, 'seq', axis=0, tiled=True)  94.6 us
    all_gather x1, waiting for transfers between devices, local(): w_out_cols = lax.all_gather(jnp.transpose(w_out), 'seq', axis=0, tiled=True)  45.8 us
    reduce_scatter x1, waiting for transfers between devices, local(): lax.psum_scatter(partial_t.astype(jnp.bfloat16), 'head', scatter_dimensio...  25.6 us
    pallas_call x1, Pallas kernels, entering_state(): pl.pallas_call(functools.partial(scan_kernel, count, tuple(shifts)), out_...  20.3 us
    psum x1, blocking collectives, local(): total_sq = lax.psum(jnp.sum(gated * gated, axis=1), 'head')  15.1 us
    dot_general x1, matrix products, local(): jnp.dot(extended, gathered, preferred_element_type=jnp.float32)  10.3 us
    dot_general x1, matrix products, local(): lax.dot_general(w_out_cols, scaled, (((1,), (1,)), ((), ())), preferred_e...  6.46 us
  transfers between devices with their start and end apart: 5, of which 3 were waited for; matrix products, arithmetic and copies ran while one was open for 11% of the time, Pallas kernels for 8%

profile of v14, /device:TPU:1, one launch (start us, length us, event | category | flops | bytes accessed | tf_op | source)
XLA Modules:
  0.0 260.5 jit_solution(16861586125331618612)
XLA Ops:
  6.5 1.5 fusion.48
  8.1 0.8 slice_select_fusion.1
  8.9 0.7 pad_maximum_fusion
  9.7 0.7 all-gather.5.cloned.1.call-update
  10.5 0.9 slice.121
  11.3 4.4 %collective-permute-start = (bf16[3,4096]{1,0:T(4,128)(2,1)S(1)}, bf16[3,4096]{1,0:T(4,128)(2,1)S(1)}, u32[]{:S(2)}, u32[]{:S(2)}) collective-permute-start(bf16[3,4096]{1,0:T(4,128)(2,1)S(1)} %slice.121), channel_id=1, source_target_pairs={{0,8},{8,16},{16,24},{24,32},{32,40},{40,48},{48,56},{56,64},{64,7... | collective-permute-start | bytes 73736 | tf_op jit(solution)/shard_map/ppermute | solution.py:16
  15.7 0.7 fusion.43
  16.4 1.1 reduce-window.14
  18.0 1.1 reduce-window.16
  19.7 0.8 fusion.50
  20.5 0.9 fusion.49
  21.5 0.7 broadcast_in_dim.53
  22.3 94.6 %all-gather.3.cloned.1.call-done = bf16[4096,1152]{1,0:T(8,128)(2,1)} async-done(((bf16[128,1152]{1,0:T(8,128)(2,1)}), bf16[4096,1152]{1,0:T(8,128)(2,1)}) %all-gather.3.cloned.1.call-update) | async-done | bytes 9437200 | tf_op jit(solution)/shard_map/all_gather | solution.py:131
  116.8 10.3 %fusion.5 = bf16[515,1152]{1,0:T(8,128)(2,1)S(1)} fusion(bf16[4096,1152]{1,0:T(8,128)(2,1)} %all-gather.3.cloned.1.call-done, bf16[512,4096]{1,0:T(8,128)(2,1)} %param.12, bf16[3,4096]{1,0:T(4,128)(2,1)S(1)} %collective-permute-done), kind=kOutput, calls=%fused_computation.7 | convolution fusion | flops 4869180928 | bytes 14842624 | tf_op jit(solution)/shard_map/dot_general | solution.py:136
  127.2 1.4 collective-permute-start.1
  128.7 0.6 multiply_convert_fusion.8
  129.4 0.5 reshape.101
  129.9 0.6 copy.31
  131.1 1.0 fusion.22
  132.1 0.8 fusion.36.msg_ref
  132.9 0.7 broadcast_in_dim.52.dec_ref
  133.6 20.3 %shard_map.118 = f32[8,64,128]{2,1,0:T(8,128)} custom-call(f32[8,64,128]{2,1,0:T(8,128)} %fusion.36.msg_ref, f32[8,128]{1,0:T(8,128)} %broadcast_in_dim.52.dec_ref, f32[8,64,128]{2,1,0:T(8,128)} %sin_ref.1), custom_call_target="tpu_custom_call" | custom-call | tf_op jit(solution)/shard_map/pallas_call | solution.py:88
  154.1 1.2 fusion.14
  155.4 0.4 fusion.17
  155.8 0.6 fusion.16
  156.5 0.3 copy.33
  156.8 2.2 multiply_reduce_fusion
  159.0 45.8 %all-gather.5.cloned.1.call-done = bf16[4096,512]{0,1:T(8,128)(2,1)} async-done(((bf16[128,512]{0,1:T(8,128)(2,1)}), bf16[4096,512]{0,1:T(8,128)(2,1)}) %all-gather.5.cloned.1.call-update) | async-done | bytes 4194320 | tf_op jit(solution)/shard_map/all_gather | solution.py:132
  204.8 6.5 %fusion = bf16[4096,512]{0,1:T(8,128)(2,1)} fusion(bf16[4096,512]{0,1:T(8,128)(2,1)} %all-gather.5.cloned.1.call-done, f32[512,512]{1,0:T(8,128)S(1)} %get-tuple-element.6, f32[512]{0:T(512)S(1)} %copy-done.4), kind=kOutput, calls=%fused_computation.1 | convolution fusion | flops 2150105088 | bytes 9439232 | tf_op jit(solution)/shard_map/dot_general | solution.py:198
  211.3 15.1 %psum.7 = f32[512]{0:T(512)S(1)} all-reduce(f32[512]{0:T(512)S(1)} %get-tuple-element.5), channel_id=1, replica_groups=mesh['seq'=32,'head'=8] {'head'}, use_global_device_ids=true, to_apply=%region_6.7 | all-reduce | flops 512 | bytes 4096 | tf_op jit(solution)/shard_map/psum | solution.py:204
  226.4 25.6 %reduce-scatter.2.cloned.1.call-done = bf16[512,512]{0,1:T(8,128)(2,1)} async-done(((bf16[4096,512]{0,1:T(8,128)(2,1)}), bf16[512,512]{0,1:T(8,128)(2,1)}) %reduce-scatter.2.cloned.1.call-update) | async-done | bytes 524304 | tf_op jit(solution)/shard_map/reduce_scatter | solution.py:202
  252.0 2.0 fusion.29
  (44 shorter events, 2.2 us)
Async XLA Ops:
  6.5 110.3 %all-gather.3.cloned.1.call-start = ((), (), s32[]{:S(2)}) async-start(), calls=%async_computation.1 | async-start | bytes 9732096 | tf_op jit(solution)/shard_map/all_gather | solution.py:131
  9.7 195.1 %all-gather.5.cloned.1.call-start = ((), (), s32[]{:S(2)}) async-start(), calls=%async_computation.2 | async-start | bytes 4325376 | tf_op jit(solution)/shard_map/all_gather | solution.py:132
  10.4 241.6 %reduce-scatter.2.cloned.1.call-start = ((), (), s32[]{:S(2)}) async-start(), calls=%async_computation.3 | async-start | bytes 4718592 | tf_op jit(solution)/shard_map/reduce_scatter | solution.py:202
  11.3 11.0 %collective-permute-start = (bf16[3,4096]{1,0:T(4,128)(2,1)S(1)}, bf16[3,4096]{1,0:T(4,128)(2,1)S(1)}, u32[]{:S(2)}, u32[]{:S(2)}) collective-permute-start(bf16[3,4096]{1,0:T(4,128)(2,1)S(1)} %slice.121), channel_id=1, source_target_pairs={{0,8},{8,16},{16,24},{24,32},{32,40},{40,48},{48,56},{56,64},{64,7... | collective-permute-start | bytes 73736 | tf_op jit(solution)/shard_map/ppermute | solution.py:16
  22.3 106.3 %copy-start.2 = (bf16[3,512]{1,0:T(4,128)(2,1)S(1)}, bf16[3,512]{1,0:T(4,128)(2,1)}, u32[]{:S(2)}) copy-start(bf16[3,512]{1,0:T(4,128)(2,1)} %param.17) | copy-start | bytes 9220
  127.2 1.6 copy-start
  127.2 3.3 %collective-permute-start.1 = (bf16[515,128]{1,0:T(8,128)(2,1)S(1)}, bf16[515,128]{1,0:T(8,128)(2,1)S(1)}, u32[]{:S(2)}, u32[]{:S(2)}) collective-permute-start(bf16[515,128]{1,0:T(8,128)(2,1)S(1)} %slice.166), channel_id=1, source_target_pairs={{0,1},{1,0},{2,3},{3,2},{4,5},{5,4},{6,7},{7,6},{8,9},{9,8},{10,11... | collective-permute-start | bytes 395528 | tf_op jit(solution)/shard_map/ppermute | solution.py:139
  128.7 1.8 copy-start.3
  154.1 1.7 copy-start.1
  156.4 48.3 %copy-start.4 = (f32[512]{0:T(512)S(1)}, f32[512]{0:T(512)}, u32[]{:S(2)}) copy-start(f32[512]{0:T(512)} %param.22) | copy-start | bytes 6148
Sparse Core Ops, SparseCore 0:
  9.9 106.8 all-gather.2
  119.3 85.4 all-gather.4
  211.4 40.5 reduce-scatter.1

commit v15 on v13

--- a/solution.py
+++ b/solution.py
@@ -124,16 +124,39 @@
     first = lax.axis_index("seq") == 0
     w_x = w_xz[:, 0, :]
     w_z = w_xz[:, 1, :]
-    packed = jnp.concatenate([w_x, w_z, w_bc], axis=1)
+    heads_count = lax.axis_size("head")
+    hindex = lax.axis_index("head")
+    core = hindex % 2
+    chip = hindex // 2
+    chips = heads_count // 2
+    width = w_bc.shape[1] // heads_count
+    w_half = lax.dynamic_slice_in_dim(w_bc, hindex * width, width, axis=1)
+    packed = jnp.concatenate([w_x, w_z, w_half], axis=1)
     gathered = lax.all_gather(packed, "seq", axis=0, tiled=True)
     w_out_cols = lax.all_gather(jnp.transpose(w_out), "seq", axis=0, tiled=True)
     lag = conv_x.shape[0] - 1
     earlier = passed_along(tokens[rows - lag :], "seq", 1)
     extended = jnp.concatenate([earlier, tokens], axis=0)
     xzbc = jnp.dot(extended, gathered, preferred_element_type=jnp.float32).astype(jnp.bfloat16)
+    own_part = xzbc[:, 2 * inner :]
+    other_part = lax.ppermute(own_part, "head", [(i, i ^ 1) for i in range(heads_count)])
+    chip_piece = jnp.where(
+        core == 0,
+        jnp.concatenate([own_part, other_part], axis=1),
+        jnp.concatenate([other_part, own_part], axis=1),
+    )
+    received = [chip_piece] + [
+        lax.ppermute(chip_piece, "head", [(i, (i + 2 * k) % heads_count) for i in range(heads_count)])
+        for k in range(1, chips)
+    ]
+    stacked = jnp.stack(received)
+    bc_all = jnp.concatenate(
+        [lax.dynamic_index_in_dim(stacked, (chip - j + chips) % chips, keepdims=False) for j in range(chips)],
+        axis=1,
+    )
     opening = lax.broadcasted_iota(jnp.int32, (rows + lag, 1), 0) < lag
     whole_x = jnp.where(first & opening, jnp.pad(tail_x, ((0, rows), (0, 0))), xzbc[:, :inner])
-    whole_bc = jnp.where(first & opening, jnp.pad(tail_bc, ((0, rows), (0, 0))), xzbc[:, 2 * inner :])
+    whole_bc = jnp.where(first & opening, jnp.pad(tail_bc, ((0, rows), (0, 0))), bc_all)
     z_val = xzbc[lag:, inner : 2 * inner]
     x_conv = depthwise(whole_x, conv_x)
     bc_conv = depthwise(whole_bc, conv_bc)

time: 268 us -> 262 us (0.978)
  waiting for transfers between devices: 170 us -> 161 us
  starting transfers between devices: 4.45 us -> 10.5 us
    all_gather x1, waiting for transfers between devices: 43.7 us -> 35.1 us  [local(): w_out_cols = lax.all_gather(jnp.transpose(w_out), 'seq', axis=0, tiled=True)]
    ppermute x0 -> x4, starting transfers between devices: none -> 6.06 us  [the longest x3 4.88 us: local(): lax.ppermute(chip_piece, 'head', [(i, (i + 2 * k) % heads_count) for i in...]
    ppermute x0 -> x4, waiting for transfers between devices: none -> 4.43 us  [the longest x3 4.43 us: local(): lax.ppermute(chip_piece, 'head', [(i, (i + 2 * k) % heads_count) for i in...]
    all_gather x1, waiting for transfers between devices: 100 us -> 95.8 us  [local(): gathered = lax.all_gather(packed, 'seq', axis=0, tiled=True)]
  transfers between devices with their start and end apart: 4 -> 8, of which waited for: 3 -> 5; matrix products, arithmetic and copies ran while one was open for 11% -> 11% of each run, Pallas kernels for 8% -> 7%
where the time goes in v15:
time: 262 us; the launch traced here: 259 us
  waiting for transfers between devices  161 us (61%)
  matrix products  20.3 us (8%)
  Pallas kernels  19 us (7%)
  blocking collectives  15.4 us (6%)
  between operations  13.5 us (5%)
  other arithmetic  10.9 us (4%)
  starting transfers between devices  10.5 us (4%)
  local copies, waits for them, and re-layouts  7.99 us (3%)
    all_gather x1, waiting for transfers between devices, local(): gathered = lax.all_gather(packed, 'seq', axis=0, tiled=True)  95.8 us
    all_gather x1, waiting for transfers between devices, local(): w_out_cols = lax.all_gather(jnp.transpose(w_out), 'seq', axis=0, tiled=True)  35.1 us
    reduce_scatter x1, waiting for transfers between devices, local(): lax.psum_scatter(partial_t.astype(jnp.bfloat16), 'head', scatter_dimensio...  25.9 us
    pallas_call x1, Pallas kernels, entering_state(): pl.pallas_call(functools.partial(scan_kernel, count, tuple(shifts)), out_...  19 us
    psum x1, blocking collectives, local(): total_sq = lax.psum(jnp.sum(gated * gated, axis=1), 'head')  15.4 us
    dot_general x1, matrix products, local(): jnp.dot(extended, gathered, preferred_element_type=jnp.float32)  10.3 us
    dot_general x1, matrix products, local(): lax.dot_general(w_out_cols, scaled, (((1,), (1,)), ((), ())), preferred_e...  6.47 us
  transfers between devices with their start and end apart: 8, of which 5 were waited for; matrix products, arithmetic and copies ran while one was open for 11% of the time, Pallas kernels for 7%

profile of v15, /device:TPU:1, one launch (start us, length us, event | category | flops | bytes accessed | tf_op | source)
XLA Modules:
  0.0 259.0 jit_solution(14426033000308074229)
XLA Ops:
  6.5 1.5 fusion.47
  8.2 0.7 pad_maximum_fusion.1
  9.0 0.9 slice.115
  9.9 4.4 %collective-permute-start = (bf16[3,4096]{1,0:T(4,128)(2,1)S(1)}, bf16[3,4096]{1,0:T(4,128)(2,1)S(1)}, u32[]{:S(2)}, u32[]{:S(2)}) collective-permute-start(bf16[3,4096]{1,0:T(4,128)(2,1)S(1)} %slice.115), channel_id=1, source_target_pairs={{0,8},{8,16},{16,24},{24,32},{32,40},{40,48},{48,56},{56,64},{64,7... | collective-permute-start | bytes 73736 | tf_op jit(solution)/shard_map/ppermute | solution.py:16
  14.4 0.7 fusion.42
  15.1 1.1 reduce-window.14
  16.7 1.1 reduce-window.16
  18.3 0.8 fusion.49
  19.2 0.9 fusion.48
  20.2 0.7 broadcast_in_dim.53
  21.0 95.8 %all-gather.3.cloned.1.call-done = bf16[4096,1056]{1,0:T(8,128)(2,1)} async-done(((bf16[128,1056]{1,0:T(8,128)(2,1)}), bf16[4096,1056]{1,0:T(8,128)(2,1)}) %all-gather.3.cloned.1.call-update) | async-done | bytes 8650768 | tf_op jit(solution)/shard_map/all_gather | solution.py:135
  116.8 10.3 %fusion.5 = bf16[515,1056]{1,0:T(8,128)(2,1)S(1)} fusion(bf16[4096,1056]{1,0:T(8,128)(2,1)} %all-gather.3.cloned.1.call-done, bf16[512,4096]{1,0:T(8,128)(2,1)} %param.12, bf16[3,4096]{1,0:T(4,128)(2,1)S(1)} %collective-permute-done), kind=kOutput, calls=%fused_computation.7 | convolution fusion | flops 4464118784 | bytes 13957312 | tf_op jit(solution)/shard_map/dot_general | solution.py:140
  127.2 1.2 collective-permute-start.1
  128.6 0.6 multiply_convert_fusion.8
  129.8 0.6 copy.31
  130.5 1.3 collective-permute-start.2
  131.8 2.4 collective-permute-start.3
  134.3 1.2 collective-permute-start.4
  135.6 0.6 collective-permute-done.2
  136.2 3.8 %collective-permute-done.3 = bf16[515,64]{1,0:T(8,128)(2,1)S(1)} collective-permute-done((bf16[515,64]{1,0:T(8,128)(2,1)S(1)}, bf16[515,64]{1,0:T(8,128)(2,1)S(1)}, u32[]{:S(2)}, u32[]{:S(2)}) %collective-permute-start.3) | collective-permute-done | bytes 65952 | tf_op jit(solution)/shard_map/ppermute | solution.py:149
  140.9 1.0 fusion.22
  141.9 0.8 fusion.35.msg_ref
  142.7 0.7 broadcast_in_dim.52.dec_ref
  143.4 19.0 %shard_map.118 = f32[8,64,128]{2,1,0:T(8,128)} custom-call(f32[8,64,128]{2,1,0:T(8,128)} %fusion.35.msg_ref, f32[8,128]{1,0:T(8,128)} %broadcast_in_dim.52.dec_ref, f32[8,64,128]{2,1,0:T(8,128)} %sin_ref.1), custom_call_target="tpu_custom_call" | custom-call | tf_op jit(solution)/shard_map/pallas_call | solution.py:88
  162.6 1.3 fusion.14
  164.3 0.6 fusion.16
  165.3 2.2 multiply_reduce_fusion
  167.5 35.1 %all-gather.5.cloned.1.call-done = bf16[4096,512]{0,1:T(8,128)(2,1)} async-done(((bf16[128,512]{0,1:T(8,128)(2,1)}), bf16[4096,512]{0,1:T(8,128)(2,1)}) %all-gather.5.cloned.1.call-update) | async-done | bytes 4194320 | tf_op jit(solution)/shard_map/all_gather | solution.py:136
  202.7 6.5 %fusion = bf16[4096,512]{0,1:T(8,128)(2,1)} fusion(bf16[4096,512]{0,1:T(8,128)(2,1)} %all-gather.5.cloned.1.call-done, f32[512,512]{1,0:T(8,128)S(1)} %get-tuple-element.6, f32[512]{0:T(512)S(1)} %copy-done.5), kind=kOutput, calls=%fused_computation.1 | convolution fusion | flops 2150105088 | bytes 9439232 | tf_op jit(solution)/shard_map/dot_general | solution.py:210
  209.2 15.4 %psum.7 = f32[512]{0:T(512)S(1)} all-reduce(f32[512]{0:T(512)S(1)} %get-tuple-element.5), channel_id=1, replica_groups=mesh['seq'=32,'head'=8] {'head'}, use_global_device_ids=true, to_apply=%region_6.7 | all-reduce | flops 512 | bytes 4096 | tf_op jit(solution)/shard_map/psum | solution.py:216
  224.6 25.9 %reduce-scatter.2.cloned.1.call-done = bf16[512,512]{0,1:T(8,128)(2,1)} async-done(((bf16[4096,512]{0,1:T(8,128)(2,1)}), bf16[512,512]{0,1:T(8,128)(2,1)}) %reduce-scatter.2.cloned.1.call-update) | async-done | bytes 524304 | tf_op jit(solution)/shard_map/reduce_scatter | solution.py:214
  250.4 2.0 fusion.29
  (56 shorter events, 4.2 us)
Async XLA Ops:
  6.5 1.5 copy-start
  6.5 110.3 %all-gather.3.cloned.1.call-start = ((), (), s32[]{:S(2)}) async-start(), calls=%async_computation.1 | async-start | bytes 9732096 | tf_op jit(solution)/shard_map/all_gather | solution.py:135
  9.0 193.7 %all-gather.5.cloned.1.call-start = ((), (), s32[]{:S(2)}) async-start(), calls=%async_computation.2 | async-start | bytes 4325376 | tf_op jit(solution)/shard_map/all_gather | solution.py:136
  9.9 11.1 %collective-permute-start = (bf16[3,4096]{1,0:T(4,128)(2,1)S(1)}, bf16[3,4096]{1,0:T(4,128)(2,1)S(1)}, u32[]{:S(2)}, u32[]{:S(2)}) collective-permute-start(bf16[3,4096]{1,0:T(4,128)(2,1)S(1)} %slice.115), channel_id=1, source_target_pairs={{0,8},{8,16},{16,24},{24,32},{32,40},{40,48},{48,56},{56,64},{64,7... | collective-permute-start | bytes 73736 | tf_op jit(solution)/shard_map/ppermute | solution.py:16
  14.3 236.1 %reduce-scatter.2.cloned.1.call-start = ((), (), s32[]{:S(2)}) async-start(), calls=%async_computation.3 | async-start | bytes 4718592 | tf_op jit(solution)/shard_map/reduce_scatter | solution.py:214
  21.0 107.4 %copy-start.3 = (bf16[3,512]{1,0:T(4,128)(2,1)S(1)}, bf16[3,512]{1,0:T(4,128)(2,1)}, u32[]{:S(2)}) copy-start(bf16[3,512]{1,0:T(4,128)(2,1)} %param.17) | copy-start | bytes 9220
  127.2 1.4 copy-start.1
  127.2 3.1 %collective-permute-start.1 = (bf16[515,32]{1,0:T(8,128)(2,1)S(1)}, bf16[515,32]{1,0:T(8,128)(2,1)S(1)}, u32[]{:S(2)}, u32[]{:S(2)}) collective-permute-start(bf16[515,32]{1,0:T(8,128)(2,1)S(1)} %get-tuple-element.12), channel_id=1, source_target_pairs={{0,1},{1,0},{2,3},{3,2},{4,5},{5,4},{6,7},{7,6},{8,9},{9,8},{10,11... | collective-permute-start | bytes 98888 | tf_op jit(solution)/shard_map/ppermute | solution.py:142
  129.2 11.0 %copy-start.4 = (bf16[3,256]{1,0:T(4,128)(2,1)S(1)}, bf16[3,256]{1,0:T(4,128)(2,1)}, u32[]{:S(2)}) copy-start(bf16[3,256]{1,0:T(4,128)(2,1)} %param.18) | copy-start | bytes 4612
  130.5 5.6 %collective-permute-start.2 = (bf16[515,64]{1,0:T(8,128)(2,1)S(1)}, bf16[515,64]{1,0:T(8,128)(2,1)S(1)}, u32[]{:S(2)}, u32[]{:S(2)}) collective-permute-start(bf16[515,64]{1,0:T(8,128)(2,1)S(1)} %maximum_select_fusion.2), channel_id=1, source_target_pairs={{0,2},{1,3},{2,4},{3,5},{4,6},{5,7},{6,0},{7,1},{8,10},{9,11},{10,... | collective-permute-start | bytes 197768 | tf_op jit(solution)/shard_map/ppermute | solution.py:149
  131.8 8.2 %collective-permute-start.3 = (bf16[515,64]{1,0:T(8,128)(2,1)S(1)}, bf16[515,64]{1,0:T(8,128)(2,1)S(1)}, u32[]{:S(2)}, u32[]{:S(2)}) collective-permute-start(bf16[515,64]{1,0:T(8,128)(2,1)S(1)} %maximum_select_fusion.2), channel_id=1, source_target_pairs={{0,4},{1,5},{2,6},{3,7},{4,0},{5,1},{6,2},{7,3},{8,12},{9,13},{10,... | collective-permute-start | bytes 197768 | tf_op jit(solution)/shard_map/ppermute | solution.py:149
  134.3 5.7 %collective-permute-start.4 = (bf16[515,64]{1,0:T(8,128)(2,1)S(1)}, bf16[515,64]{1,0:T(8,128)(2,1)S(1)}, u32[]{:S(2)}, u32[]{:S(2)}) collective-permute-start(bf16[515,64]{1,0:T(8,128)(2,1)S(1)} %maximum_select_fusion.2), channel_id=1, source_target_pairs={{0,6},{1,7},{2,0},{3,1},{4,2},{5,3},{6,4},{7,5},{8,14},{9,15},{10,... | collective-permute-start | bytes 197768 | tf_op jit(solution)/shard_map/ppermute | solution.py:149
  162.6 1.7 copy-start.2
  165.0 37.7 %copy-start.5 = (f32[512]{0:T(512)S(1)}, f32[512]{0:T(512)}, u32[]{:S(2)}) copy-start(f32[512]{0:T(512)} %param.22) | copy-start | bytes 6148
Sparse Core Ops, SparseCore 0:
  9.9 106.8 all-gather.2
  119.3 83.3 all-gather.4
  209.3 41.0 reduce-scatter.1

commit v16 on v11

--- a/solution.py
+++ b/solution.py
@@ -51,6 +51,8 @@
             s_send[k] = out_ref[...].astype(s_send.dtype)
             a_send[k] = dec_acc[...]
         target = ((me + d) % count, hy, hc)
+        sends = 1 - (me + d) // count
+        receives = (me - d + count) // count
         pair = []
         for index, (src, dst) in enumerate(((s_send, s_recv), (a_send, a_recv))):
             copy = pltpu.make_async_remote_copy(
@@ -61,11 +63,11 @@
                 device_id=target,
                 device_id_type=pl.DeviceIdType.MESH,
             )
-            copy.start()
+            pl.when(sends == 1)(copy.start)
             pair.append(copy)
-        copies.extend(pair)
+        copies.append((sends, pair))
         for copy in pair:
-            copy.wait_recv()
+            pl.when(receives == 1)(copy.wait_recv)
         far_s = s_recv[k].astype(jnp.float32)
         far_a = a_recv[k]
         if k == 0:
@@ -74,18 +76,17 @@
         else:
             acc_s = out_ref[...]
             acc_a = dec_acc[...]
-            rows = acc_s.shape[1]
-            acc_a_rows = jnp.tile(acc_a, (1, rows // acc_a.shape[1], 1))
-            out_ref[...] = jnp.where(me >= d, acc_a_rows * far_s + acc_s, acc_s)
+            out_ref[...] = jnp.where(me >= d, acc_a[:, None, :] * far_s + acc_s, acc_s)
             dec_acc[...] = jnp.where(me >= d, acc_a * far_a, acc_a)
-    for copy in copies:
-        copy.wait_send()
+    for sends, pair in copies:
+        for copy in pair:
+            pl.when(sends == 1)(copy.wait_send)
 
 
 def entering_state(decay, end_state, state_in):
     count = lax.axis_size("seq")
     heads, rows, lanes = end_state.shape
-    decay_rows = jnp.broadcast_to(decay[:, None, None], (heads, 8, lanes))
+    decay_rows = jnp.broadcast_to(decay[:, None], (heads, lanes))
     shifts = [1]
     step = 1
     while step < count:
@@ -131,16 +132,39 @@
     first = lax.axis_index("seq") == 0
     w_x = w_xz[:, 0, :]
     w_z = w_xz[:, 1, :]
-    packed = jnp.concatenate([w_x, w_z, w_bc], axis=1)
+    heads_count = head_size()
+    hindex = lax.axis_index(HEAD)
+    core = hindex % 2
+    chip = hindex // 2
+    chips = heads_count // 2
+    width = w_bc.shape[1] // heads_count
+    w_half = lax.dynamic_slice_in_dim(w_bc, hindex * width, width, axis=1)
+    packed = jnp.concatenate([w_x, w_z, w_half], axis=1)
     gathered = lax.all_gather(packed, "seq", axis=0, tiled=True)
     w_out_cols = lax.all_gather(jnp.transpose(w_out), "seq", axis=0, tiled=True)
     lag = conv_x.shape[0] - 1
     earlier = passed_along(tokens[rows - lag :], "seq", 1)
     extended = jnp.concatenate([earlier, tokens], axis=0)
     xzbc = jnp.dot(extended, gathered, preferred_element_type=jnp.float32).astype(jnp.bfloat16)
+    own_part = xzbc[:, 2 * inner :]
+    other_part = lax.ppermute(own_part, HEAD, [(i, i ^ 1) for i in range(heads_count)])
+    chip_piece = jnp.where(
+        core == 0,
+        jnp.concatenate([own_part, other_part], axis=1),
+        jnp.concatenate([other_part, own_part], axis=1),
+    )
+    received = [chip_piece] + [
+        lax.ppermute(chip_piece, HEAD, [(i, (i + 2 * k) % heads_count) for i in range(heads_count)])
+        for k in range(1, chips)
+    ]
+    stacked = jnp.stack(received)
+    bc_all = jnp.concatenate(
+        [lax.dynamic_index_in_dim(stacked, (chip - j + chips) % chips, keepdims=False) for j in range(chips)],
+        axis=1,
+    )
     opening = lax.broadcasted_iota(jnp.int32, (rows + lag, 1), 0) < lag
     whole_x = jnp.where(first & opening, jnp.pad(tail_x, ((0, rows), (0, 0))), xzbc[:, :inner])
-    whole_bc = jnp.where(first & opening, jnp.pad(tail_bc, ((0, rows), (0, 0))), xzbc[:, 2 * inner :])
+    whole_bc = jnp.where(first & opening, jnp.pad(tail_bc, ((0, rows), (0, 0))), bc_all)
     z_val = xzbc[lag:, inner : 2 * inner]
     x_conv = depthwise(whole_x, conv_x)
     bc_conv = depthwise(whole_bc, conv_bc)
@@ -191,15 +215,15 @@
     y_val = parts / nstate + jnp.repeat(skip_gain, head_dim)[None, :] * x_conv.astype(jnp.float32)
     gated = y_val * jax.nn.silu(z_val.astype(jnp.float32))
     scaled = (gated * norm_gain[None, :]).astype(jnp.bfloat16)
-    partial_t = lax.dot_general(
-        w_out_cols, scaled, (((1,), (1,)), ((), ())), preferred_element_type=jnp.float32
-    )
     cores = lax.axis_size("hc")
     mine = lax.axis_index("hc")
-    split = partial_t.reshape(lax.axis_size("hy"), cores, -1, partial_t.shape[1])
-    other = jnp.where(mine == 0, split[:, 1], split[:, 0])
-    kept = jnp.where(mine == 0, split[:, 0], split[:, 1])
-    got = lax.ppermute(other.astype(jnp.bfloat16), "hc", [(i, (i + 1) % cores) for i in range(cores)])
+    blocks = w_out_cols.reshape(lax.axis_size("hy"), cores, -1, w_out_cols.shape[1])
+    w_mine = lax.dynamic_index_in_dim(blocks, mine, axis=1, keepdims=False)
+    w_other = lax.dynamic_index_in_dim(blocks, 1 - mine, axis=1, keepdims=False)
+    numbers = (((2,), (1,)), ((), ()))
+    kept = lax.dot_general(w_mine, scaled, numbers, preferred_element_type=jnp.float32)
+    sent = lax.dot_general(w_other, scaled, numbers, preferred_element_type=jnp.float32).astype(jnp.bfloat16)
+    got = lax.ppermute(sent, "hc", [(i, (i + 1) % cores) for i in range(cores)])
     chip_sum = (kept + got.astype(jnp.float32)).astype(jnp.bfloat16)
     result = jnp.transpose(
         lax.psum_scatter(chip_sum, "hy", scatter_dimension=0, tiled=False)

time: 296 us -> 332 us (1.12)
  waiting for transfers between devices: 136 us -> 189 us
  Pallas kernels: 47.3 us -> 18.2 us
  local copies, waits for them, and re-layouts: 34.4 us -> 50.9 us
  other arithmetic: 20.4 us -> 12.4 us
  starting transfers between devices: 7.58 us -> 14.2 us
    all_gather x1, waiting for transfers between devices: 14.8 us -> 68.4 us  [local(): w_out_cols = lax.all_gather(jnp.transpose(w_out), 'seq', axis=0, tiled=True)]
    pallas_call x1, Pallas kernels: 47.3 us -> 18.2 us  [entering_state(): pl.pallas_call(functools.partial(scan_kernel, count, tuple(shifts)), out_...]
    unnamed x32 -> x40, local copies, waits for them, and re-layouts: 0.07 us -> 19.7 us
    all_gather x1, waiting for transfers between devices: 96 us -> 79.4 us  [local(): gathered = lax.all_gather(packed, 'seq', axis=0, tiled=True)]
    reduce_scatter x1, waiting for transfers between devices: 20.3 us -> 35.1 us  [local(): lax.psum_scatter(chip_sum, 'hy', scatter_dimension=0, tiled=False)]
    dynamic_slice x0 -> x2, local copies, waits for them, and re-layouts: none -> 11.5 us  [the longest x1 11.4 us: local(): w_mine = lax.dynamic_index_in_dim(blocks, mine, axis=1, keepdims=False)]
    slice x2 -> x1, local copies, waits for them, and re-layouts: 11.4 us -> 0.16 us  [the longest x1 11.2 us: local(): kept = jnp.where(mine == 0, split[:, 0], split[:, 1])]
    ppermute x1 -> x5, starting transfers between devices: 3.13 us -> 9.78 us  [the longest x3 4.88 us: local(): lax.ppermute(chip_piece, HEAD, [(i, (i + 2 * k) % heads_count) for i in r...]
  transfers between devices with their start and end apart: 5 -> 9, of which waited for: 4 -> 5; matrix products, arithmetic and copies ran while one was open for 13% -> 16% of each run, Pallas kernels for 16% -> 0%
where the time goes in v16:
time: 332 us; the launch traced here: 331 us
  waiting for transfers between devices  189 us (57%)
  local copies, waits for them, and re-layouts  50.9 us (15%)
  matrix products  21.6 us (7%)
  Pallas kernels  18.2 us (5%)
  starting transfers between devices  14.2 us (4%)
  between operations  13.6 us (4%)
  other arithmetic  12.4 us (4%)
  blocking collectives  11.8 us (4%)
    all_gather x1, waiting for transfers between devices, local(): gathered = lax.all_gather(packed, 'seq', axis=0, tiled=True)  79.4 us
    all_gather x1, waiting for transfers between devices, local(): w_out_cols = lax.all_gather(jnp.transpose(w_out), 'seq', axis=0, tiled=True)  68.4 us
    reduce_scatter x1, waiting for transfers between devices, local(): lax.psum_scatter(chip_sum, 'hy', scatter_dimension=0, tiled=False)  35.1 us
    unnamed x40, local copies, waits for them, and re-layouts  19.7 us
    pallas_call x1, Pallas kernels, entering_state(): pl.pallas_call(functools.partial(scan_kernel, count, tuple(shifts)), out_...  18.2 us
    psum x1, blocking collectives, local(): total_sq = lax.psum(jnp.sum(gated * gated, axis=1), HEAD)  11.8 us
    dynamic_slice x1, local copies, waits for them, and re-layouts, local(): w_mine = lax.dynamic_index_in_dim(blocks, mine, axis=1, keepdims=False)  11.4 us
    dot_general x1, matrix products, local(): jnp.dot(extended, gathered, preferred_element_type=jnp.float32)  10.3 us
  transfers between devices with their start and end apart: 9, of which 5 were waited for; matrix products, arithmetic and copies ran while one was open for 16% of the time, Pallas kernels for 0%

profile of v16, /device:TPU:1, one launch (start us, length us, event | category | flops | bytes accessed | tf_op | source)
XLA Modules:
  0.0 331.3 jit_solution(7759096204951645137)
XLA Ops:
  7.5 1.5 fusion.58
  9.8 0.9 slice.115
  10.7 4.4 %collective-permute-start = (bf16[3,4096]{1,0:T(4,128)(2,1)S(1)}, bf16[3,4096]{1,0:T(4,128)(2,1)S(1)}, u32[]{:S(2)}, u32[]{:S(2)}) collective-permute-start(bf16[3,4096]{1,0:T(4,128)(2,1)S(1)} %slice.115), channel_id=1, source_target_pairs={{0,8},{8,16},{16,24},{24,32},{32,40},{40,48},{48,56},{56,64},{64,7... | collective-permute-start | bytes 73736 | tf_op jit(solution)/shard_map/ppermute | solution.py:23
  15.9 1.1 reduce-window.14
  17.5 1.1 reduce-window.16
  22.2 1.4 fusion.60
  25.2 68.4 %all-gather.3.cloned.1.call-done = bf16[4096,512]{0,1:T(8,128)(2,1)} async-done(((bf16[128,512]{0,1:T(8,128)(2,1)}), bf16[4096,512]{0,1:T(8,128)(2,1)}) %all-gather.3.cloned.1.call-update) | async-done | bytes 4194320 | tf_op jit(solution)/shard_map/all_gather | solution.py:144
  93.6 7.8 %reshape.151 = bf16[4,2,512,512]{2,1,0,3:T(2,128)(2,1)} reshape(bf16[4096,512]{0,1:T(8,128)(2,1)} %all-gather.3.cloned.1.call-done) | data formatting | bytes 8388608 | tf_op jit(solution)/shard_map/reshape | solution.py:220
  101.4 11.4 %constant_dynamic-slice_fusion.2 = (bf16[4,1,512,512]{2,1,0,3:T(2,128)(2,1)}, bf16[4,1,512,512]{2,1,0,3:T(2,128)(2,1)}) fusion(bf16[4,2,512,512]{2,1,0,3:T(2,128)(2,1)} %reshape.151, s32[]{:T(128)S(6)} %select_n.84, s32[]{:T(128)S(6)} %select_n.104), kind=kLoop, calls=%fused_computation.95 | loop fusion | bytes 8388616 | tf_op jit(solution)/shard_map/jit(dynamic_index_in_dim)/dynamic_slice | solution.py:221
  112.8 10.5 %copy.48 = bf16[4,1,512,512]{3,2,0,1:T(8,128)(2,1)} copy(bf16[4,1,512,512]{2,1,0,3:T(2,128)(2,1)} %get-tuple-element.12) | data formatting | bytes 4194304
  123.3 79.4 %all-gather.5.cloned.1.call-done = bf16[4096,1056]{1,0:T(8,128)(2,1)} async-done(((bf16[128,1056]{1,0:T(8,128)(2,1)}), bf16[4096,1056]{1,0:T(8,128)(2,1)}) %all-gather.5.cloned.1.call-update) | async-done | bytes 8650768 | tf_op jit(solution)/shard_map/all_gather | solution.py:143
  202.7 10.3 %fusion.4 = bf16[515,1056]{1,0:T(8,128)(2,1)S(1)} fusion(bf16[4096,1056]{1,0:T(8,128)(2,1)} %all-gather.5.cloned.1.call-done, bf16[512,4096]{1,0:T(8,128)(2,1)} %param.12, bf16[3,4096]{1,0:T(4,128)(2,1)S(1)} %collective-permute-done), kind=kOutput, calls=%fused_computation.6 | convolution fusion | flops 4464118784 | bytes 13957312 | tf_op jit(solution)/shard_map/dot_general | solution.py:148
  213.8 1.1 collective-permute-start.1
  216.9 1.1 maximum_select_fusion.2
  218.1 1.3 collective-permute-start.2
  219.3 2.4 collective-permute-start.3
  221.8 1.2 collective-permute-start.4
  223.1 1.2 collective-permute-done.2
  224.3 3.8 %collective-permute-done.3 = bf16[515,64]{1,0:T(8,128)(2,1)S(1)} collective-permute-done((bf16[515,64]{1,0:T(8,128)(2,1)S(1)}, bf16[515,64]{1,0:T(8,128)(2,1)S(1)}, u32[]{:S(2)}, u32[]{:S(2)}) %collective-permute-start.3) | collective-permute-done | bytes 65952 | tf_op jit(solution)/shard_map/ppermute | solution.py:157
  229.3 1.2 fusion.22
  230.6 1.0 fusion.30
  233.5 18.2 %shard_map.118 = f32[8,64,128]{2,1,0:T(8,128)} custom-call(f32[8,64,128]{2,1,0:T(8,128)} %fusion.44.msg_ref, f32[8,128]{1,0:T(8,128)} %broadcast_in_dim.52.dec_ref, f32[8,64,128]{2,1,0:T(8,128)} %sin_ref.1), custom_call_target="tpu_custom_call" | custom-call | tf_op jit(solution)/shard_map/pallas_call | solution.py:96
  251.7 1.6 fusion.24
  253.6 2.4 multiply_reduce_fusion
  256.0 2.6 fusion.17
  258.7 3.8 %collective-permute-start.5 = (bf16[4,512,512]{2,1,0:T(8,128)(2,1)}, bf16[4,512,512]{2,1,0:T(8,128)(2,1)}, u32[]{:S(2)}, u32[]{:S(2)}) collective-permute-start(bf16[4,512,512]{2,1,0:T(8,128)(2,1)} %fusion.17), channel_id=1, source_target_pairs={{0,1},{1,0},{2,3},{3,2},{4,5},{5,4},{6,7},{7,6},{8,9},{9,8},{10,11... | collective-permute-start | bytes 6291464 | tf_op jit(solution)/shard_map/ppermute | solution.py:226
  262.5 9.1 %copy.45 = bf16[4,1,512,512]{3,2,0,1:T(8,128)(2,1)S(1)} copy(bf16[4,1,512,512]{2,1,0,3:T(2,128)(2,1)} %get-tuple-element.11) | data formatting | bytes 4194304
  271.6 4.2 %add_convert_fusion = bf16[4,512,512]{2,1,0:T(8,128)(2,1)} fusion(bf16[4,512,512]{2,1,0:T(8,128)(2,1)} %collective-permute-done.5, bf16[4,1,512,512]{3,2,0,1:T(8,128)(2,1)S(1)} %copy.45, f32[512,512]{1,0:T(8,128)S(1)} %copy-done.4, f32[512]{0:T(512)S(1)} %copy-done.18), kind=kOutput, calls=%fused_computation.4 | convolution fusion | flops 1077411840 | bytes 7342080 | tf_op jit(solution)/shard_map/dot_general | solution.py:224
  275.8 11.8 %psum.7 = f32[512]{0:T(512)S(1)} all-reduce(f32[512]{0:T(512)S(1)} %get-tuple-element.5), channel_id=1, replica_groups=mesh['seq'=32,'hy'=4,'hc'=2] {'hy','hc'}, use_global_device_ids=true, to_apply=%region_6.7 | all-reduce | flops 512 | bytes 4096 | tf_op jit(solution)/shard_map/psum | solution.py:231
  287.6 35.1 %reduce-scatter.2.cloned.1.call-done = bf16[1,512,512]{2,1,0:T(8,128)(2,1)} async-done(((bf16[4,512,512]{2,1,0:T(8,128)(2,1)}), bf16[1,512,512]{2,1,0:T(8,128)(2,1)}) %reduce-scatter.2.cloned.1.call-update) | async-done | bytes 524304 | tf_op jit(solution)/shard_map/reduce_scatter | solution.py:229
  322.7 1.1 fusion.39
  323.8 1.0 copy.42
  (90 shorter events, 14.2 us)
Async XLA Ops:
  6.5 0.8 copy-start
  6.5 87.0 %all-gather.3.cloned.1.call-start = ((), (), s32[]{:S(2)}) async-start(), calls=%async_computation.1 | async-start | bytes 4325376 | tf_op jit(solution)/shard_map/all_gather | solution.py:144
  7.3 195.4 %all-gather.5.cloned.1.call-start = ((), (), s32[]{:S(2)}) async-start(), calls=%async_computation.2 | async-start | bytes 9732096 | tf_op jit(solution)/shard_map/all_gather | solution.py:143
  9.8 312.9 %reduce-scatter.2.cloned.1.call-start = ((), (), s32[]{:S(2)}) async-start(), calls=%async_computation.3 | async-start | bytes 2621440 | tf_op jit(solution)/shard_map/reduce_scatter | solution.py:229
  10.7 112.6 %collective-permute-start = (bf16[3,4096]{1,0:T(4,128)(2,1)S(1)}, bf16[3,4096]{1,0:T(4,128)(2,1)S(1)}, u32[]{:S(2)}, u32[]{:S(2)}) collective-permute-start(bf16[3,4096]{1,0:T(4,128)(2,1)S(1)} %slice.115), channel_id=1, source_target_pairs={{0,8},{8,16},{16,24},{24,32},{32,40},{40,48},{48,56},{56,64},{64,7... | collective-permute-start | bytes 73736 | tf_op jit(solution)/shard_map/ppermute | solution.py:23
  20.2 194.7 %copy-start.13 = (pred[515]{0:T(1024)(128)(4,1)}, pred[515]{0:T(1024)(128)(4,1)S(1)}, u32[]{:S(2)}) copy-start(pred[515]{0:T(1024)(128)(4,1)S(1)} %fusion.50) | copy-start | bytes 1549
  123.3 91.6 %copy-start.8 = (bf16[3,512]{1,0:T(4,128)(2,1)S(1)}, bf16[3,512]{1,0:T(4,128)(2,1)}, u32[]{:S(2)}) copy-start(bf16[3,512]{1,0:T(4,128)(2,1)} %param.17) | copy-start | bytes 9220
  213.0 2.0 copy-start.2
  213.8 3.1 collective-permute-start.1
  216.2 12.1 %copy-start.14 = (pred[515]{0:T(1024)(128)(4,1)S(1)}, pred[515]{0:T(1024)(128)(4,1)}, u32[]{:S(2)}) copy-start(pred[515]{0:T(1024)(128)(4,1)} %copy-done.13) | copy-start | bytes 1549
  216.2 12.1 %copy-start.15 = (bf16[3,256]{1,0:T(4,128)(2,1)S(1)}, bf16[3,256]{1,0:T(4,128)(2,1)}, u32[]{:S(2)}) copy-start(bf16[3,256]{1,0:T(4,128)(2,1)} %param.18) | copy-start | bytes 4612
  216.3 12.4 %copy-start.9 = (f32[1,256]{1,0:T(1,128)S(1)}, f32[1,256]{1,0:T(1,128)}, u32[]{:S(2)}) copy-start(f32[1,256]{1,0:T(1,128)} %get-tuple-element.29) | copy-start | bytes 3076
  216.3 12.4 %copy-start.10 = (f32[1,256]{1,0:T(1,128)S(1)}, f32[1,256]{1,0:T(1,128)}, u32[]{:S(2)}) copy-start(f32[1,256]{1,0:T(1,128)} %get-tuple-element.30) | copy-start | bytes 3076
  216.3 12.4 %copy-start.11 = (f32[1,256]{1,0:T(1,128)S(1)}, f32[1,256]{1,0:T(1,128)}, u32[]{:S(2)}) copy-start(f32[1,256]{1,0:T(1,128)} %get-tuple-element.31) | copy-start | bytes 3076
  216.3 12.4 %copy-start.12 = (f32[1,256]{1,0:T(1,128)S(1)}, f32[1,256]{1,0:T(1,128)}, u32[]{:S(2)}) copy-start(f32[1,256]{1,0:T(1,128)} %get-tuple-element.32) | copy-start | bytes 3076
  216.9 12.4 %copy-start.5 = (pred[256,256]{1,0:T(8,128)(4,1)S(1)}, pred[256,256]{1,0:T(8,128)(4,1)}, u32[]{:S(2)}) copy-start(pred[256,256]{1,0:T(8,128)(4,1)} %iota_compare_fusion) | copy-start | bytes 196612
  216.9 12.4 %copy-start.6 = (f32[2,8,256]{2,1,0:T(8,128)S(1)}, f32[2,8,256]{2,1,0:T(8,128)}, u32[]{:S(2)}) copy-start(f32[2,8,256]{2,1,0:T(8,128)} %get-tuple-element.10) | copy-start | bytes 49156
  218.1 6.3 %collective-permute-start.2 = (bf16[515,64]{1,0:T(8,128)(2,1)S(1)}, bf16[515,64]{1,0:T(8,128)(2,1)S(1)}, u32[]{:S(2)}, u32[]{:S(2)}) collective-permute-start(bf16[515,64]{1,0:T(8,128)(2,1)S(1)} %maximum_select_fusion.2), channel_id=1, source_target_pairs={{0,2},{1,3},{2,4},{3,5},{4,6},{5,7},{6,0},{7,1},{8,10},{9,11},{10,... | collective-permute-start | bytes 197768 | tf_op jit(solution)/shard_map/ppermute | solution.py:157
  219.3 8.8 %collective-permute-start.3 = (bf16[515,64]{1,0:T(8,128)(2,1)S(1)}, bf16[515,64]{1,0:T(8,128)(2,1)S(1)}, u32[]{:S(2)}, u32[]{:S(2)}) collective-permute-start(bf16[515,64]{1,0:T(8,128)(2,1)S(1)} %maximum_select_fusion.2), channel_id=1, source_target_pairs={{0,4},{1,5},{2,6},{3,7},{4,0},{5,1},{6,2},{7,3},{8,12},{9,13},{10,... | collective-permute-start | bytes 197768 | tf_op jit(solution)/shard_map/ppermute | solution.py:157
  221.8 6.4 %collective-permute-start.4 = (bf16[515,64]{1,0:T(8,128)(2,1)S(1)}, bf16[515,64]{1,0:T(8,128)(2,1)S(1)}, u32[]{:S(2)}, u32[]{:S(2)}) collective-permute-start(bf16[515,64]{1,0:T(8,128)(2,1)S(1)} %maximum_select_fusion.2), channel_id=1, source_target_pairs={{0,6},{1,7},{2,0},{3,1},{4,2},{5,3},{6,4},{7,5},{8,14},{9,15},{10,... | collective-permute-start | bytes 197768 | tf_op jit(solution)/shard_map/ppermute | solution.py:157
  229.3 2.7 copy-start.17
  230.6 2.3 copy-start.16
  230.6 23.0 %copy-start.7 = (f32[512]{0:T(512)S(1)}, f32[512]{0:T(512)}, u32[]{:S(2)}) copy-start(f32[512]{0:T(512)} %mul.217) | copy-start | bytes 6148
  253.3 2.7 copy-start.18
  253.6 2.4 copy-start.1
  256.0 6.5 %copy-start.3 = (f32[512,512]{1,0:T(8,128)}, f32[512,512]{1,0:T(8,128)S(1)}, u32[]{:S(2)}) copy-start(f32[512,512]{1,0:T(8,128)S(1)} %get-tuple-element.6) | copy-start | bytes 3145732
  258.7 12.9 %collective-permute-start.5 = (bf16[4,512,512]{2,1,0:T(8,128)(2,1)}, bf16[4,512,512]{2,1,0:T(8,128)(2,1)}, u32[]{:S(2)}, u32[]{:S(2)}) collective-permute-start(bf16[4,512,512]{2,1,0:T(8,128)(2,1)} %fusion.17), channel_id=1, source_target_pairs={{0,1},{1,0},{2,3},{3,2},{4,5},{5,4},{6,7},{7,6},{8,9},{9,8},{10,11... | collective-permute-start | bytes 6291464 | tf_op jit(solution)/shard_map/ppermute | solution.py:226
  262.5 9.1 %copy-start.4 = (f32[512,512]{1,0:T(8,128)S(1)}, f32[512,512]{1,0:T(8,128)}, u32[]{:S(2)}) copy-start(f32[512,512]{1,0:T(8,128)} %copy-done.3) | copy-start | bytes 3145732
Sparse Core Ops, SparseCore 0:
  9.8 83.7 all-gather.2
  96.2 106.4 all-gather.4
  275.9 46.6 reduce-scatter.1

commit v17 on v15

--- a/solution.py
+++ b/solution.py
@@ -131,9 +131,11 @@
     chips = heads_count // 2
     width = w_bc.shape[1] // heads_count
     w_half = lax.dynamic_slice_in_dim(w_bc, hindex * width, width, axis=1)
-    packed = jnp.concatenate([w_x, w_z, w_half], axis=1)
-    gathered = lax.all_gather(packed, "seq", axis=0, tiled=True)
-    w_out_cols = lax.all_gather(jnp.transpose(w_out), "seq", axis=0, tiled=True)
+    packed = jnp.concatenate([w_x, w_z, w_half, jnp.transpose(w_out)], axis=1)
+    gathered_all = lax.all_gather(packed, "seq", axis=0, tiled=True)
+    proj = w_x.shape[1] + w_z.shape[1] + w_half.shape[1]
+    gathered = gathered_all[:, :proj]
+    w_out_cols = gathered_all[:, proj:]
     lag = conv_x.shape[0] - 1
     earlier = passed_along(tokens[rows - lag :], "seq", 1)
     extended = jnp.concatenate([earlier, tokens], axis=0)

time: 262 us -> 270 us (1.031)
  waiting for transfers between devices: 161 us -> 166 us
    reduce_scatter x1, waiting for transfers between devices: 25.9 us -> 43.5 us  [local(): lax.psum_scatter(partial_t.astype(jnp.bfloat16), 'head', scatter_dimensio...]
    all_gather x2 -> x1, waiting for transfers between devices: 131 us -> 118 us  [local(): gathered_all = lax.all_gather(packed, 'seq', axis=0, tiled=True)]
  transfers between devices with their start and end apart: 8 -> 7, of which waited for: 5 -> 4; matrix products, arithmetic and copies ran while one was open for 11% -> 4% of each run, Pallas kernels for 7% -> 0%
where the time goes in v17:
time: 270 us; the launch traced here: 267 us
  waiting for transfers between devices  166 us (61%)
  matrix products  21.3 us (8%)
  Pallas kernels  17.9 us (7%)
  blocking collectives  14.6 us (5%)
  between operations  13.8 us (5%)
  starting transfers between devices  12.5 us (5%)
  other arithmetic  11 us (4%)
  local copies, waits for them, and re-layouts  10.2 us (4%)
    all_gather x1, waiting for transfers between devices, local(): gathered_all = lax.all_gather(packed, 'seq', axis=0, tiled=True)  118 us
    reduce_scatter x1, waiting for transfers between devices, local(): lax.psum_scatter(partial_t.astype(jnp.bfloat16), 'head', scatter_dimensio...  43.5 us
    pallas_call x1, Pallas kernels, entering_state(): pl.pallas_call(functools.partial(scan_kernel, count, tuple(shifts)), out_...  17.9 us
    psum x1, blocking collectives, local(): total_sq = lax.psum(jnp.sum(gated * gated, axis=1), 'head')  14.6 us
    dot_general x1, matrix products, local(): jnp.dot(extended, gathered, preferred_element_type=jnp.float32)  10.3 us
    dot_general x1, matrix products, local(): lax.dot_general(w_out_cols, scaled, (((1,), (1,)), ((), ())), preferred_e...  6.52 us
  transfers between devices with their start and end apart: 7, of which 4 were waited for; matrix products, arithmetic and copies ran while one was open for 4% of the time, Pallas kernels for 0%

profile of v17, /device:TPU:1, one launch (start us, length us, event | category | flops | bytes accessed | tf_op | source)
XLA Modules:
  0.0 267.5 jit_solution(12324013688871554533)
XLA Ops:
  6.5 0.8 copy-done
  7.5 1.6 fusion.50
  9.5 1.7 pad_maximum_fusion.1
  11.2 0.9 slice.124
  12.1 4.4 %collective-permute-start = (bf16[3,4096]{1,0:T(4,128)(2,1)S(1)}, bf16[3,4096]{1,0:T(4,128)(2,1)S(1)}, u32[]{:S(2)}, u32[]{:S(2)}) collective-permute-start(bf16[3,4096]{1,0:T(4,128)(2,1)S(1)} %slice.124), channel_id=1, source_target_pairs={{0,8},{8,16},{16,24},{24,32},{32,40},{40,48},{48,56},{56,64},{64,7... | collective-permute-start | bytes 73736 | tf_op jit(solution)/shard_map/ppermute | solution.py:16
  16.5 0.7 fusion.45
  17.2 1.1 reduce-window.14
  18.8 1.1 reduce-window.16
  20.4 0.8 fusion.52
  21.3 0.9 fusion.51
  22.3 0.7 broadcast_in_dim.53
  23.1 118.1 %all-gather.2.cloned.1.call-done = bf16[4096,1568]{0,1:T(8,128)(2,1)} async-done(((bf16[128,1568]{0,1:T(8,128)(2,1)}), bf16[4096,1568]{0,1:T(8,128)(2,1)}) %all-gather.2.cloned.1.call-update) | async-done | bytes 12845072 | tf_op jit(solution)/shard_map/all_gather | solution.py:135
  141.3 10.3 %fusion.6 = bf16[515,1056]{1,0:T(8,128)(2,1)S(1)} fusion(bf16[4096,1568]{0,1:T(8,128)(2,1)} %all-gather.2.cloned.1.call-done, bf16[512,4096]{1,0:T(8,128)(2,1)} %param.12, bf16[3,4096]{1,0:T(4,128)(2,1)S(1)} %collective-permute-done), kind=kOutput, calls=%fused_computation.8 | convolution fusion | flops 4464118784 | bytes 13957312 | tf_op jit(solution)/shard_map/dot_general | solution.py:142
  151.6 3.2 %collective-permute-start.1 = (bf16[515,32]{1,0:T(8,128)(2,1)S(1)}, bf16[515,32]{1,0:T(8,128)(2,1)S(1)}, u32[]{:S(2)}, u32[]{:S(2)}) collective-permute-start(bf16[515,32]{1,0:T(8,128)(2,1)S(1)} %get-tuple-element.12), channel_id=1, source_target_pairs={{0,1},{1,0},{2,3},{3,2},{4,5},{5,4},{6,7},{7,6},{8,9},{9,8},{10,11... | collective-permute-start | bytes 98888 | tf_op jit(solution)/shard_map/ppermute | solution.py:144
  155.0 0.6 multiply_convert_fusion.8
  156.2 0.6 copy.37
  157.0 1.3 collective-permute-start.2
  158.3 2.4 collective-permute-start.3
  160.7 1.2 collective-permute-start.4
  162.6 3.8 %collective-permute-done.3 = bf16[515,64]{1,0:T(8,128)(2,1)S(1)} collective-permute-done((bf16[515,64]{1,0:T(8,128)(2,1)S(1)}, bf16[515,64]{1,0:T(8,128)(2,1)S(1)}, u32[]{:S(2)}, u32[]{:S(2)}) %collective-permute-start.3) | collective-permute-done | bytes 65952 | tf_op jit(solution)/shard_map/ppermute | solution.py:151
  167.5 1.3 fusion.17
  168.8 1.0 fusion.25
  170.2 0.8 fusion.38.msg_ref
  171.0 0.7 broadcast_in_dim.52.dec_ref
  171.7 17.9 %shard_map.118 = f32[8,64,128]{2,1,0:T(8,128)} custom-call(f32[8,64,128]{2,1,0:T(8,128)} %fusion.38.msg_ref, f32[8,128]{1,0:T(8,128)} %broadcast_in_dim.52.dec_ref, f32[8,64,128]{2,1,0:T(8,128)} %sin_ref.1), custom_call_target="tpu_custom_call" | custom-call | tf_op jit(solution)/shard_map/pallas_call | solution.py:88
  189.6 1.6 fusion.19
  191.5 2.2 multiply_reduce_fusion
  193.8 6.5 %convolution_convert_fusion = bf16[4096,512]{1,0:T(8,128)(2,1)} fusion(bf16[4096,1568]{0,1:T(8,128)(2,1)} %all-gather.2.cloned.1.call-done, f32[512,512]{1,0:T(8,128)S(1)} %get-tuple-element.6, f32[512]{0:T(512)S(1)} %copy-done.4), kind=kOutput, calls=%fused_computation.2 | convolution fusion | flops 2150105088 | bytes 9439232 | tf_op jit(solution)/shard_map/dot_general | solution.py:212
  200.3 14.6 %psum.7 = f32[512]{0:T(512)S(1)} all-reduce(f32[512]{0:T(512)S(1)} %get-tuple-element.5), channel_id=1, replica_groups=mesh['seq'=32,'head'=8] {'head'}, use_global_device_ids=true, to_apply=%region_6.7 | all-reduce | flops 512 | bytes 4096 | tf_op jit(solution)/shard_map/psum | solution.py:218
  215.0 43.5 %reduce-scatter.2.cloned.1.call-done = bf16[512,512]{1,0:T(8,128)(2,1)} async-done(((bf16[4096,512]{1,0:T(8,128)(2,1)}), bf16[512,512]{1,0:T(8,128)(2,1)}) %reduce-scatter.2.cloned.1.call-update) | async-done | bytes 524304 | tf_op jit(solution)/shard_map/reduce_scatter | solution.py:216
  258.5 1.1 fusion.32
  259.6 1.0 copy.40
  (54 shorter events, 5.1 us)
Async XLA Ops:
  6.5 0.8 copy-start
  6.5 134.7 %all-gather.2.cloned.1.call-start = ((), (), s32[]{:S(2)}) async-start(), calls=%async_computation.1 | async-start | bytes 13246464 | tf_op jit(solution)/shard_map/all_gather | solution.py:135
  11.2 247.4 %reduce-scatter.2.cloned.1.call-start = ((), (), s32[]{:S(2)}) async-start(), calls=%async_computation.2 | async-start | bytes 4718592 | tf_op jit(solution)/shard_map/reduce_scatter | solution.py:216
  12.1 11.1 %collective-permute-start = (bf16[3,4096]{1,0:T(4,128)(2,1)S(1)}, bf16[3,4096]{1,0:T(4,128)(2,1)S(1)}, u32[]{:S(2)}, u32[]{:S(2)}) collective-permute-start(bf16[3,4096]{1,0:T(4,128)(2,1)S(1)} %slice.124), channel_id=1, source_target_pairs={{0,8},{8,16},{16,24},{24,32},{32,40},{40,48},{48,56},{56,64},{64,7... | collective-permute-start | bytes 73736 | tf_op jit(solution)/shard_map/ppermute | solution.py:16
  23.1 131.7 %copy-start.2 = (bf16[3,512]{1,0:T(4,128)(2,1)S(1)}, bf16[3,512]{1,0:T(4,128)(2,1)}, u32[]{:S(2)}) copy-start(bf16[3,512]{1,0:T(4,128)(2,1)} %param.17) | copy-start | bytes 9220
  151.6 3.4 %copy-start.1 = (bf16[515,1056]{1,0:T(8,128)(2,1)}, bf16[515,1056]{1,0:T(8,128)(2,1)S(1)}, u32[]{:S(2)}) copy-start(bf16[515,1056]{1,0:T(8,128)(2,1)S(1)} %fusion.6) | copy-start | bytes 3263044
  151.6 5.2 %collective-permute-start.1 = (bf16[515,32]{1,0:T(8,128)(2,1)S(1)}, bf16[515,32]{1,0:T(8,128)(2,1)S(1)}, u32[]{:S(2)}, u32[]{:S(2)}) collective-permute-start(bf16[515,32]{1,0:T(8,128)(2,1)S(1)} %get-tuple-element.12), channel_id=1, source_target_pairs={{0,1},{1,0},{2,3},{3,2},{4,5},{5,4},{6,7},{7,6},{8,9},{9,8},{10,11... | collective-permute-start | bytes 98888 | tf_op jit(solution)/shard_map/ppermute | solution.py:144
  155.7 10.9 %copy-start.3 = (bf16[3,256]{1,0:T(4,128)(2,1)S(1)}, bf16[3,256]{1,0:T(4,128)(2,1)}, u32[]{:S(2)}) copy-start(bf16[3,256]{1,0:T(4,128)(2,1)} %param.18) | copy-start | bytes 4612
  157.0 5.5 %collective-permute-start.2 = (bf16[515,64]{1,0:T(8,128)(2,1)S(1)}, bf16[515,64]{1,0:T(8,128)(2,1)S(1)}, u32[]{:S(2)}, u32[]{:S(2)}) collective-permute-start(bf16[515,64]{1,0:T(8,128)(2,1)S(1)} %maximum_select_fusion.2), channel_id=1, source_target_pairs={{0,2},{1,3},{2,4},{3,5},{4,6},{5,7},{6,0},{7,1},{8,10},{9,11},{10,... | collective-permute-start | bytes 197768 | tf_op jit(solution)/shard_map/ppermute | solution.py:151
  158.3 8.1 %collective-permute-start.3 = (bf16[515,64]{1,0:T(8,128)(2,1)S(1)}, bf16[515,64]{1,0:T(8,128)(2,1)S(1)}, u32[]{:S(2)}, u32[]{:S(2)}) collective-permute-start(bf16[515,64]{1,0:T(8,128)(2,1)S(1)} %maximum_select_fusion.2), channel_id=1, source_target_pairs={{0,4},{1,5},{2,6},{3,7},{4,0},{5,1},{6,2},{7,3},{8,12},{9,13},{10,... | collective-permute-start | bytes 197768 | tf_op jit(solution)/shard_map/ppermute | solution.py:151
  160.7 5.7 %collective-permute-start.4 = (bf16[515,64]{1,0:T(8,128)(2,1)S(1)}, bf16[515,64]{1,0:T(8,128)(2,1)S(1)}, u32[]{:S(2)}, u32[]{:S(2)}) collective-permute-start(bf16[515,64]{1,0:T(8,128)(2,1)S(1)} %maximum_select_fusion.2), channel_id=1, source_target_pairs={{0,6},{1,7},{2,0},{3,1},{4,2},{5,3},{6,4},{7,5},{8,14},{9,15},{10,... | collective-permute-start | bytes 197768 | tf_op jit(solution)/shard_map/ppermute | solution.py:151
  191.2 2.6 copy-start.4
Sparse Core Ops, SparseCore 0:
  11.3 129.9 all-gather.1
  200.4 58.0 reduce-scatter.1

commit v18 on v15

--- a/solution.py
+++ b/solution.py
@@ -206,16 +206,15 @@
     parts = (parts + correction * jnp.exp(cum_range)[:, :, None]).reshape(rows, inner)
     y_val = parts / nstate + jnp.repeat(skip_gain, head_dim)[None, :] * x_conv.astype(jnp.float32)
     gated = y_val * jax.nn.silu(z_val.astype(jnp.float32))
-    scaled = (gated * norm_gain[None, :]).astype(jnp.bfloat16)
-    partial_t = lax.dot_general(
-        w_out_cols, scaled, (((1,), (1,)), ((), ())), preferred_element_type=jnp.float32
-    )
-    result = jnp.transpose(
-        lax.psum_scatter(partial_t.astype(jnp.bfloat16), "head", scatter_dimension=0, tiled=True)
-    ).astype(jnp.float32)
     total_sq = lax.psum(jnp.sum(gated * gated, axis=1), "head")
     meansq = total_sq / (inner * lax.axis_size("head"))
-    return (result * lax.rsqrt(meansq[:, None] + 1e-05)).astype(jnp.bfloat16)
+    normed = (gated * lax.rsqrt(meansq[:, None] + 1e-05) * norm_gain[None, :]).astype(jnp.bfloat16)
+    partial_t = lax.dot_general(
+        w_out_cols, normed, (((1,), (1,)), ((), ())), preferred_element_type=jnp.float32
+    )
+    return jnp.transpose(
+        lax.psum_scatter(partial_t.astype(jnp.bfloat16), "head", scatter_dimension=0, tiled=True)
+    )
 
 
 def solution(mesh):

time: 262 us -> 260 us (level)
    all_gather x1, waiting for transfers between devices: 35.1 us -> 18.6 us  [local(): w_out_cols = lax.all_gather(jnp.transpose(w_out), 'seq', axis=0, tiled=True)]
    reduce_scatter x1, waiting for transfers between devices: 25.9 us -> 41.3 us  [local(): lax.psum_scatter(partial_t.astype(jnp.bfloat16), 'head', scatter_dimensio...]
where the time goes in v18:
time: 260 us; the launch traced here: 257 us
  waiting for transfers between devices  160 us (62%)
  matrix products  20.4 us (8%)
  Pallas kernels  19 us (7%)
  blocking collectives  16.5 us (6%)
  between operations  13.5 us (5%)
  starting transfers between devices  10.5 us (4%)
  other arithmetic  8.95 us (3%)
  local copies, waits for them, and re-layouts  7.99 us (3%)
    all_gather x1, waiting for transfers between devices, local(): gathered = lax.all_gather(packed, 'seq', axis=0, tiled=True)  95.8 us
    reduce_scatter x1, waiting for transfers between devices, local(): lax.psum_scatter(partial_t.astype(jnp.bfloat16), 'head', scatter_dimensio...  41.3 us
    pallas_call x1, Pallas kernels, entering_state(): pl.pallas_call(functools.partial(scan_kernel, count, tuple(shifts)), out_...  19 us
    all_gather x1, waiting for transfers between devices, local(): w_out_cols = lax.all_gather(jnp.transpose(w_out), 'seq', axis=0, tiled=True)  18.6 us
    psum x1, blocking collectives, local(): total_sq = lax.psum(jnp.sum(gated * gated, axis=1), 'head')  16.5 us
    dot_general x1, matrix products, local(): jnp.dot(extended, gathered, preferred_element_type=jnp.float32)  10.3 us
    dot_general x1, matrix products, local(): lax.dot_general(w_out_cols, normed, (((1,), (1,)), ((), ())), preferred_e...  6.51 us
  transfers between devices with their start and end apart: 8, of which 5 were waited for; matrix products, arithmetic and copies ran while one was open for 11% of the time, Pallas kernels for 7%

profile of v18, /device:TPU:1, one launch (start us, length us, event | category | flops | bytes accessed | tf_op | source)
XLA Modules:
  0.0 257.0 jit_solution(9553818617259712944)
XLA Ops:
  6.5 1.5 fusion.47
  8.2 0.7 pad_maximum_fusion.1
  9.0 0.9 slice.115
  9.9 4.4 %collective-permute-start = (bf16[3,4096]{1,0:T(4,128)(2,1)S(1)}, bf16[3,4096]{1,0:T(4,128)(2,1)S(1)}, u32[]{:S(2)}, u32[]{:S(2)}) collective-permute-start(bf16[3,4096]{1,0:T(4,128)(2,1)S(1)} %slice.115), channel_id=1, source_target_pairs={{0,8},{8,16},{16,24},{24,32},{32,40},{40,48},{48,56},{56,64},{64,7... | collective-permute-start | bytes 73736 | tf_op jit(solution)/shard_map/ppermute | solution.py:16
  14.4 0.7 fusion.42
  15.1 1.1 reduce-window.14
  16.7 1.1 reduce-window.16
  18.3 0.8 fusion.49
  19.2 0.9 fusion.48
  20.2 0.7 broadcast_in_dim.53
  21.0 95.8 %all-gather.3.cloned.1.call-done = bf16[4096,1056]{1,0:T(8,128)(2,1)} async-done(((bf16[128,1056]{1,0:T(8,128)(2,1)}), bf16[4096,1056]{1,0:T(8,128)(2,1)}) %all-gather.3.cloned.1.call-update) | async-done | bytes 8650768 | tf_op jit(solution)/shard_map/all_gather | solution.py:135
  116.8 10.3 %fusion.5 = bf16[515,1056]{1,0:T(8,128)(2,1)S(1)} fusion(bf16[4096,1056]{1,0:T(8,128)(2,1)} %all-gather.3.cloned.1.call-done, bf16[512,4096]{1,0:T(8,128)(2,1)} %param.12, bf16[3,4096]{1,0:T(4,128)(2,1)S(1)} %collective-permute-done), kind=kOutput, calls=%fused_computation.7 | convolution fusion | flops 4464118784 | bytes 13957312 | tf_op jit(solution)/shard_map/dot_general | solution.py:140
  127.2 1.2 collective-permute-start.1
  128.6 0.6 multiply_convert_fusion.7
  129.2 0.5 reshape.156
  129.8 0.6 copy.31
  130.5 1.3 collective-permute-start.2
  131.8 2.4 collective-permute-start.3
  134.3 1.2 collective-permute-start.4
  135.6 0.6 collective-permute-done.2
  136.2 3.8 %collective-permute-done.3 = bf16[515,64]{1,0:T(8,128)(2,1)S(1)} collective-permute-done((bf16[515,64]{1,0:T(8,128)(2,1)S(1)}, bf16[515,64]{1,0:T(8,128)(2,1)S(1)}, u32[]{:S(2)}, u32[]{:S(2)}) %collective-permute-start.3) | collective-permute-done | bytes 65952 | tf_op jit(solution)/shard_map/ppermute | solution.py:149
  140.9 1.0 fusion.22
  141.9 0.8 fusion.35.msg_ref
  142.7 0.7 broadcast_in_dim.52.dec_ref
  143.4 19.0 %shard_map.118 = f32[8,64,128]{2,1,0:T(8,128)} custom-call(f32[8,64,128]{2,1,0:T(8,128)} %fusion.35.msg_ref, f32[8,128]{1,0:T(8,128)} %broadcast_in_dim.52.dec_ref, f32[8,64,128]{2,1,0:T(8,128)} %sin_ref.1), custom_call_target="tpu_custom_call" | custom-call | tf_op jit(solution)/shard_map/pallas_call | solution.py:88
  162.6 1.3 fusion.14
  164.3 0.6 fusion.16
  165.3 2.2 multiply_reduce_fusion
  167.5 16.5 %psum.7 = f32[512]{0:T(512)S(1)} all-reduce(f32[512]{0:T(512)S(1)} %get-tuple-element.5), channel_id=1, replica_groups=mesh['seq'=32,'head'=8] {'head'}, use_global_device_ids=true, to_apply=%region_5.6 | all-reduce | flops 512 | bytes 4096 | tf_op jit(solution)/shard_map/psum | solution.py:209
  184.0 18.6 %all-gather.5.cloned.1.call-done = bf16[4096,512]{0,1:T(8,128)(2,1)} async-done(((bf16[128,512]{0,1:T(8,128)(2,1)}), bf16[4096,512]{0,1:T(8,128)(2,1)}) %all-gather.5.cloned.1.call-update) | async-done | bytes 4194320 | tf_op jit(solution)/shard_map/all_gather | solution.py:136
  202.7 6.5 %fusion = bf16[4096,512]{0,1:T(8,128)(2,1)} fusion(bf16[4096,512]{0,1:T(8,128)(2,1)} %all-gather.5.cloned.1.call-done, f32[512,512]{1,0:T(8,128)S(1)} %get-tuple-element.6, f32[512]{0:T(512)S(1)} %copy-done.5, f32[512]{0:T(512)S(1)} %add_rsqrt_fusion), kind=kOutput, calls=%fused_computation.1 | convolution fusion | flops 2150367232 | bytes 9441280 | tf_op jit(solution)/shard_map/dot_general | solution.py:212
  209.2 41.3 %reduce-scatter.2.cloned.1.call-done = bf16[512,512]{0,1:T(8,128)(2,1)} async-done(((bf16[4096,512]{0,1:T(8,128)(2,1)}), bf16[512,512]{0,1:T(8,128)(2,1)}) %reduce-scatter.2.cloned.1.call-update) | async-done | bytes 524304 | tf_op jit(solution)/shard_map/reduce_scatter | solution.py:216
  (55 shorter events, 3.7 us)
Async XLA Ops:
  6.5 1.5 copy-start
  6.5 110.3 %all-gather.3.cloned.1.call-start = ((), (), s32[]{:S(2)}) async-start(), calls=%async_computation.1 | async-start | bytes 9732096 | tf_op jit(solution)/shard_map/all_gather | solution.py:135
  9.0 193.7 %all-gather.5.cloned.1.call-start = ((), (), s32[]{:S(2)}) async-start(), calls=%async_computation.2 | async-start | bytes 4325376 | tf_op jit(solution)/shard_map/all_gather | solution.py:136
  9.9 11.1 %collective-permute-start = (bf16[3,4096]{1,0:T(4,128)(2,1)S(1)}, bf16[3,4096]{1,0:T(4,128)(2,1)S(1)}, u32[]{:S(2)}, u32[]{:S(2)}) collective-permute-start(bf16[3,4096]{1,0:T(4,128)(2,1)S(1)} %slice.115), channel_id=1, source_target_pairs={{0,8},{8,16},{16,24},{24,32},{32,40},{40,48},{48,56},{56,64},{64,7... | collective-permute-start | bytes 73736 | tf_op jit(solution)/shard_map/ppermute | solution.py:16
  14.3 236.1 %reduce-scatter.2.cloned.1.call-start = ((), (), s32[]{:S(2)}) async-start(), calls=%async_computation.3 | async-start | bytes 4718592 | tf_op jit(solution)/shard_map/reduce_scatter | solution.py:216
  21.0 107.4 %copy-start.3 = (bf16[3,512]{1,0:T(4,128)(2,1)S(1)}, bf16[3,512]{1,0:T(4,128)(2,1)}, u32[]{:S(2)}) copy-start(bf16[3,512]{1,0:T(4,128)(2,1)} %param.17) | copy-start | bytes 9220
  127.2 1.4 copy-start.1
  127.2 3.1 %collective-permute-start.1 = (bf16[515,32]{1,0:T(8,128)(2,1)S(1)}, bf16[515,32]{1,0:T(8,128)(2,1)S(1)}, u32[]{:S(2)}, u32[]{:S(2)}) collective-permute-start(bf16[515,32]{1,0:T(8,128)(2,1)S(1)} %get-tuple-element.12), channel_id=1, source_target_pairs={{0,1},{1,0},{2,3},{3,2},{4,5},{5,4},{6,7},{7,6},{8,9},{9,8},{10,11... | collective-permute-start | bytes 98888 | tf_op jit(solution)/shard_map/ppermute | solution.py:142
  129.2 11.0 %copy-start.4 = (bf16[3,256]{1,0:T(4,128)(2,1)S(1)}, bf16[3,256]{1,0:T(4,128)(2,1)}, u32[]{:S(2)}) copy-start(bf16[3,256]{1,0:T(4,128)(2,1)} %param.18) | copy-start | bytes 4612
  130.5 5.6 %collective-permute-start.2 = (bf16[515,64]{1,0:T(8,128)(2,1)S(1)}, bf16[515,64]{1,0:T(8,128)(2,1)S(1)}, u32[]{:S(2)}, u32[]{:S(2)}) collective-permute-start(bf16[515,64]{1,0:T(8,128)(2,1)S(1)} %maximum_select_fusion.2), channel_id=1, source_target_pairs={{0,2},{1,3},{2,4},{3,5},{4,6},{5,7},{6,0},{7,1},{8,10},{9,11},{10,... | collective-permute-start | bytes 197768 | tf_op jit(solution)/shard_map/ppermute | solution.py:149
  131.8 8.2 %collective-permute-start.3 = (bf16[515,64]{1,0:T(8,128)(2,1)S(1)}, bf16[515,64]{1,0:T(8,128)(2,1)S(1)}, u32[]{:S(2)}, u32[]{:S(2)}) collective-permute-start(bf16[515,64]{1,0:T(8,128)(2,1)S(1)} %maximum_select_fusion.2), channel_id=1, source_target_pairs={{0,4},{1,5},{2,6},{3,7},{4,0},{5,1},{6,2},{7,3},{8,12},{9,13},{10,... | collective-permute-start | bytes 197768 | tf_op jit(solution)/shard_map/ppermute | solution.py:149
  134.3 5.7 %collective-permute-start.4 = (bf16[515,64]{1,0:T(8,128)(2,1)S(1)}, bf16[515,64]{1,0:T(8,128)(2,1)S(1)}, u32[]{:S(2)}, u32[]{:S(2)}) collective-permute-start(bf16[515,64]{1,0:T(8,128)(2,1)S(1)} %maximum_select_fusion.2), channel_id=1, source_target_pairs={{0,6},{1,7},{2,0},{3,1},{4,2},{5,3},{6,4},{7,5},{8,14},{9,15},{10,... | collective-permute-start | bytes 197768 | tf_op jit(solution)/shard_map/ppermute | solution.py:149
  162.6 1.7 copy-start.2
  165.0 37.7 %copy-start.5 = (f32[512]{0:T(512)S(1)}, f32[512]{0:T(512)}, u32[]{:S(2)}) copy-start(f32[512]{0:T(512)} %param.22) | copy-start | bytes 6148
Sparse Core Ops, SparseCore 0:
  9.9 106.8 all-gather.2
  119.3 83.3 all-gather.4
  209.3 41.0 reduce-scatter.1
